TPU v7x, 128 devices: a whole 4x4x4 slice. The times are simulated.
128 devices in a mesh: gx: 16 (over z_lo, x, core), gy: 8 (over y, z_hi).
Axes of the slice: x: 4, y: 4, z: 4 (z_hi: 2, z_lo: 2; z = z_hi * 2 + z_lo), core: 2. Of those that a mesh axis runs over, the one named last changes fastest.
Arguments:
- disp_prev: float32 [3, 256, 128, 384], P(None, 'gx', 'gy'), may hold values from -6 to 6
- disp_now: float32 [3, 256, 128, 384], P(None, 'gx', 'gy'), may hold values from -6 to 6
- buoyancy: float32 [256, 128, 384], P('gx', 'gy'), may hold values from 0.4 to 1
- shear_mod: float32 [256, 128, 384], P('gx', 'gy'), may hold values from 0.3 to 1
- lame_first: float32 [256, 128, 384], P('gx', 'gy'), may hold values from 0.3 to 1
- foot_offset: int32 [16384, 2], P(('gx', 'gy')), may hold values from 0 to 8
- owner_source: int32 [16384], P(('gx', 'gy')), may hold values from 0 to 16383, as said below
- owner_count: int32 [128], P(('gx', 'gy')), may hold values from 96 to 128, as said below
- force_history: float32 [31, 64, 16384], P(None, None, ('gx', 'gy')), may hold values from -6 to 6
- participation: float32 [192, 64], replicated, may hold values from -0.4375 to 0.4375
- kernels: float32 [64, 32], replicated, may hold values from -1 to 1
Outputs:
- disp_mid: float32 [3, 256, 128, 384], P(None, 'gx', 'gy')
- disp_next: float32 [3, 256, 128, 384], P(None, 'gx', 'gy')
- responses: float32 [2, 64, 16384], P(None, None, ('gx', 'gy'))
Inputs may be any that keep to these rules, and one draw needn't show every extreme that they name: `owner_source`: building slot s belongs to owner device s // 128; its first owner_count slots are live. Among the live slots of one owner at most 2 name footprints on one tile, and every owner reaches 2. Footprints cluster on a few tiles. `owner_count`: some owner holds 128.
All inputs are finite; a program needn't handle non-finite values.
Results may differ from a plain program's by a relative error of at most 0.00012.
Values sent between devices are 32-bit elements; how exact they have to be, the bound alone decides.
No kernel may reach another device: no remote copies, remote signals or barrier semaphores. Data moves between devices by JAX's collectives and lax.ppermute only.
A program may use at most 128 MiB of HBM per device.

v0:
```python
import jax
import jax.numpy as jnp
from jax import lax
from jax.experimental import pallas as pl
from jax.experimental.pallas import tpu as pltpu
from jax.sharding import PartitionSpec as P


PX = 8
SIDE = 16
LANES = 128
HIGHEST = lax.Precision.HIGHEST
F32 = jnp.float32
VMEM_BYTES = 16 << 20

VMEM_SPEC = pl.BlockSpec(memory_space=pltpu.VMEM)
HBM_SPEC = pl.BlockSpec(memory_space=pltpu.HBM)
SMEM_SPEC = pl.BlockSpec(memory_space=pltpu.SMEM)


def iota(shape, axis):
    return lax.broadcasted_iota(jnp.int32, shape, axis)


def in_vmem(array):
    return pltpu.with_memory_space_constraint(array, pltpu.VMEM)


def in_hbm(array):
    return pltpu.with_memory_space_constraint(array, pltpu.HBM)


def parity(axis):
    return lax.axis_index(axis) % 2


def first_of(a1, b1, a2, b2):
    return (a1 - b1) - (a2 - b2) * 0.125


def second_of(a1, b1, a2, b2):
    return (a1 + b1) - (a2 + b2) * 0.0625


def z_four(below, columns, above):
    lane = iota(columns[0].shape, 1)
    zero = jnp.zeros_like(columns[0])
    count = len(columns)
    out = [[] for _ in columns]
    for s in (1, -1, 2, -2):
        turned = [pltpu.roll(c, (-s) % LANES, axis=1) for c in columns]
        if s > 0:
            turned.append(zero if above is None else pltpu.roll(above, LANES - s, axis=1))
        else:
            turned.insert(0, zero if below is None else pltpu.roll(below, -s, axis=1))
        for k in range(count):
            if s > 0:
                out[k].append(jnp.where(lane < LANES - s, turned[k], turned[k + 1]))
            else:
                out[k].append(jnp.where(lane >= -s, turned[k + 1], turned[k]))
    return out


def z_first(below, columns, above):
    return [first_of(*four) for four in z_four(below, columns, above)]


def fill_rims(vp, xa, xb, ya, yb):
    rows = vp.shape[1] - 4
    odd_x, odd_y = parity("gx"), parity("gy")
    vp[:, pl.ds((rows + 2) * (1 - odd_x), 2), 8:24, :] = xa[...]
    vp[:, pl.ds((rows + 2) * odd_x, 2), 8:24, :] = xb[...]

    @pl.when(odd_y == 0)
    def _():
        vp[:, :, 6:8, :] = yb[...]
        vp[:, :, 24:26, :] = ya[...]

    @pl.when(odd_y == 1)
    def _():
        vp[:, :, 6:8, :] = ya[...]
        vp[:, :, 24:26, :] = yb[...]


def step_columns(vp, prev, buoy, mu, lam, out, byx, syz, first, last, ready, done):
    rows = vp.shape[1] - 4
    total = vp.shape[3] // LANES
    span = range(first, last)
    lanes = lambda k: pl.ds(k * LANES, LANES)

    def y_four(c, r, h, k):
        return [vp[c, r, pl.ds(8 + 8 * h + d, 8), lanes(k)] for d in (1, -1, 2, -2)]

    def ends(get):
        below = get(first - 1) if first > 0 else None
        above = get(last) if last < total else None
        return below, [get(k) for k in span], above

    def inner(r, carry):
        for h in range(2):
            here = pl.ds(8 * h, 8)
            core = pl.ds(8 + 8 * h, 8)
            dz = z_first(*ends(lambda k: vp[2, r, core, lanes(k)]))
            for n, k in enumerate(span):
                byx[r, here, lanes(k - first)] = first_of(*y_four(0, r, h, k))
                syz[r, here, lanes(k - first)] = first_of(*y_four(1, r, h, k)) + dz[n]
        return carry

    lax.fori_loop(0, rows + 4, inner, 0)

    def outer(i, carry):
        r = i + 2
        for h in range(2):
            here = pl.ds(8 * h, 8)
            core = pl.ds(8 + 8 * h, 8)

            def x_four(c, k):
                return [vp[c, r + d, core, lanes(k)] for d in (1, -1, 2, -2)]

            def derived(ref, k):
                return first_of(*[ref[r + d, here, lanes(k - first)] for d in (1, -1, 2, -2)])

            yz = z_first(*ends(lambda k: first_of(*y_four(2, r, h, k))))
            xy = z_first(*ends(lambda k: first_of(*x_four(0, k)) + first_of(*y_four(1, r, h, k))))
            along_z = [z_four(*ends(lambda k: vp[c, r, core, lanes(k)])) for c in range(3)]
            for n, k in enumerate(span):
                shear = mu[i, here, lanes(k - first)]
                both = lam[i, here, lanes(k - first)] + shear
                scale = buoy[i, here, lanes(k - first)] * 0.12
                mixed = [derived(syz, k), derived(byx, k) + yz[n], xy[n]]
                for c in range(3):
                    centre = vp[c, r, core, lanes(k)]
                    q = [second_of(*x_four(c, k)), second_of(*y_four(c, r, h, k)), second_of(*along_z[c][n])]
                    laplace = (q[0] + q[1]) + (q[2] - centre * 5.625)
                    along = (q[c] - centre * 1.875) + mixed[c] * (1.0 / 3.0)
                    update = shear * laplace + both * along
                    out[c, i, here, lanes(k - first)] = (
                        2.0 * centre - prev[c, i, here, lanes(k - first)]
                    ) + scale * update
        return carry

    ready()
    for start in range(0, rows, rows // 4):
        lax.fori_loop(start, start + rows // 4, outer, 0)
        done(start, rows // 4)


def surface_rows(field, first):
    cells = SIDE * SIDE
    flat = jnp.zeros((8, cells), F32)
    for c in range(3):
        pick = jnp.where((iota((8, LANES), 0) == first + c) & (iota((8, LANES), 1) == 0), 1.0, 0.0)
        flat = flat + lax.dot_general(
            pick,
            field[c, :, :, 0:LANES].reshape(cells, LANES),
            (((1,), (1,)), ((), ())),
            precision=HIGHEST,
            preferred_element_type=F32,
        )
    return flat


def started(pairs, sems):
    copies = [pltpu.make_async_copy(src, dst, sems.at[n]) for n, (src, dst) in enumerate(pairs)]
    for copy in copies:
        copy.start()
    return copies


def wait_all(copies):
    for copy in copies:
        copy.wait()


def first_step_kernel(
    v, prev, buoy, mu, lam, xa, xb, ya, yb, mid, out, nxa, nxb, nlo, nhi, top, vp, pv, bv, mv, lv, byx, syz, sems
):
    rows = v.shape[1]
    copies = started(
        [(v, vp.at[:, 2 : rows + 2, 8:24, :]), (prev, pv), (buoy, bv), (mu, mv), (lam, lv)], sems
    )
    fill_rims(vp, xa, xb, ya, yb)
    copies[0].wait()
    stores = []

    def done(row, count):
        part = (slice(None), pl.ds(row, count))
        stores.extend(started([(out.at[part], mid.at[part])], sems.at[pl.ds(5 + len(stores), 1)]))

    step_columns(
        vp, pv, bv, mv, lv, out, byx, syz, 0, v.shape[3] // LANES, lambda: wait_all(copies[1:]), done
    )
    odd_x = parity("gx")
    nxa[...] = out[:, pl.ds((rows - 2) * (1 - odd_x), 2), :, :]
    nxb[...] = out[:, pl.ds((rows - 2) * odd_x, 2), :, :]
    nlo[...] = out[:, :, 0:2, :]
    nhi[...] = out[:, :, 14:16, :]
    top[...] = surface_rows(out, 0)
    wait_all(stores)


def first_step(v, halos, prev, buoy, mu, lam):
    _, rows, cols, depth = v.shape
    whole = pltpu.VMEM(v.shape, F32)
    one = pltpu.VMEM((rows, cols, depth), F32)
    return pl.pallas_call(
        first_step_kernel,
        out_shape=(
            pltpu.HBM(v.shape, F32),
            whole,
            pltpu.VMEM((3, 2, cols, depth), F32),
            pltpu.VMEM((3, 2, cols, depth), F32),
            pltpu.VMEM((3, rows, 2, depth), F32),
            pltpu.VMEM((3, rows, 2, depth), F32),
            pltpu.VMEM((8, SIDE * SIDE), F32),
        ),
        in_specs=[VMEM_SPEC] + [HBM_SPEC] * 4 + [VMEM_SPEC] * 4,
        out_specs=(HBM_SPEC,) + (VMEM_SPEC,) * 6,
        scratch_shapes=[
            pltpu.VMEM((3, rows + 4, 32, depth), F32),
            whole,
            one,
            one,
            one,
            pltpu.VMEM((rows + 4, cols, depth), F32),
            pltpu.VMEM((rows + 4, cols, depth), F32),
            pltpu.SemaphoreType.DMA((9,)),
        ],
        compiler_params=pltpu.CompilerParams(vmem_limit_bytes=VMEM_BYTES),
        name="first_step",
    )(v, prev, buoy, mu, lam, *halos)


def main_step_kernel(prev, buoy, mu, lam, v, xa, xb, nxt, near, vp, pv, bv, mv, lv, out, byx, syz, sems):
    rows = v.shape[1]
    copies = started([(prev, pv), (buoy, bv), (mu, mv), (lam, lv)], sems)
    odd_x = parity("gx")
    vp[:, 2 : rows + 2, 8:24, :] = v[...]
    vp[:, pl.ds((rows + 2) * (1 - odd_x), 2), 8:24, :] = xa[...]
    vp[:, pl.ds((rows + 2) * odd_x, 2), 8:24, :] = xb[...]
    none = jnp.zeros((vp.shape[0], vp.shape[1], 2, vp.shape[3]), F32)
    vp[:, :, 6:8, :] = none
    vp[:, :, 24:26, :] = none
    stores = []
    rest = pl.ds(LANES, v.shape[3] - LANES)

    def done(row, count):
        part = pl.ds(row, count)
        near[:, part] = out[:, part, :, 0:LANES]
        stores.extend(
            started([(out.at[:, part, :, rest], nxt.at[:, part, :, rest])], sems.at[pl.ds(4 + len(stores), 1)])
        )

    step_columns(
        vp, pv, bv, mv, lv, out, byx, syz, 0, v.shape[3] // LANES, lambda: wait_all(copies), done
    )
    wait_all(stores)


def main_step(v, xa, xb, prev, buoy, mu, lam):
    _, rows, cols, depth = v.shape
    whole = pltpu.VMEM(v.shape, F32)
    one = pltpu.VMEM((rows, cols, depth), F32)
    return pl.pallas_call(
        main_step_kernel,
        out_shape=(pltpu.HBM(v.shape, F32), pltpu.VMEM((3, rows, cols, LANES), F32)),
        in_specs=[HBM_SPEC] * 4 + [VMEM_SPEC] * 3,
        out_specs=(HBM_SPEC, VMEM_SPEC),
        scratch_shapes=[
            pltpu.VMEM((3, rows + 4, 32, depth), F32),
            whole,
            one,
            one,
            one,
            whole,
            pltpu.VMEM((rows + 4, cols, depth), F32),
            pltpu.VMEM((rows + 4, cols, depth), F32),
            pltpu.SemaphoreType.DMA((8,)),
        ],
        compiler_params=pltpu.CompilerParams(vmem_limit_bytes=VMEM_BYTES),
        name="main_step",
    )(prev, buoy, mu, lam, v, xa, xb)


def fill_north(rim, ya, yb):
    odd_y = parity("gy")
    rim[:, :, 8:16, :] = jnp.zeros((rim.shape[0], rim.shape[1], 8, rim.shape[3]), F32)

    @pl.when(odd_y == 0)
    def _():
        rim[:, :, 6:8, :] = yb[...]
        rim[:, :, 16:18, :] = ya[...]

    @pl.when(odd_y == 1)
    def _():
        rim[:, :, 6:8, :] = ya[...]
        rim[:, :, 16:18, :] = yb[...]


def add_north(rim, buoy, mu, lam, out, ex, ey, first, last, ready):
    rows = rim.shape[1] - 4
    total = rim.shape[3] // LANES
    span = range(first, last)
    lanes = lambda k: pl.ds(k * LANES, LANES)
    local = lambda k: pl.ds((k - first) * LANES, LANES)
    below, above = max(first - 1, 0), min(last + 1, total)

    def y_four(c, r, k):
        return [rim[c, r, pl.ds(8 + d, 8), lanes(k)] for d in (1, -1, 2, -2)]

    def ends(get):
        return (
            get(first - 1) if first > 0 else None,
            [get(k) for k in span],
            get(last) if last < total else None,
        )

    def inner(r, carry):
        for k in range(below, above):
            ey[r, :, lanes(k)] = first_of(*y_four(1, r, k))
        for k in span:
            ex[r, :, lanes(k)] = first_of(*y_four(0, r, k))
        return carry

    lax.fori_loop(0, rows + 4, inner, 0)
    ready()

    def outer(i, carry):
        r = i + 2
        yz = z_first(*ends(lambda k: first_of(*y_four(2, r, k))))
        xy = z_first(*ends(lambda k: ey[r, :, lanes(k)]))
        low = iota((8, LANES), 0) < 4
        for n, k in enumerate(span):

            def packed(ref):
                return jnp.where(low, ref[i, 0:8, local(k)], ref[i, 8:16, local(k)])

            def derived(ref):
                return first_of(*[ref[r + d, :, lanes(k)] for d in (1, -1, 2, -2)])

            shear = packed(mu)
            both = packed(lam) + shear
            scale = packed(buoy) * 0.12
            mixed = [derived(ey), derived(ex) + yz[n], xy[n]]
            for c in range(3):
                q = second_of(*y_four(c, r, k))
                along = mixed[c] * (1.0 / 3.0)
                if c == 1:
                    along = along + q
                update = scale * (shear * q + both * along)
                out[c, i, 0:8, local(k)] = out[c, i, 0:8, local(k)] + jnp.where(low, update, 0.0)
                out[c, i, 8:16, local(k)] = out[c, i, 8:16, local(k)] + jnp.where(low, 0.0, update)
        return carry

    lax.fori_loop(0, rows, outer, 0)


def window_tables(flat, windows):
    span = SIDE - PX + 1
    halves = [flat[:, :LANES], flat[:, LANES:]]
    lane = iota((8, LANES), 1)
    windows[span * span * 8 :, :] = jnp.zeros((windows.shape[0] - span * span * 8, LANES), F32)
    for ox in range(span):
        for oy in range(span):
            half, shift = divmod(ox * SIDE + oy, LANES)
            moved = halves[half]
            if shift:
                other = pltpu.roll(halves[1], LANES - shift, axis=1) if half == 0 else jnp.zeros_like(moved)
                moved = jnp.where(lane < LANES - shift, pltpu.roll(moved, LANES - shift, axis=1), other)
            windows[pl.ds((ox * span + oy) * 8, 8), :] = moved


def corner_forces(flat, weights, windows):
    window_tables(flat, windows)
    total = jnp.zeros((LANES, weights.shape[2]), F32)
    for c in range(3):
        total = total + jnp.dot(
            windows[pl.ds(c, LANES, stride=8), :], weights[c], precision=HIGHEST, preferred_element_type=F32
        )
    return total


def spread(part, c):
    shape = (LANES, part.shape[1])
    cell = iota(shape, 0)
    row = c * PX * PX + (cell // SIDE) * PX + cell % SIDE
    place = jnp.where((iota(shape, 1) == row) & (cell % SIDE < PX), 1.0, 0.0)
    return lax.dot_general(
        place, part[...], (((1,), (1,)), ((), ())), precision=HIGHEST, preferred_element_type=F32
    )


def prepare_kernel(top, asked, offset, part, chosen, weights, early, windows):
    span = SIDE - PX + 1
    shape = (LANES, LANES)
    where = offset[0:1, :] * span + offset[1:2, :]
    corner = jnp.where(iota(shape, 0) == where, 1.0, 0.0)
    lane = iota(shape, 1)
    for r in range(2):
        slot = jnp.where(lane == asked[:, r : r + 1], 1.0, 0.0)
        chosen[pl.ds(r, LANES, stride=2), :] = lax.dot_general(
            slot, corner, (((1,), (1,)), ((), ())), preferred_element_type=F32
        )
    for c in range(3):
        weights[c] = spread(part, c)
    forces = corner_forces(top[...], weights, windows)
    early[...] = jnp.dot(chosen[...], forces, precision=HIGHEST, preferred_element_type=F32)


def prepare(top, asked, offset, part):
    modes = part.shape[0]
    return pl.pallas_call(
        prepare_kernel,
        out_shape=(
            pltpu.VMEM((2 * LANES, LANES), F32),
            pltpu.VMEM((3, LANES, modes), F32),
            pltpu.VMEM((2 * LANES, modes), F32),
        ),
        in_specs=[VMEM_SPEC] * 4,
        out_specs=(VMEM_SPEC,) * 3,
        scratch_shapes=[pltpu.VMEM((8 * LANES, LANES), F32)],
        compiler_params=pltpu.CompilerParams(vmem_limit_bytes=VMEM_BYTES),
        name="prepare",
    )(top, asked, offset, part)


def near_north_kernel(
    buoy, mu, lam, before, near, ya, yb, chosen, weights, early,
    nxt, yao, ybo, ans, rim, bv, mv, lv, out, ex, ey, windows, sems,
):
    column = pl.ds(0, LANES)
    copies = started([(full.at[:, :, column], own) for full, own in ((buoy, bv), (mu, mv), (lam, lv))], sems)
    stores = started([(ya, yao), (yb, ybo)], sems.at[pl.ds(3, 2)])
    fill_north(rim, ya, yb)
    out[...] = near[...]
    add_north(rim, bv, mv, lv, out, ex, ey, 0, 1, lambda: wait_all(copies))
    stores += started([(out, nxt.at[:, :, :, column])], sems.at[pl.ds(5, 1)])
    forces = corner_forces(surface_rows(out, 0), weights, windows)
    late = jnp.dot(chosen[...], forces, precision=HIGHEST, preferred_element_type=F32)
    ans[...] = jnp.concatenate([early[...], late], axis=1)
    wait_all(stores)


def near_north(nxt, near, ya, yb, prepared, buoy, mu, lam):
    _, rows, cols, depth = nxt.shape
    one = pltpu.VMEM((rows, cols, LANES), F32)
    rim = pltpu.HBM(ya.shape, F32)
    return pl.pallas_call(
        near_north_kernel,
        out_shape=(pltpu.HBM(nxt.shape, F32), rim, rim, jax.ShapeDtypeStruct((2 * LANES, LANES), F32)),
        in_specs=[HBM_SPEC] * 4 + [VMEM_SPEC] * 6,
        out_specs=(HBM_SPEC,) * 3 + (VMEM_SPEC,),
        input_output_aliases={3: 0},
        scratch_shapes=[
            pltpu.VMEM((3, rows + 4, 24, depth), F32),
            one,
            one,
            one,
            pltpu.VMEM((3, rows, cols, LANES), F32),
            pltpu.VMEM((rows + 4, 8, depth), F32),
            pltpu.VMEM((rows + 4, 8, depth), F32),
            pltpu.VMEM((8 * LANES, LANES), F32),
            pltpu.SemaphoreType.DMA((6,)),
        ],
        compiler_params=pltpu.CompilerParams(vmem_limit_bytes=VMEM_BYTES),
        name="near_north",
    )(buoy, mu, lam, nxt, near, ya, yb, *prepared)


def far_north_kernel(buoy, mu, lam, before, ya, yb, nxt, rim, yav, ybv, bv, mv, lv, out, ex, ey, sems):
    count = out.shape[3]
    columns = pl.ds(LANES, count)
    copies = started(
        [(ya, yav), (yb, ybv), (before.at[:, :, :, columns], out)]
        + [(full.at[:, :, columns], own) for full, own in ((buoy, bv), (mu, mv), (lam, lv))],
        sems,
    )
    wait_all(copies[:2])
    fill_north(rim, yav, ybv)
    add_north(rim, bv, mv, lv, out, ex, ey, 1, 1 + count // LANES, lambda: wait_all(copies[2:]))
    wait_all(started([(out, nxt.at[:, :, :, columns])], sems.at[pl.ds(6, 1)]))


def far_north(nxt, ya, yb, buoy, mu, lam):
    _, rows, cols, depth = nxt.shape
    rest = depth - LANES
    one = pltpu.VMEM((rows, cols, rest), F32)
    return pl.pallas_call(
        far_north_kernel,
        out_shape=jax.ShapeDtypeStruct(nxt.shape, F32),
        in_specs=[HBM_SPEC] * 6,
        out_specs=HBM_SPEC,
        input_output_aliases={3: 0},
        scratch_shapes=[
            pltpu.VMEM((3, rows + 4, 24, depth), F32),
            pltpu.VMEM(ya.shape, F32),
            pltpu.VMEM(ya.shape, F32),
            one,
            one,
            one,
            pltpu.VMEM((3, rows, cols, rest), F32),
            pltpu.VMEM((rows + 4, 8, depth), F32),
            pltpu.VMEM((rows + 4, 8, depth), F32),
            pltpu.SemaphoreType.DMA((7,)),
        ],
        compiler_params=pltpu.CompilerParams(vmem_limit_bytes=VMEM_BYTES),
        name="far_north",
    )(buoy, mu, lam, nxt, ya, yb)


def north_kernel(low, high, xa, xb, ya, yb):
    rows = low.shape[1]
    odd_x, odd_y = parity("gx"), parity("gy")
    after = pl.ds((rows + 2) * (1 - odd_x), 2)
    before = pl.ds((rows + 2) * odd_x, 2)

    def gather(out, own, edge):
        out[:, 2 : rows + 2] = own[...]
        out[:, after] = xa[:, :, edge : edge + 2, :]
        out[:, before] = xb[:, :, edge : edge + 2, :]

    top = SIDE - 2

    @pl.when(odd_y == 0)
    def _():
        gather(ya, high, top)
        gather(yb, low, 0)

    @pl.when(odd_y == 1)
    def _():
        gather(ya, low, 0)
        gather(yb, high, top)


def north_edges(low, high, xa, xb):
    _, rows, _, depth = low.shape
    out = pltpu.VMEM((3, rows + 4, 2, depth), F32)
    return pl.pallas_call(
        north_kernel,
        out_shape=(out, out),
        in_specs=[VMEM_SPEC] * 4,
        out_specs=(VMEM_SPEC, VMEM_SPEC),
        compiler_params=pltpu.CompilerParams(vmem_limit_bytes=VMEM_BYTES),
        name="north_edges",
    )(low, high, xa, xb)


def request_kernel(source, count, req, pos):
    shape = (LANES, LANES)
    src = source[...]
    slot = iota((1, LANES), 1)
    live = slot < count[0]
    tile = src // LANES
    local = (src % LANES).astype(F32)
    mine = jnp.where((iota(shape, 0) == tile) & live, 1.0, 0.0)
    earlier = jnp.where(iota(shape, 0) < iota(shape, 1), 1.0, 0.0)
    before = jnp.dot(mine, earlier, preferred_element_type=F32)
    rank = jnp.sum(before * mine, axis=0, keepdims=True)
    wanted = mine * local
    lane = iota(shape, 1)
    first = jnp.sum(jnp.where(rank < 0.5, wanted, 0.0), axis=1, keepdims=True)
    second = jnp.sum(jnp.where(rank > 0.5, wanted, 0.0), axis=1, keepdims=True)
    req[...] = jnp.where(lane == 0, first, jnp.where(lane == 1, second, 0.0)).astype(jnp.int32)
    pos[...] = jnp.where(live, tile * 2 + rank.astype(jnp.int32), -1)


def make_requests(source, count):
    return pl.pallas_call(
        request_kernel,
        out_shape=(
            jax.ShapeDtypeStruct((LANES, LANES), jnp.int32),
            jax.ShapeDtypeStruct((1, LANES), jnp.int32),
        ),
        in_specs=[VMEM_SPEC, SMEM_SPEC],
        out_specs=(VMEM_SPEC, VMEM_SPEC),
        compiler_params=pltpu.CompilerParams(vmem_limit_bytes=VMEM_BYTES),
        name="requests",
    )(source.reshape(1, LANES), count)


def columns_of(ker):
    taps = ker.shape[0]
    same = jnp.where(iota((taps, taps), 0) == iota((taps, taps), 1), 1.0, 0.0)
    return lax.dot_general(
        ker[...], same, (((0,), (0,)), ((), ())), precision=HIGHEST, preferred_element_type=F32
    )


def history_kernel(hist, ker, out):
    k = columns_of(ker)
    steps = hist.shape[0]
    half = hist.shape[1] // 2
    for part in range(2):
        rows = pl.ds(part * half, half)
        kp = k[part * half : (part + 1) * half]
        first = jnp.zeros((half, LANES), F32)
        second = jnp.zeros((half, LANES), F32)
        for h in range(steps):
            past = hist[h, rows, :]
            first = first + kp[:, steps - h : steps - h + 1] * past
            if h > 0:
                second = second + kp[:, steps + 1 - h : steps + 2 - h] * past
        out[0, rows, :] = first
        out[1, rows, :] = second


def history_part(hist, ker):
    return pl.pallas_call(
        history_kernel,
        out_shape=jax.ShapeDtypeStruct((2,) + hist.shape[1:], F32),
        in_specs=[VMEM_SPEC, VMEM_SPEC],
        out_specs=VMEM_SPEC,
        compiler_params=pltpu.CompilerParams(vmem_limit_bytes=VMEM_BYTES),
        name="history",
    )(hist, ker)


def response_kernel(ans, pos, base, ker, out):
    at = pos[...]
    chosen = jnp.where(iota((2 * LANES, LANES), 0) == at, 1.0, 0.0)
    forces = lax.dot_general(
        ans[...], chosen, (((0,), (0,)), ((), ())), precision=HIGHEST, preferred_element_type=F32
    )
    k = columns_of(ker)
    modes = k.shape[0]
    early, late = forces[:modes], forces[modes:]
    live = at >= 0
    out[0] = jnp.where(live, base[0] + k[:, 0:1] * early, 0.0)
    out[1] = jnp.where(live, base[1] + k[:, 0:1] * late + k[:, 1:2] * early, 0.0)


def make_responses(ans, pos, base, ker):
    return pl.pallas_call(
        response_kernel,
        out_shape=jax.ShapeDtypeStruct(base.shape, F32),
        in_specs=[VMEM_SPEC] * 4,
        out_specs=VMEM_SPEC,
        compiler_params=pltpu.CompilerParams(vmem_limit_bytes=VMEM_BYTES),
        name="responses",
    )(ans, pos, base, ker)


def swap(array, axis, first):
    pairs = []
    for low in range(first, lax.axis_size(axis) - 1, 2):
        pairs += [(low, low + 1), (low + 1, low)]
    return in_vmem(lax.ppermute(array, axis, pairs))


def east_swaps(xa, xb):
    return swap(xa, "gx", 0), swap(xb, "gx", 1)


def north_swaps(ya, yb):
    return swap(ya, "gy", 0), swap(yb, "gy", 1)


def per_device(
    disp_prev,
    disp_now,
    buoyancy,
    shear_mod,
    lame_first,
    foot_offset,
    owner_source,
    owner_count,
    force_history,
    participation,
    kernels,
):
    return steps(
        disp_prev,
        disp_now,
        tuple(in_hbm(a) for a in (buoyancy, shear_mod, lame_first)),
        foot_offset.T,
        owner_source,
        owner_count,
        force_history,
        participation.T,
        kernels.T,
    )


def exchange(array):
    rows = array.reshape(LANES, -1, LANES)
    out = lax.all_to_all(rows, ("gx", "gy"), split_axis=0, concat_axis=0, tiled=True)
    return out.reshape(array.shape)


def steps(prev, now, medium, offset, source, count, history, part, kernels):
    edge = SIDE - 2
    odd_x = parity("gx")
    east = east_swaps(
        lax.dynamic_slice_in_dim(now, edge * (1 - odd_x), 2, axis=1),
        lax.dynamic_slice_in_dim(now, edge * odd_x, 2, axis=1),
    )
    low, high = in_vmem(now[:, :, :2]), in_vmem(now[:, :, edge:])
    req, pos = make_requests(source, count)
    east, low, high, req = lax.optimization_barrier((east, low, high, req))
    north = north_edges(low, high, *east)
    north = north_swaps(*north)
    asked = exchange(req)
    disp_mid, mid, xa, xb, low, high, top = first_step(in_vmem(now), east + north, in_hbm(prev), *medium)
    east = east_swaps(xa, xb)
    base = history_part(history, kernels)
    prepared = prepare(top, in_vmem(asked), offset, part)
    east, base, prepared = lax.optimization_barrier((east, base, prepared))
    north = north_edges(low, high, *east)
    north = north_swaps(*north)
    rest, near = main_step(mid, *east, in_hbm(now), *medium)
    north, rest, near = lax.optimization_barrier((north, rest, near))
    disp_next, ya, yb, ans = near_north(in_hbm(rest), near, *north, prepared, *medium)
    back = exchange(ans)
    disp_next = far_north(in_hbm(disp_next), in_hbm(ya), in_hbm(yb), *medium)
    responses = make_responses(back, pos, base, kernels)
    return disp_mid, disp_next, responses


def solution(mesh):
    return jax.shard_map(
        per_device,
        mesh=mesh,
        in_specs=(
            P(None, "gx", "gy", None),
            P(None, "gx", "gy", None),
            P("gx", "gy", None),
            P("gx", "gy", None),
            P("gx", "gy", None),
            P(("gx", "gy"), None),
            P(("gx", "gy")),
            P(("gx", "gy")),
            P(None, None, ("gx", "gy")),
            P(),
            P(),
        ),
        out_specs=(
            P(None, "gx", "gy", None),
            P(None, "gx", "gy", None),
            P(None, None, ("gx", "gy")),
        ),
        check_vma=False,
    )
```

profile of v0, /device:TPU:1, one launch (start us, length us, event | category | flops | bytes accessed | tf_op | source)
XLA Modules:
  0.0 88.9 jit_solution(8174773970561949875)
XLA Ops:
  0.7 1.1 %constant_dynamic-slice_fusion = (f32[3,2,16,384]{3,2,1,0:T(8,128)S(1)}, f32[3,2,16,384]{3,2,1,0:T(8,128)S(1)}) fusion(f32[3,16,16,384]{3,2,1,0:T(8,128)} %prev.3, s32[]{:T(128)S(6)} %select_n.15, s32[]{:T(128)S(6)} %select_n.14), kind=kLoop, calls=%fused_computation | loop fusion | bytes 589832 | tf_op jit(solution)/shard_map/dynamic_slice | solution.py:695
  1.8 4.5 %collective-permute-start.1 = (f32[3,2,16,384]{3,2,1,0:T(8,128)S(1)}, f32[3,2,16,384]{3,2,1,0:T(8,128)S(1)}, u32[]{:S(2)}, u32[]{:S(2)}) collective-permute-start(f32[3,2,16,384]{3,2,1,0:T(8,128)S(1)} %get-tuple-element.79), channel_id=1, source_target_pairs={{8,16},{16,8},{24,32},{32,24},{40,48},{48,40},{56,64},{64,56},{72,... | collective-permute-start | bytes 442376 | tf_op jit(solution)/shard_map/ppermute | solution.py:647
  7.0 0.6 copy-done.8
  8.0 0.6 copy-done.6
  8.6 1.3 %fusion = (f32[3,16,2,384]{3,2,1,0:T(2,128)S(1)}, f32[3,16,2,384]{3,2,1,0:T(2,128)S(1)}) fusion(f32[3,16,16,384]{3,2,1,0:T(8,128)} %prev.3), kind=kLoop, calls=%fused_computation.2 | loop fusion | bytes 589824 | tf_op jit(solution)/shard_map/slice | solution.py:697
  10.0 3.7 %collective-permute-start.2 = (f32[3,20,2,384]{3,2,1,0:T(2,128)S(1)}, f32[3,20,2,384]{3,2,1,0:T(2,128)S(1)}, u32[]{:S(2)}, u32[]{:S(2)}) collective-permute-start(f32[3,20,2,384]{3,2,1,0:T(2,128)S(1)} %get-tuple-element.45), channel_id=1, source_target_pairs={{0,1},{1,0},{2,3},{3,2},{4,5},{5,4},{6,7},{7,6},{8,9},{9,8},{10,11... | collective-permute-start | bytes 552968 | tf_op jit(solution)/shard_map/ppermute | solution.py:647
  13.7 0.8 collective-permute-start.3
  14.5 3.7 %collective-permute-done.2.ya = f32[3,20,2,384]{3,2,1,0:T(2,128)S(1)} collective-permute-done((f32[3,20,2,384]{3,2,1,0:T(2,128)S(1)}, f32[3,20,2,384]{3,2,1,0:T(2,128)S(1)}, u32[]{:S(2)}, u32[]{:S(2)}) %collective-permute-start.2) | collective-permute-done | bytes 184352 | tf_op jit(solution)/shard_map/ppermute | solution.py:647
  18.2 7.3 %first_step.1 = (f32[3,16,16,384]{3,2,1,0:T(8,128)}, f32[3,16,16,384]{3,2,1,0:T(8,128)S(1)}, f32[3,2,16,384]{3,2,1,0:T(8,128)}, f32[3,2,16,384]{3,2,1,0:T(8,128)...) custom-call(f32[3,16,16,384]{3,2,1,0:T(8,128)S(1)} %copy-done, ...), custom_call_target="tpu_custom_call" | custom-call | tf_op jit(solution)/shard_map/first_step/pallas_call | solution.py:206
  25.5 0.6 copy-done.2
  26.2 4.3 %collective-permute-start.4 = (f32[3,2,16,384]{3,2,1,0:T(8,128)}, f32[3,2,16,384]{3,2,1,0:T(8,128)S(1)}, u32[]{:S(2)}, u32[]{:S(2)}) collective-permute-start(f32[3,2,16,384]{3,2,1,0:T(8,128)} %get-tuple-element.50), channel_id=1, source_target_pairs={{0,8},{8,0},{16,24},{24,16},{32,40},{40,32},{48,56},{56,48},{64,72... | collective-permute-start | bytes 442376 | tf_op jit(solution)/shard_map/ppermute | solution.py:647
  30.5 3.1 %collective-permute-start.5 = (f32[3,2,16,384]{3,2,1,0:T(8,128)}, f32[3,2,16,384]{3,2,1,0:T(8,128)S(1)}, u32[]{:S(2)}, u32[]{:S(2)}) collective-permute-start(f32[3,2,16,384]{3,2,1,0:T(8,128)} %get-tuple-element.51), channel_id=1, source_target_pairs={{8,16},{16,8},{24,32},{32,24},{40,48},{48,40},{56,64},{64,56},{72,... | collective-permute-start | bytes 442376 | tf_op jit(solution)/shard_map/ppermute | solution.py:647
  33.6 10.8 %all-to-all-start = ((s32[128,1,128]{2,1,0:T(1,128)}), s32[128,1,128]{2,1,0:T(1,128)S(1)}, u32[]{:S(2)}, u32[]{:S(2)}) async-start(s32[128,1,128]{2,1,0:T(1,128)} %bitcast.15), calls=%async_computation | async-start | bytes 131072 | tf_op jit(solution)/shard_map/all_to_all | solution.py:686
  44.4 0.7 history.1.base
  45.1 8.6 %all-to-all-done = s32[128,1,128]{2,1,0:T(1,128)S(1)} async-done(((s32[128,1,128]{2,1,0:T(1,128)}), s32[128,1,128]{2,1,0:T(1,128)S(1)}, u32[]{:S(2)}, u32[]{:S(2)}) %all-to-all-start) | async-done | bytes 65568 | tf_op jit(solution)/shard_map/all_to_all | solution.py:686
  53.7 1.2 %prepare.1 = (f32[256,128]{1,0:T(8,128)S(1)}, f32[3,128,64]{2,1,0:T(8,128)S(1)}, f32[256,64]{1,0:T(8,128)S(1)}) custom-call(f32[8,256]{1,0:T(8,128)S(1)} %get-tuple-element.52.top, s32[128,128]{1,0:T(8,128)S(1)} %bitcast.11, s32[2,128]{1,0:T(2,128)S(1)} %bitcast.16, f32[64,192]{1,0:T(8,128)S(1)} %bitcast.14), custom_call_target="tpu_custom_call" | custom-call | tf_op jit(solution)/shard_map/prepare/pallas_call | solution.py:412
  55.1 1.3 %collective-permute-start.6 = (f32[3,20,2,384]{3,2,1,0:T(2,128)S(1)}, f32[3,20,2,384]{3,2,1,0:T(2,128)S(1)}, u32[]{:S(2)}, u32[]{:S(2)}) collective-permute-start(f32[3,20,2,384]{3,2,1,0:T(2,128)S(1)} %get-tuple-element.59), channel_id=1, source_target_pairs={{0,1},{1,0},{2,3},{3,2},{4,5},{5,4},{6,7},{7,6},{8,9},{9,8},{10,11... | collective-permute-start | bytes 552968 | tf_op jit(solution)/shard_map/ppermute | solution.py:647
  56.4 0.7 collective-permute-start.7
  57.0 6.5 %main_step.1 = (f32[3,16,16,384]{3,2,1,0:T(8,128)}, f32[3,16,16,128]{3,2,1,0:T(8,128)S(1)}) custom-call(f32[3,16,16,384]{3,2,1,0:T(8,128)} %prev.3, f32[16,16,384]{2,1,0:T(8,128)} %buoy.7, f32[16,16,384]{2,1,0:T(8,128)} %mu.7, f32[16,16,384]{2,1,0:T(8,128)} %lam.7, f32[3,16,16,384]{3,2,1,0:T(8,128)S(1)} %get-tuple-element.61.v, ...), custom_call_target="tpu_custom_call" | custom-call | tf_op jit(solution)/shard_map/main_step/pallas_call | solution.py:264
  63.6 5.5 %near_north.1 = (f32[3,16,16,384]{3,2,1,0:T(8,128)}, f32[3,20,2,384]{3,2,1,0:T(2,128)}, f32[3,20,2,384]{3,2,1,0:T(2,128)}, f32[256,128]{1,0:T(8,128)}) custom-call(f32[16,16,384]{2,1,0:T(8,128)} %buoy.7, f32[16,16,384]{2,1,0:T(8,128)} %mu.7, f32[16,16,384]{2,1,0:T(8,128)} %lam.7, ...), custom_call_target="tpu_custom_call", output_to_operand_aliasing={{0}: (3, {})} | custom-call | tf_op jit(solution)/shard_map/near_north/pallas_call | solution.py:448
  69.1 8.9 %all-to-all-start.1 = ((f32[128,2,128]{2,1,0:T(2,128)}), f32[128,2,128]{2,1,0:T(2,128)S(1)}, u32[]{:S(2)}, u32[]{:S(2)}) async-start(f32[128,2,128]{2,1,0:T(2,128)} %bitcast.7), calls=%async_computation.1 | async-start | bytes 262144 | tf_op jit(solution)/shard_map/all_to_all | solution.py:686
  78.0 4.2 %far_north.1 = f32[3,16,16,384]{3,2,1,0:T(8,128)} custom-call(f32[16,16,384]{2,1,0:T(8,128)} %buoy.7, f32[16,16,384]{2,1,0:T(8,128)} %mu.7, f32[16,16,384]{2,1,0:T(8,128)} %lam.7, f32[3,16,16,384]{3,2,1,0:T(8,128)} %get-tuple-element.71.before, f32[3,20,2,384]{3,2,1,0:T(2,128)} %get-tuple-element.72.ya, ...), custom_call_target="tpu_custom_call", output_to_operand_aliasing={{}: (3, {})} | custom-call | tf_op jit(solution)/shard_map/far_north/pallas_call | solution.py:488
  82.2 5.6 %all-to-all-done.1 = f32[128,2,128]{2,1,0:T(2,128)S(1)} async-done(((f32[128,2,128]{2,1,0:T(2,128)}), f32[128,2,128]{2,1,0:T(2,128)S(1)}, u32[]{:S(2)}, u32[]{:S(2)}) %all-to-all-start.1) | async-done | bytes 131104 | tf_op jit(solution)/shard_map/all_to_all | solution.py:686
  87.8 1.1 %responses.1 = f32[2,64,128]{2,1,0:T(8,128)} custom-call(f32[256,128]{1,0:T(8,128)S(1)} %bitcast.10, s32[1,128]{1,0:T(1,128)S(1)} %get-tuple-element.75.pos, f32[2,64,128]{2,1,0:T(8,128)S(1)} %history.1.base, f32[32,64]{1,0:T(8,128)S(1)} %bitcast.13), custom_call_target="tpu_custom_call" | custom-call | tf_op jit(solution)/shard_map/responses/pallas_call | solution.py:633
  (26 shorter events, 0.6 us)
Async XLA Ops:
  0.6 17.6 %copy-start = (f32[3,16,16,384]{3,2,1,0:T(8,128)S(1)}, f32[3,16,16,384]{3,2,1,0:T(8,128)}, u32[]{:S(2)}) copy-start(f32[3,16,16,384]{3,2,1,0:T(8,128)} %prev.3) | copy-start | bytes 3538948
  1.8 8.2 %collective-permute-start.1 = (f32[3,2,16,384]{3,2,1,0:T(8,128)S(1)}, f32[3,2,16,384]{3,2,1,0:T(8,128)S(1)}, u32[]{:S(2)}, u32[]{:S(2)}) collective-permute-start(f32[3,2,16,384]{3,2,1,0:T(8,128)S(1)} %get-tuple-element.79), channel_id=1, source_target_pairs={{8,16},{16,8},{24,32},{32,24},{40,48},{48,40},{56,64},{64,56},{72,... | collective-permute-start | bytes 442376 | tf_op jit(solution)/shard_map/ppermute | solution.py:647
  6.3 3.7 %collective-permute-start = (f32[3,2,16,384]{3,2,1,0:T(8,128)S(1)}, f32[3,2,16,384]{3,2,1,0:T(8,128)S(1)}, u32[]{:S(2)}, u32[]{:S(2)}) collective-permute-start(f32[3,2,16,384]{3,2,1,0:T(8,128)S(1)} %get-tuple-element.80), channel_id=1, source_target_pairs={{0,8},{8,0},{16,24},{24,16},{32,40},{40,32},{48,56},{56,48},{64,72... | collective-permute-start | bytes 442376 | tf_op jit(solution)/shard_map/ppermute | solution.py:647
  7.0 0.7 copy-start.8
  7.9 0.6 copy-start.6
  10.0 8.2 %collective-permute-start.2 = (f32[3,20,2,384]{3,2,1,0:T(2,128)S(1)}, f32[3,20,2,384]{3,2,1,0:T(2,128)S(1)}, u32[]{:S(2)}, u32[]{:S(2)}) collective-permute-start(f32[3,20,2,384]{3,2,1,0:T(2,128)S(1)} %get-tuple-element.45), channel_id=1, source_target_pairs={{0,1},{1,0},{2,3},{3,2},{4,5},{5,4},{6,7},{7,6},{8,9},{9,8},{10,11... | collective-permute-start | bytes 552968 | tf_op jit(solution)/shard_map/ppermute | solution.py:647
  13.7 30.7 %copy-start.1 = (f32[31,64,128]{2,1,0:T(8,128)S(1)}, f32[31,64,128]{2,1,0:T(8,128)}, u32[]{:S(2)}) copy-start(f32[31,64,128]{2,1,0:T(8,128)} %hist.1) | copy-start | bytes 3047428
  13.7 30.7 %copy-start.4 = (f32[64,32]{0,1:T(8,128)S(1)}, f32[64,32]{0,1:T(8,128)}, u32[]{:S(2)}) copy-start(f32[64,32]{0,1:T(8,128)} %param.21) | copy-start | bytes 24580
  13.7 4.5 %collective-permute-start.3 = (f32[3,20,2,384]{3,2,1,0:T(2,128)S(1)}, f32[3,20,2,384]{3,2,1,0:T(2,128)S(1)}, u32[]{:S(2)}, u32[]{:S(2)}) collective-permute-start(f32[3,20,2,384]{3,2,1,0:T(2,128)S(1)} %get-tuple-element.46), channel_id=1, source_target_pairs={{1,2},{2,1},{3,4},{4,3},{5,6},{6,5},{9,10},{10,9},{11,12},{12,11},... | collective-permute-start | bytes 552968 | tf_op jit(solution)/shard_map/ppermute | solution.py:647
  25.5 0.6 copy-start.2
  26.2 27.6 %copy-start.5 = (f32[192,64]{0,1:T(8,128)S(1)}, f32[192,64]{0,1:T(8,128)}, u32[]{:S(2)}) copy-start(f32[192,64]{0,1:T(8,128)} %param.20) | copy-start | bytes 147460
  26.2 27.6 %copy-start.7 = (s32[128,2]{0,1:T(2,128)S(1)}, s32[128,2]{0,1:T(2,128)}, u32[]{:S(2)}) copy-start(s32[128,2]{0,1:T(2,128)} %param.16) | copy-start | bytes 3076
  26.2 28.9 %copy-start.3 = (f32[3,16,2,384]{3,2,1,0:T(2,128)S(1)}, f32[3,16,2,384]{3,2,1,0:T(2,128)}, u32[]{:S(2)}) copy-start(f32[3,16,2,384]{3,2,1,0:T(2,128)} %copy-done.2) | copy-start | bytes 442372
  26.2 28.8 %collective-permute-start.4 = (f32[3,2,16,384]{3,2,1,0:T(8,128)}, f32[3,2,16,384]{3,2,1,0:T(8,128)S(1)}, u32[]{:S(2)}, u32[]{:S(2)}) collective-permute-start(f32[3,2,16,384]{3,2,1,0:T(8,128)} %get-tuple-element.50), channel_id=1, source_target_pairs={{0,8},{8,0},{16,24},{24,16},{32,40},{40,32},{48,56},{56,48},{64,72... | collective-permute-start | bytes 442376 | tf_op jit(solution)/shard_map/ppermute | solution.py:647
  30.5 24.6 %collective-permute-start.5 = (f32[3,2,16,384]{3,2,1,0:T(8,128)}, f32[3,2,16,384]{3,2,1,0:T(8,128)S(1)}, u32[]{:S(2)}, u32[]{:S(2)}) collective-permute-start(f32[3,2,16,384]{3,2,1,0:T(8,128)} %get-tuple-element.51), channel_id=1, source_target_pairs={{8,16},{16,8},{24,32},{32,24},{40,48},{48,40},{56,64},{64,56},{72,... | collective-permute-start | bytes 442376 | tf_op jit(solution)/shard_map/ppermute | solution.py:647
  33.6 20.1 %all-to-all-start = ((s32[128,1,128]{2,1,0:T(1,128)}), s32[128,1,128]{2,1,0:T(1,128)S(1)}, u32[]{:S(2)}, u32[]{:S(2)}) async-start(s32[128,1,128]{2,1,0:T(1,128)} %bitcast.15), calls=%async_computation | async-start | bytes 131072 | tf_op jit(solution)/shard_map/all_to_all | solution.py:686
  55.1 8.4 %collective-permute-start.6 = (f32[3,20,2,384]{3,2,1,0:T(2,128)S(1)}, f32[3,20,2,384]{3,2,1,0:T(2,128)S(1)}, u32[]{:S(2)}, u32[]{:S(2)}) collective-permute-start(f32[3,20,2,384]{3,2,1,0:T(2,128)S(1)} %get-tuple-element.59), channel_id=1, source_target_pairs={{0,1},{1,0},{2,3},{3,2},{4,5},{5,4},{6,7},{7,6},{8,9},{9,8},{10,11... | collective-permute-start | bytes 552968 | tf_op jit(solution)/shard_map/ppermute | solution.py:647
  56.4 7.2 %collective-permute-start.7 = (f32[3,20,2,384]{3,2,1,0:T(2,128)S(1)}, f32[3,20,2,384]{3,2,1,0:T(2,128)S(1)}, u32[]{:S(2)}, u32[]{:S(2)}) collective-permute-start(f32[3,20,2,384]{3,2,1,0:T(2,128)S(1)} %get-tuple-element.60), channel_id=1, source_target_pairs={{1,2},{2,1},{3,4},{4,3},{5,6},{6,5},{9,10},{10,9},{11,12},{12,11},... | collective-permute-start | bytes 552968 | tf_op jit(solution)/shard_map/ppermute | solution.py:647
  69.1 18.7 %all-to-all-start.1 = ((f32[128,2,128]{2,1,0:T(2,128)}), f32[128,2,128]{2,1,0:T(2,128)S(1)}, u32[]{:S(2)}, u32[]{:S(2)}) async-start(f32[128,2,128]{2,1,0:T(2,128)} %bitcast.7), calls=%async_computation.1 | async-start | bytes 262144 | tf_op jit(solution)/shard_map/all_to_all | solution.py:686
where the time goes:
time: 89.2 us; the launch traced here: 88.9 us
  starting transfers between devices  38.1 us (43%)
  Pallas kernels  26.9 us (30%)
  waiting for transfers between devices  17.9 us (20%)
  local copies, waits for them, and re-layouts  4.38 us (5%)
  between operations  1.54 us (2%)
    all_to_all x2, starting transfers between devices, exchange(): lax.all_to_all(rows, ('gx', 'gy'), split_axis=0, concat_axis=0, tiled=True)  19.7 us
    ppermute x8, starting transfers between devices, swap(): return in_vmem(lax.ppermute(array, axis, pairs))  18.4 us
    all_to_all x2, waiting for transfers between devices, exchange(): lax.all_to_all(rows, ('gx', 'gy'), split_axis=0, concat_axis=0, tiled=True)  14.2 us
    pallas_call x1, Pallas kernels, first_step(): pl.pallas_call(first_step_kernel, out_shape=(pltpu.HBM(v.shape, F32), who...  7.28 us
    pallas_call x1, Pallas kernels, main_step(): pl.pallas_call(main_step_kernel, out_shape=(pltpu.HBM(v.shape, F32), pltp...  6.49 us
    pallas_call x1, Pallas kernels, near_north(): pl.pallas_call(near_north_kernel, out_shape=(pltpu.HBM(nxt.shape, F32), r...  5.49 us
    pallas_call x1, Pallas kernels, far_north(): pl.pallas_call(far_north_kernel, out_shape=jax.ShapeDtypeStruct(nxt.shape...  4.23 us
    ppermute x8, waiting for transfers between devices, swap(): return in_vmem(lax.ppermute(array, axis, pairs))  3.73 us
  transfers between devices with their start and end apart: 10, of which 3 were waited for; matrix products, arithmetic and copies ran while one was open for 2% of the time, Pallas kernels for 15%

commit v1 on v0

--- a/solution.py
+++ b/solution.py
@@ -65,24 +65,7 @@
     return [first_of(*four) for four in z_four(below, columns, above)]
 
 
-def fill_rims(vp, xa, xb, ya, yb):
-    rows = vp.shape[1] - 4
-    odd_x, odd_y = parity("gx"), parity("gy")
-    vp[:, pl.ds((rows + 2) * (1 - odd_x), 2), 8:24, :] = xa[...]
-    vp[:, pl.ds((rows + 2) * odd_x, 2), 8:24, :] = xb[...]
-
-    @pl.when(odd_y == 0)
-    def _():
-        vp[:, :, 6:8, :] = yb[...]
-        vp[:, :, 24:26, :] = ya[...]
-
-    @pl.when(odd_y == 1)
-    def _():
-        vp[:, :, 6:8, :] = ya[...]
-        vp[:, :, 24:26, :] = yb[...]
-
-
-def step_columns(vp, prev, buoy, mu, lam, out, byx, syz, first, last, ready, done):
+def step_columns(vp, prev, buoy, mu, lam, out, pack, byx, syz, first, last, ready, done):
     rows = vp.shape[1] - 4
     total = vp.shape[3] // LANES
     span = range(first, last)
@@ -110,6 +93,8 @@
 
     def outer(i, carry):
         r = i + 2
+        low = iota((8, LANES), 0) < 4
+        lower = {}
         for h in range(2):
             here = pl.ds(8 * h, 8)
             core = pl.ds(8 + 8 * h, 8)
@@ -127,6 +112,11 @@
                 shear = mu[i, here, lanes(k - first)]
                 both = lam[i, here, lanes(k - first)] + shear
                 scale = buoy[i, here, lanes(k - first)] * 0.12
+                for which, factor in enumerate((shear, both, scale)):
+                    if h == 0:
+                        lower[which, k] = factor
+                    else:
+                        pack[which, i, :, lanes(k - first)] = jnp.where(low, lower[which, k], factor)
                 mixed = [derived(syz, k), derived(byx, k) + yz[n], xy[n]]
                 for c in range(3):
                     centre = vp[c, r, core, lanes(k)]
@@ -172,77 +162,135 @@
         copy.wait()
 
 
-def first_step_kernel(
-    v, prev, buoy, mu, lam, xa, xb, ya, yb, mid, out, nxa, nxb, nlo, nhi, top, vp, pv, bv, mv, lv, byx, syz, sems
-):
-    rows = v.shape[1]
+def east_pack_kernel(now, prev, buoy, mu, lam, pa, pb, sems):
+    rows = now.shape[1]
+    odd = parity("gx")
+    pairs = []
+    for out, side in ((pa, 1 - odd), (pb, odd)):
+        four = pl.ds((rows - 4) * side, 4)
+        two = pl.ds((rows - 2) * side, 2)
+        for c in range(3):
+            pairs.append((now.at[c, four], out.at[pl.ds(4 * c, 4)]))
+            pairs.append((prev.at[c, two], out.at[pl.ds(12 + 2 * c, 2)]))
+        for n, field in enumerate((buoy, mu, lam)):
+            pairs.append((field.at[two], out.at[pl.ds(18 + 2 * n, 2)]))
+    wait_all(started(pairs, sems))
+
+
+def east_pack(now, prev, buoy, mu, lam):
+    _, _, cols, depth = now.shape
+    out = pltpu.VMEM((24, cols, depth), F32)
+    return pl.pallas_call(
+        east_pack_kernel,
+        out_shape=(out, out),
+        in_specs=[HBM_SPEC] * 5,
+        out_specs=(VMEM_SPEC,) * 2,
+        scratch_shapes=[pltpu.SemaphoreType.DMA((18,))],
+        compiler_params=pltpu.CompilerParams(vmem_limit_bytes=VMEM_BYTES),
+        name="east_pack",
+    )(now, prev, buoy, mu, lam)
+
+
+def clear_north(vp):
+    none = jnp.zeros((vp.shape[0], vp.shape[1], 2, vp.shape[3]), F32)
+    vp[:, :, 6:8, :] = none
+    vp[:, :, 24:26, :] = none
+
+
+def first_main_kernel(prev, buoy, mu, lam, now, xa, xb, out, pack, vp, pv, bv, mv, lv, byx, syz, sems):
+    rows = now.shape[1]
+    own = pl.ds(2, rows)
     copies = started(
-        [(v, vp.at[:, 2 : rows + 2, 8:24, :]), (prev, pv), (buoy, bv), (mu, mv), (lam, lv)], sems
+        [(prev, pv.at[:, own])] + [(src, dst.at[own]) for src, dst in ((buoy, bv), (mu, mv), (lam, lv))], sems
     )
-    fill_rims(vp, xa, xb, ya, yb)
-    copies[0].wait()
-    stores = []
-
-    def done(row, count):
-        part = (slice(None), pl.ds(row, count))
-        stores.extend(started([(out.at[part], mid.at[part])], sems.at[pl.ds(5 + len(stores), 1)]))
-
+    odd = parity("gx")
+    vp[:, 4 : rows + 4, 8:24, :] = now[...]
+    for edge, side in ((xa, 1 - odd), (xb, odd)):
+        four = pl.ds((rows + 4) * side, 4)
+        two = pl.ds((rows + 2) * side, 2)
+        for c in range(3):
+            vp[c, four, 8:24, :] = edge[4 * c : 4 * c + 4]
+            pv[c, two] = edge[12 + 2 * c : 14 + 2 * c]
+        for n, field in enumerate((bv, mv, lv)):
+            field[two] = edge[18 + 2 * n : 20 + 2 * n]
+    clear_north(vp)
     step_columns(
-        vp, pv, bv, mv, lv, out, byx, syz, 0, v.shape[3] // LANES, lambda: wait_all(copies[1:]), done
+        vp, pv, bv, mv, lv, out, pack, byx, syz, 0, now.shape[3] // LANES,
+        lambda: wait_all(copies), lambda row, count: None,
     )
-    odd_x = parity("gx")
-    nxa[...] = out[:, pl.ds((rows - 2) * (1 - odd_x), 2), :, :]
-    nxb[...] = out[:, pl.ds((rows - 2) * odd_x, 2), :, :]
-    nlo[...] = out[:, :, 0:2, :]
-    nhi[...] = out[:, :, 14:16, :]
-    top[...] = surface_rows(out, 0)
-    wait_all(stores)
-
-
-def first_step(v, halos, prev, buoy, mu, lam):
-    _, rows, cols, depth = v.shape
-    whole = pltpu.VMEM(v.shape, F32)
-    one = pltpu.VMEM((rows, cols, depth), F32)
-    return pl.pallas_call(
-        first_step_kernel,
-        out_shape=(
-            pltpu.HBM(v.shape, F32),
-            whole,
-            pltpu.VMEM((3, 2, cols, depth), F32),
-            pltpu.VMEM((3, 2, cols, depth), F32),
-            pltpu.VMEM((3, rows, 2, depth), F32),
-            pltpu.VMEM((3, rows, 2, depth), F32),
-            pltpu.VMEM((8, SIDE * SIDE), F32),
-        ),
-        in_specs=[VMEM_SPEC] + [HBM_SPEC] * 4 + [VMEM_SPEC] * 4,
-        out_specs=(HBM_SPEC,) + (VMEM_SPEC,) * 6,
+
+
+def first_main(now, xa, xb, prev, buoy, mu, lam):
+    _, rows, cols, depth = now.shape
+    wide = rows + 4
+    one = pltpu.VMEM((wide, cols, depth), F32)
+    return pl.pallas_call(
+        first_main_kernel,
+        out_shape=(pltpu.VMEM((3, wide, cols, depth), F32), pltpu.VMEM((3, wide, 8, depth), F32)),
+        in_specs=[HBM_SPEC] * 4 + [VMEM_SPEC] * 3,
+        out_specs=(VMEM_SPEC,) * 2,
         scratch_shapes=[
-            pltpu.VMEM((3, rows + 4, 32, depth), F32),
-            whole,
+            pltpu.VMEM((3, wide + 4, 32, depth), F32),
+            pltpu.VMEM((3, wide, cols, depth), F32),
             one,
             one,
             one,
-            pltpu.VMEM((rows + 4, cols, depth), F32),
-            pltpu.VMEM((rows + 4, cols, depth), F32),
-            pltpu.SemaphoreType.DMA((9,)),
+            pltpu.VMEM((wide + 4, cols, depth), F32),
+            pltpu.VMEM((wide + 4, cols, depth), F32),
+            pltpu.SemaphoreType.DMA((4,)),
         ],
         compiler_params=pltpu.CompilerParams(vmem_limit_bytes=VMEM_BYTES),
-        name="first_step",
-    )(v, prev, buoy, mu, lam, *halos)
-
-
-def main_step_kernel(prev, buoy, mu, lam, v, xa, xb, nxt, near, vp, pv, bv, mv, lv, out, byx, syz, sems):
-    rows = v.shape[1]
+        name="first_main",
+    )(prev, buoy, mu, lam, now, xa, xb)
+
+
+def first_north_kernel(main, pack, ya, yb, mid, ma, mb, top, rim, ex, ey):
+    rows = main.shape[1] - 4
+    fill_north(rim, ya, yb)
+    add_north(rim, pack, main, mid, ex, ey, 0, main.shape[3] // LANES)
+    odd = parity("gy")
+
+    @pl.when(odd == 0)
+    def _():
+        ma[...] = mid[:, :, 14:16, :]
+        mb[...] = mid[:, :, 0:2, :]
+
+    @pl.when(odd == 1)
+    def _():
+        ma[...] = mid[:, :, 0:2, :]
+        mb[...] = mid[:, :, 14:16, :]
+
+    top[...] = surface_rows(mid.at[:, pl.ds(2, rows)], 0)
+
+
+def first_north(main, pack, ya, yb):
+    _, wide, _, depth = main.shape
+    edge = pltpu.VMEM((3, wide, 2, depth), F32)
+    return pl.pallas_call(
+        first_north_kernel,
+        out_shape=(pltpu.VMEM(main.shape, F32), edge, edge, pltpu.VMEM((8, SIDE * SIDE), F32)),
+        in_specs=[VMEM_SPEC] * 4,
+        out_specs=(VMEM_SPEC,) * 4,
+        scratch_shapes=[
+            pltpu.VMEM((3, wide + 4, 24, depth), F32),
+            pltpu.VMEM((wide + 4, 8, depth), F32),
+            pltpu.VMEM((wide + 4, 8, depth), F32),
+        ],
+        compiler_params=pltpu.CompilerParams(vmem_limit_bytes=VMEM_BYTES),
+        name="first_north",
+    )(main, pack, ya, yb)
+
+
+def second_main_kernel(
+    prev, buoy, mu, lam, v, mid, nxt, far, near, close, vp, pv, bv, mv, lv, out, pack, byx, syz, sems
+):
+    rows = prev.shape[1]
+    total = prev.shape[3] // LANES
     copies = started([(prev, pv), (buoy, bv), (mu, mv), (lam, lv)], sems)
-    odd_x = parity("gx")
-    vp[:, 2 : rows + 2, 8:24, :] = v[...]
-    vp[:, pl.ds((rows + 2) * (1 - odd_x), 2), 8:24, :] = xa[...]
-    vp[:, pl.ds((rows + 2) * odd_x, 2), 8:24, :] = xb[...]
-    none = jnp.zeros((vp.shape[0], vp.shape[1], 2, vp.shape[3]), F32)
-    vp[:, :, 6:8, :] = none
-    vp[:, :, 24:26, :] = none
-    stores = []
-    rest = pl.ds(LANES, v.shape[3] - LANES)
+    stores = started([(v.at[:, pl.ds(2, rows)], mid)], sems.at[pl.ds(4, 1)])
+    vp[:, :, 8:24, :] = v[...]
+    clear_north(vp)
+    rest = pl.ds(LANES, prev.shape[3] - LANES)
 
     def done(row, count):
         part = pl.ds(row, count)
@@ -252,20 +300,28 @@
         )
 
     step_columns(
-        vp, pv, bv, mv, lv, out, byx, syz, 0, v.shape[3] // LANES, lambda: wait_all(copies), done
+        vp, pv, bv, mv, lv, out, pack, byx, syz, 0, total, lambda: wait_all(copies), done
     )
+    stores += started([(pack.at[:, :, :, rest], far)], sems.at[pl.ds(9, 1)])
+    close[...] = pack[:, :, :, 0:LANES]
     wait_all(stores)
 
 
-def main_step(v, xa, xb, prev, buoy, mu, lam):
-    _, rows, cols, depth = v.shape
-    whole = pltpu.VMEM(v.shape, F32)
+def second_main(v, prev, buoy, mu, lam):
+    _, rows, cols, depth = prev.shape
+    whole = pltpu.VMEM(prev.shape, F32)
     one = pltpu.VMEM((rows, cols, depth), F32)
     return pl.pallas_call(
-        main_step_kernel,
-        out_shape=(pltpu.HBM(v.shape, F32), pltpu.VMEM((3, rows, cols, LANES), F32)),
-        in_specs=[HBM_SPEC] * 4 + [VMEM_SPEC] * 3,
-        out_specs=(HBM_SPEC, VMEM_SPEC),
+        second_main_kernel,
+        out_shape=(
+            pltpu.HBM(prev.shape, F32),
+            pltpu.HBM(prev.shape, F32),
+            pltpu.HBM((3, rows, 8, depth - LANES), F32),
+            pltpu.VMEM((3, rows, cols, LANES), F32),
+            pltpu.VMEM((3, rows, 8, LANES), F32),
+        ),
+        in_specs=[HBM_SPEC] * 4 + [VMEM_SPEC],
+        out_specs=(HBM_SPEC,) * 3 + (VMEM_SPEC,) * 2,
         scratch_shapes=[
             pltpu.VMEM((3, rows + 4, 32, depth), F32),
             whole,
@@ -273,33 +329,35 @@
             one,
             one,
             whole,
+            pltpu.VMEM((3, rows, 8, depth), F32),
             pltpu.VMEM((rows + 4, cols, depth), F32),
             pltpu.VMEM((rows + 4, cols, depth), F32),
-            pltpu.SemaphoreType.DMA((8,)),
+            pltpu.SemaphoreType.DMA((10,)),
         ],
         compiler_params=pltpu.CompilerParams(vmem_limit_bytes=VMEM_BYTES),
-        name="main_step",
-    )(prev, buoy, mu, lam, v, xa, xb)
+        name="second_main",
+    )(prev, buoy, mu, lam, v)
 
 
 def fill_north(rim, ya, yb):
     odd_y = parity("gy")
     rim[:, :, 8:16, :] = jnp.zeros((rim.shape[0], rim.shape[1], 8, rim.shape[3]), F32)
 
+    wide = rim.shape[3]
+
     @pl.when(odd_y == 0)
     def _():
-        rim[:, :, 6:8, :] = yb[...]
-        rim[:, :, 16:18, :] = ya[...]
+        rim[:, :, 6:8, :] = yb[:, :, :, :wide]
+        rim[:, :, 16:18, :] = ya[:, :, :, :wide]
 
     @pl.when(odd_y == 1)
     def _():
-        rim[:, :, 6:8, :] = ya[...]
-        rim[:, :, 16:18, :] = yb[...]
-
-
-def add_north(rim, buoy, mu, lam, out, ex, ey, first, last, ready):
+        rim[:, :, 6:8, :] = ya[:, :, :, :wide]
+        rim[:, :, 16:18, :] = yb[:, :, :, :wide]
+
+
+def add_north(rim, pack, main, out, ex, ey, first, last, ready=None, total=3):
     rows = rim.shape[1] - 4
-    total = rim.shape[3] // LANES
     span = range(first, last)
     lanes = lambda k: pl.ds(k * LANES, LANES)
     local = lambda k: pl.ds((k - first) * LANES, LANES)
@@ -323,7 +381,8 @@
         return carry
 
     lax.fori_loop(0, rows + 4, inner, 0)
-    ready()
+    if ready is not None:
+        ready()
 
     def outer(i, carry):
         r = i + 2
@@ -332,15 +391,10 @@
         low = iota((8, LANES), 0) < 4
         for n, k in enumerate(span):
 
-            def packed(ref):
-                return jnp.where(low, ref[i, 0:8, local(k)], ref[i, 8:16, local(k)])
-
             def derived(ref):
                 return first_of(*[ref[r + d, :, lanes(k)] for d in (1, -1, 2, -2)])
 
-            shear = packed(mu)
-            both = packed(lam) + shear
-            scale = packed(buoy) * 0.12
+            shear, both, scale = [pack[which, i, :, local(k)] for which in range(3)]
             mixed = [derived(ey), derived(ex) + yz[n], xy[n]]
             for c in range(3):
                 q = second_of(*y_four(c, r, k))
@@ -348,8 +402,8 @@
                 if c == 1:
                     along = along + q
                 update = scale * (shear * q + both * along)
-                out[c, i, 0:8, local(k)] = out[c, i, 0:8, local(k)] + jnp.where(low, update, 0.0)
-                out[c, i, 8:16, local(k)] = out[c, i, 8:16, local(k)] + jnp.where(low, 0.0, update)
+                out[c, i, 0:8, local(k)] = main[c, i, 0:8, local(k)] + jnp.where(low, update, 0.0)
+                out[c, i, 8:16, local(k)] = main[c, i, 8:16, local(k)] + jnp.where(low, 0.0, update)
         return carry
 
     lax.fori_loop(0, rows, outer, 0)
@@ -390,7 +444,7 @@
     )
 
 
-def prepare_kernel(top, asked, offset, part, chosen, weights, early, windows):
+def prepare_kernel(asked, offset, part, chosen, weights):
     span = SIDE - PX + 1
     shape = (LANES, LANES)
     where = offset[0:1, :] * span + offset[1:2, :]
@@ -403,146 +457,142 @@
         )
     for c in range(3):
         weights[c] = spread(part, c)
+
+
+def prepare(asked, offset, part):
+    modes = part.shape[0]
+    return pl.pallas_call(
+        prepare_kernel,
+        out_shape=(pltpu.VMEM((2 * LANES, LANES), F32), pltpu.VMEM((3, LANES, modes), F32)),
+        in_specs=[VMEM_SPEC] * 3,
+        out_specs=(VMEM_SPEC,) * 2,
+        compiler_params=pltpu.CompilerParams(vmem_limit_bytes=VMEM_BYTES),
+        name="prepare",
+    )(asked, offset, part)
+
+
+def early_kernel(top, chosen, weights, early, windows):
     forces = corner_forces(top[...], weights, windows)
     early[...] = jnp.dot(chosen[...], forces, precision=HIGHEST, preferred_element_type=F32)
 
 
-def prepare(top, asked, offset, part):
-    modes = part.shape[0]
-    return pl.pallas_call(
-        prepare_kernel,
-        out_shape=(
-            pltpu.VMEM((2 * LANES, LANES), F32),
-            pltpu.VMEM((3, LANES, modes), F32),
-            pltpu.VMEM((2 * LANES, modes), F32),
-        ),
-        in_specs=[VMEM_SPEC] * 4,
-        out_specs=(VMEM_SPEC,) * 3,
+def early_forces(top, chosen, weights):
+    return pl.pallas_call(
+        early_kernel,
+        out_shape=pltpu.VMEM((2 * LANES, weights.shape[2]), F32),
+        in_specs=[VMEM_SPEC] * 3,
+        out_specs=VMEM_SPEC,
         scratch_shapes=[pltpu.VMEM((8 * LANES, LANES), F32)],
         compiler_params=pltpu.CompilerParams(vmem_limit_bytes=VMEM_BYTES),
-        name="prepare",
-    )(top, asked, offset, part)
+        name="early_forces",
+    )(top, chosen, weights)
 
 
 def near_north_kernel(
-    buoy, mu, lam, before, near, ya, yb, chosen, weights, early,
-    nxt, yao, ybo, ans, rim, bv, mv, lv, out, ex, ey, windows, sems,
+    before, near, pack, ya, yb, chosen, weights, early, nxt, yao, ybo, ans, rim, out, ex, ey, windows, sems
 ):
-    column = pl.ds(0, LANES)
-    copies = started([(full.at[:, :, column], own) for full, own in ((buoy, bv), (mu, mv), (lam, lv))], sems)
-    stores = started([(ya, yao), (yb, ybo)], sems.at[pl.ds(3, 2)])
+    stores = started([(ya, yao), (yb, ybo)], sems)
     fill_north(rim, ya, yb)
-    out[...] = near[...]
-    add_north(rim, bv, mv, lv, out, ex, ey, 0, 1, lambda: wait_all(copies))
-    stores += started([(out, nxt.at[:, :, :, column])], sems.at[pl.ds(5, 1)])
+    add_north(rim, pack, near, out, ex, ey, 0, 1)
+    stores += started([(out, nxt.at[:, :, :, pl.ds(0, LANES)])], sems.at[pl.ds(2, 1)])
     forces = corner_forces(surface_rows(out, 0), weights, windows)
     late = jnp.dot(chosen[...], forces, precision=HIGHEST, preferred_element_type=F32)
     ans[...] = jnp.concatenate([early[...], late], axis=1)
     wait_all(stores)
 
 
-def near_north(nxt, near, ya, yb, prepared, buoy, mu, lam):
-    _, rows, cols, depth = nxt.shape
-    one = pltpu.VMEM((rows, cols, LANES), F32)
+def near_north(nxt, near, pack, ya, yb, chosen, weights, early):
+    _, rows, cols, _ = nxt.shape
     rim = pltpu.HBM(ya.shape, F32)
     return pl.pallas_call(
         near_north_kernel,
         out_shape=(pltpu.HBM(nxt.shape, F32), rim, rim, jax.ShapeDtypeStruct((2 * LANES, LANES), F32)),
-        in_specs=[HBM_SPEC] * 4 + [VMEM_SPEC] * 6,
+        in_specs=[HBM_SPEC] + [VMEM_SPEC] * 7,
         out_specs=(HBM_SPEC,) * 3 + (VMEM_SPEC,),
-        input_output_aliases={3: 0},
+        input_output_aliases={0: 0},
         scratch_shapes=[
-            pltpu.VMEM((3, rows + 4, 24, depth), F32),
-            one,
-            one,
-            one,
+            pltpu.VMEM((3, rows + 4, 24, 2 * LANES), F32),
             pltpu.VMEM((3, rows, cols, LANES), F32),
-            pltpu.VMEM((rows + 4, 8, depth), F32),
-            pltpu.VMEM((rows + 4, 8, depth), F32),
+            pltpu.VMEM((rows + 4, 8, 2 * LANES), F32),
+            pltpu.VMEM((rows + 4, 8, 2 * LANES), F32),
             pltpu.VMEM((8 * LANES, LANES), F32),
-            pltpu.SemaphoreType.DMA((6,)),
+            pltpu.SemaphoreType.DMA((3,)),
         ],
         compiler_params=pltpu.CompilerParams(vmem_limit_bytes=VMEM_BYTES),
         name="near_north",
-    )(buoy, mu, lam, nxt, near, ya, yb, *prepared)
-
-
-def far_north_kernel(buoy, mu, lam, before, ya, yb, nxt, rim, yav, ybv, bv, mv, lv, out, ex, ey, sems):
+    )(nxt, near, pack, ya, yb, chosen, weights, early)
+
+
+def far_north_kernel(before, pack, ya, yb, nxt, rim, yav, ybv, pv, main, out, ex, ey, sems):
     count = out.shape[3]
     columns = pl.ds(LANES, count)
-    copies = started(
-        [(ya, yav), (yb, ybv), (before.at[:, :, :, columns], out)]
-        + [(full.at[:, :, columns], own) for full, own in ((buoy, bv), (mu, mv), (lam, lv))],
-        sems,
-    )
+    copies = started([(ya, yav), (yb, ybv), (before.at[:, :, :, columns], main), (pack, pv)], sems)
     wait_all(copies[:2])
     fill_north(rim, yav, ybv)
-    add_north(rim, bv, mv, lv, out, ex, ey, 1, 1 + count // LANES, lambda: wait_all(copies[2:]))
-    wait_all(started([(out, nxt.at[:, :, :, columns])], sems.at[pl.ds(6, 1)]))
-
-
-def far_north(nxt, ya, yb, buoy, mu, lam):
+    add_north(rim, pv, main, out, ex, ey, 1, 1 + count // LANES, lambda: wait_all(copies[2:]))
+    wait_all(started([(out, nxt.at[:, :, :, columns])], sems.at[pl.ds(4, 1)]))
+
+
+def far_north(nxt, pack, ya, yb):
     _, rows, cols, depth = nxt.shape
     rest = depth - LANES
-    one = pltpu.VMEM((rows, cols, rest), F32)
+    part = pltpu.VMEM((3, rows, cols, rest), F32)
     return pl.pallas_call(
         far_north_kernel,
         out_shape=jax.ShapeDtypeStruct(nxt.shape, F32),
-        in_specs=[HBM_SPEC] * 6,
+        in_specs=[HBM_SPEC] * 4,
         out_specs=HBM_SPEC,
-        input_output_aliases={3: 0},
+        input_output_aliases={0: 0},
         scratch_shapes=[
             pltpu.VMEM((3, rows + 4, 24, depth), F32),
             pltpu.VMEM(ya.shape, F32),
             pltpu.VMEM(ya.shape, F32),
-            one,
-            one,
-            one,
-            pltpu.VMEM((3, rows, cols, rest), F32),
+            pltpu.VMEM(pack.shape, F32),
+            part,
+            part,
             pltpu.VMEM((rows + 4, 8, depth), F32),
             pltpu.VMEM((rows + 4, 8, depth), F32),
-            pltpu.SemaphoreType.DMA((7,)),
+            pltpu.SemaphoreType.DMA((5,)),
         ],
         compiler_params=pltpu.CompilerParams(vmem_limit_bytes=VMEM_BYTES),
         name="far_north",
-    )(buoy, mu, lam, nxt, ya, yb)
-
-
-def north_kernel(low, high, xa, xb, ya, yb):
-    rows = low.shape[1]
+    )(nxt, pack, ya, yb)
+
+
+def north_kernel(now, xa, xb, ya, yb):
+    rows = now.shape[1]
     odd_x, odd_y = parity("gx"), parity("gy")
-    after = pl.ds((rows + 2) * (1 - odd_x), 2)
-    before = pl.ds((rows + 2) * odd_x, 2)
-
-    def gather(out, own, edge):
-        out[:, 2 : rows + 2] = own[...]
-        out[:, after] = xa[:, :, edge : edge + 2, :]
-        out[:, before] = xb[:, :, edge : edge + 2, :]
-
-    top = SIDE - 2
+
+    def gather(out, edge):
+        out[:, 4 : rows + 4] = now[:, :, edge : edge + 2, :]
+        for rim, side in ((xa, 1 - odd_x), (xb, odd_x)):
+            for c in range(3):
+                out[c, pl.ds((rows + 4) * side, 4)] = rim[4 * c : 4 * c + 4, edge : edge + 2, :]
+
+    high = SIDE - 2
 
     @pl.when(odd_y == 0)
     def _():
-        gather(ya, high, top)
-        gather(yb, low, 0)
+        gather(ya, high)
+        gather(yb, 0)
 
     @pl.when(odd_y == 1)
     def _():
-        gather(ya, low, 0)
-        gather(yb, high, top)
-
-
-def north_edges(low, high, xa, xb):
-    _, rows, _, depth = low.shape
-    out = pltpu.VMEM((3, rows + 4, 2, depth), F32)
+        gather(ya, 0)
+        gather(yb, high)
+
+
+def north_edges(now, xa, xb):
+    _, rows, _, depth = now.shape
+    out = pltpu.VMEM((3, rows + 8, 2, depth), F32)
     return pl.pallas_call(
         north_kernel,
         out_shape=(out, out),
-        in_specs=[VMEM_SPEC] * 4,
+        in_specs=[VMEM_SPEC] * 3,
         out_specs=(VMEM_SPEC, VMEM_SPEC),
         compiler_params=pltpu.CompilerParams(vmem_limit_bytes=VMEM_BYTES),
         name="north_edges",
-    )(low, high, xa, xb)
+    )(now, xa, xb)
 
 
 def request_kernel(source, count, req, pos):
@@ -688,30 +738,25 @@
 
 
 def steps(prev, now, medium, offset, source, count, history, part, kernels):
-    edge = SIDE - 2
-    odd_x = parity("gx")
-    east = east_swaps(
-        lax.dynamic_slice_in_dim(now, edge * (1 - odd_x), 2, axis=1),
-        lax.dynamic_slice_in_dim(now, edge * odd_x, 2, axis=1),
-    )
-    low, high = in_vmem(now[:, :, :2]), in_vmem(now[:, :, edge:])
+    held = in_vmem(now)
+    east = east_pack(in_hbm(now), in_hbm(prev), *medium)
+    east = east_swaps(*east)
     req, pos = make_requests(source, count)
-    east, low, high, req = lax.optimization_barrier((east, low, high, req))
-    north = north_edges(low, high, *east)
+    asked = exchange(req)
+    north = north_edges(held, *east)
     north = north_swaps(*north)
-    asked = exchange(req)
-    disp_mid, mid, xa, xb, low, high, top = first_step(in_vmem(now), east + north, in_hbm(prev), *medium)
-    east = east_swaps(xa, xb)
     base = history_part(history, kernels)
-    prepared = prepare(top, in_vmem(asked), offset, part)
-    east, base, prepared = lax.optimization_barrier((east, base, prepared))
-    north = north_edges(low, high, *east)
-    north = north_swaps(*north)
-    rest, near = main_step(mid, *east, in_hbm(now), *medium)
-    north, rest, near = lax.optimization_barrier((north, rest, near))
-    disp_next, ya, yb, ans = near_north(in_hbm(rest), near, *north, prepared, *medium)
+    prepared = prepare(in_vmem(asked), offset, part)
+    main = first_main(held, *east, in_hbm(prev), *medium)
+    north, main, base, prepared = lax.optimization_barrier((north, main, base, prepared))
+    mid, ya, yb, top = first_north(*main, *north)
+    north = north_swaps(ya, yb)
+    early = early_forces(top, *prepared)
+    disp_mid, rest, far, near, close = second_main(mid, in_hbm(now), *medium)
+    north, rest, far, near, close, early = lax.optimization_barrier((north, rest, far, near, close, early))
+    disp_next, ya, yb, ans = near_north(in_hbm(rest), near, close, *north, *prepared, early)
     back = exchange(ans)
-    disp_next = far_north(in_hbm(disp_next), in_hbm(ya), in_hbm(yb), *medium)
+    disp_next = far_north(in_hbm(disp_next), in_hbm(far), in_hbm(ya), in_hbm(yb))
     responses = make_responses(back, pos, base, kernels)
     return disp_mid, disp_next, responses
 

time: 89.2 us -> 93.9 us (1.053)
  Pallas kernels: 26.9 us -> 33.8 us
  waiting for transfers between devices: 17.9 us -> 22.7 us
  local copies, waits for them, and re-layouts: 4.38 us -> 0.86 us
  starting transfers between devices: 38.1 us -> 34.8 us
    pallas_call x2 -> x5, Pallas kernels: 13.8 us -> 20.8 us  [the longest x1 7.08 us: first_main(): pl.pallas_call(first_main_kernel, out_shape=(pltpu.VMEM((3, wide, cols, d...]
    ppermute x8 -> x6, starting transfers between devices: 18.4 us -> 11.7 us  [swap(): return in_vmem(lax.ppermute(array, axis, pairs))]
    ppermute x8 -> x6, waiting for transfers between devices: 3.73 us -> 8.43 us  [swap(): return in_vmem(lax.ppermute(array, axis, pairs))]
    all_to_all x2, starting transfers between devices: 19.7 us -> 23.1 us  [exchange(): lax.all_to_all(rows, ('gx', 'gy'), split_axis=0, concat_axis=0, tiled=True)]
    slice x1 -> x0, local copies, waits for them, and re-layouts: 1.34 us -> none  [steps(): low, high = (in_vmem(now[:, :, :2]), in_vmem(now[:, :, edge:]))]
    dynamic_slice x1 -> x0, local copies, waits for them, and re-layouts: 1.1 us -> none  [steps(): lax.dynamic_slice_in_dim(now, edge * odd_x, 2, axis=1)]
    unnamed x18 -> x12, local copies, waits for them, and re-layouts: 1.94 us -> 0.86 us
  transfers between devices with their start and end apart: 10 -> 8, of which waited for: 3 -> 3; matrix products, arithmetic and copies ran while one was open for 2% -> 0% of each run, Pallas kernels for 15% -> 22%
where the time goes in v1:
time: 93.9 us; the launch traced here: 93.5 us
  starting transfers between devices  34.8 us (37%)
  Pallas kernels  33.8 us (36%)
  waiting for transfers between devices  22.7 us (24%)
  between operations  1.45 us (2%)
    all_to_all x2, starting transfers between devices, exchange(): lax.all_to_all(rows, ('gx', 'gy'), split_axis=0, concat_axis=0, tiled=True)  23.1 us
    all_to_all x2, waiting for transfers between devices, exchange(): lax.all_to_all(rows, ('gx', 'gy'), split_axis=0, concat_axis=0, tiled=True)  14.3 us
    ppermute x6, starting transfers between devices, swap(): return in_vmem(lax.ppermute(array, axis, pairs))  11.7 us
    ppermute x6, waiting for transfers between devices, swap(): return in_vmem(lax.ppermute(array, axis, pairs))  8.43 us
    pallas_call x1, Pallas kernels, first_main(): pl.pallas_call(first_main_kernel, out_shape=(pltpu.VMEM((3, wide, cols, d...  7.08 us
    pallas_call x1, Pallas kernels, second_main(): pl.pallas_call(second_main_kernel, out_shape=(pltpu.HBM(prev.shape, F32),...  6.65 us
    pallas_call x1, Pallas kernels, near_north(): pl.pallas_call(near_north_kernel, out_shape=(pltpu.HBM(nxt.shape, F32), r...  4.72 us
    pallas_call x1, Pallas kernels, first_north(): pl.pallas_call(first_north_kernel, out_shape=(pltpu.VMEM(main.shape, F32)...  4.63 us
  transfers between devices with their start and end apart: 8, of which 3 were waited for; matrix products, arithmetic and copies ran while one was open for 0% of the time, Pallas kernels for 22%

profile of v1, /device:TPU:1, one launch (start us, length us, event | category | flops | bytes accessed | tf_op | source)
XLA Modules:
  0.0 93.5 jit_solution(1656880013854975352)
XLA Ops:
  0.6 1.5 %east_pack.1 = (f32[24,16,384]{2,1,0:T(8,128)S(1)}, f32[24,16,384]{2,1,0:T(8,128)S(1)}) custom-call(f32[3,16,16,384]{3,2,1,0:T(8,128)} %prev.5, f32[3,16,16,384]{3,2,1,0:T(8,128)} %prev.4, f32[16,16,384]{2,1,0:T(8,128)} %buoy.5, f32[16,16,384]{2,1,0:T(8,128)} %mu.5, f32[16,16,384]{2,1,0:T(8,128)} %lam.5), custom_call_target="tpu_custom_call" | custom-call | tf_op jit(solution)/shard_map/east_pack/pallas_call | solution.py:183
  2.2 1.5 %collective-permute-start = (f32[24,16,384]{2,1,0:T(8,128)S(1)}, f32[24,16,384]{2,1,0:T(8,128)S(1)}, u32[]{:S(2)}, u32[]{:S(2)}) collective-permute-start(f32[24,16,384]{2,1,0:T(8,128)S(1)} %get-tuple-element.40), channel_id=1, source_target_pairs={{0,8},{8,0},{16,24},{24,16},{32,40},{40,32},{48,56},{56,48},{64,72... | collective-permute-start | bytes 1769480 | tf_op jit(solution)/shard_map/ppermute | solution.py:697
  3.6 3.3 %collective-permute-start.1 = (f32[24,16,384]{2,1,0:T(8,128)S(1)}, f32[24,16,384]{2,1,0:T(8,128)S(1)}, u32[]{:S(2)}, u32[]{:S(2)}) collective-permute-start(f32[24,16,384]{2,1,0:T(8,128)S(1)} %get-tuple-element.41), channel_id=1, source_target_pairs={{8,16},{16,8},{24,32},{32,24},{40,48},{48,40},{56,64},{64,56},{72,... | collective-permute-start | bytes 1769480 | tf_op jit(solution)/shard_map/ppermute | solution.py:697
  7.0 8.4 %collective-permute-done.1.xb = f32[24,16,384]{2,1,0:T(8,128)S(1)} collective-permute-done((f32[24,16,384]{2,1,0:T(8,128)S(1)}, f32[24,16,384]{2,1,0:T(8,128)S(1)}, u32[]{:S(2)}, u32[]{:S(2)}) %collective-permute-start.1) | collective-permute-done | bytes 589856 | tf_op jit(solution)/shard_map/ppermute | solution.py:697
  15.4 0.9 north_edges.1
  16.3 3.7 %collective-permute-start.2 = (f32[3,24,2,384]{3,2,1,0:T(2,128)}, f32[3,24,2,384]{3,2,1,0:T(2,128)}, u32[]{:S(2)}, u32[]{:S(2)}) collective-permute-start(f32[3,24,2,384]{3,2,1,0:T(2,128)} %get-tuple-element.42), channel_id=1, source_target_pairs={{0,1},{1,0},{2,3},{3,2},{4,5},{5,4},{6,7},{7,6},{8,9},{9,8},{10,11... | collective-permute-start | bytes 663560 | tf_op jit(solution)/shard_map/ppermute | solution.py:697
  20.0 1.3 %collective-permute-start.3 = (f32[3,24,2,384]{3,2,1,0:T(2,128)}, f32[3,24,2,384]{3,2,1,0:T(2,128)}, u32[]{:S(2)}, u32[]{:S(2)}) collective-permute-start(f32[3,24,2,384]{3,2,1,0:T(2,128)} %get-tuple-element.43), channel_id=1, source_target_pairs={{1,2},{2,1},{3,4},{4,3},{5,6},{6,5},{9,10},{10,9},{11,12},{12,11},... | collective-permute-start | bytes 663560 | tf_op jit(solution)/shard_map/ppermute | solution.py:697
  22.0 0.9 requests.1
  22.9 14.2 %all-to-all-start = ((s32[128,1,128]{2,1,0:T(1,128)}), s32[128,1,128]{2,1,0:T(1,128)S(1)}, u32[]{:S(2)}, u32[]{:S(2)}) async-start(s32[128,1,128]{2,1,0:T(1,128)} %bitcast.3), calls=%async_computation | async-start | bytes 131072 | tf_op jit(solution)/shard_map/all_to_all | solution.py:736
  37.1 0.7 history.1.base
  37.8 8.6 %all-to-all-done = s32[128,1,128]{2,1,0:T(1,128)S(1)} async-done(((s32[128,1,128]{2,1,0:T(1,128)}), s32[128,1,128]{2,1,0:T(1,128)S(1)}, u32[]{:S(2)}, u32[]{:S(2)}) %all-to-all-start) | async-done | bytes 65568 | tf_op jit(solution)/shard_map/all_to_all | solution.py:736
  46.4 0.8 copy-done.3
  47.3 0.5 prepare.1
  47.8 7.1 %first_main.1 = (f32[3,20,16,384]{3,2,1,0:T(8,128)S(1)}, f32[3,20,8,384]{3,2,1,0:T(8,128)S(1)}) custom-call(f32[3,16,16,384]{3,2,1,0:T(8,128)} %prev.4, f32[16,16,384]{2,1,0:T(8,128)} %buoy.5, f32[16,16,384]{2,1,0:T(8,128)} %mu.5, f32[16,16,384]{2,1,0:T(8,128)} %lam.5, f32[3,16,16,384]{3,2,1,0:T(8,128)S(1)} %copy-done, ...), custom_call_target="tpu_custom_call" | custom-call | tf_op jit(solution)/shard_map/first_main/pallas_call | solution.py:227
  54.9 4.6 %first_north.1 = (f32[3,20,16,384]{3,2,1,0:T(8,128)S(1)}, f32[3,20,2,384]{3,2,1,0:T(2,128)S(1)}, f32[3,20,2,384]{3,2,1,0:T(2,128)S(1)}, f32[8,256]{1,0:T(8,128)S(1)}) custom-call(f32[3,20,16,384]{3,2,1,0:T(8,128)S(1)} %get-tuple-element.49.main, f32[3,20,8,384]{3,2,1,0:T(8,128)S(1)} %get-tuple-element.50.pack, f32[3,24,2,384]{3,2,1,0:T(2,128)} %collective-permute-done.2.ya, ...), custom_call_target="tpu_custom_call" | custom-call | tf_op jit(solution)/shard_map/first_north/pallas_call | solution.py:269
  59.5 1.2 %collective-permute-start.4 = (f32[3,20,2,384]{3,2,1,0:T(2,128)S(1)}, f32[3,20,2,384]{3,2,1,0:T(2,128)S(1)}, u32[]{:S(2)}, u32[]{:S(2)}) collective-permute-start(f32[3,20,2,384]{3,2,1,0:T(2,128)S(1)} %get-tuple-element.55), channel_id=1, source_target_pairs={{0,1},{1,0},{2,3},{3,2},{4,5},{5,4},{6,7},{7,6},{8,9},{9,8},{10,11... | collective-permute-start | bytes 552968 | tf_op jit(solution)/shard_map/ppermute | solution.py:697
  60.7 0.7 collective-permute-start.5
  61.4 6.6 %second_main.1 = (f32[3,16,16,384]{3,2,1,0:T(8,128)}, f32[3,16,16,384]{3,2,1,0:T(8,128)}, f32[3,16,8,256]{3,2,1,0:T(8,128)}, f32[3,16,16,128]{3,2,1,0:T(8,128)S(1)}, f32[3,16,8,128]{3,2,1,0:T(8,128)S(1)}) custom-call(f32[3,16,16,384]{3,2,1,0:T(8,128)} %prev.5, f32[16,16,384]{2,1,0:T(8,128)} %buoy.5, f32[16,16,384]{2,1,0:T(8,128)} %mu.5, f32[16,16,384]{2,1,0:T(8,128)} %lam.5, ...), custom_call_target="tpu_custom_call" | custom-call | tf_op jit(solution)/shard_map/second_main/pallas_call | solution.py:314
  68.0 0.9 %early_forces.1.early = f32[256,64]{1,0:T(8,128)S(1)} custom-call(f32[8,256]{1,0:T(8,128)S(1)} %get-tuple-element.61.top, f32[256,128]{1,0:T(8,128)S(1)} %get-tuple-element.62.chosen, f32[3,128,64]{2,1,0:T(8,128)S(1)} %get-tuple-element.63.weights), custom_call_target="tpu_custom_call" | custom-call | tf_op jit(solution)/shard_map/early_forces/pallas_call | solution.py:480
  69.0 4.7 %near_north.1 = (f32[3,16,16,384]{3,2,1,0:T(8,128)}, f32[3,20,2,384]{3,2,1,0:T(2,128)}, f32[3,20,2,384]{3,2,1,0:T(2,128)}, f32[256,128]{1,0:T(8,128)}) custom-call(f32[3,16,16,384]{3,2,1,0:T(8,128)} %get-tuple-element.64.before, f32[3,16,16,128]{3,2,1,0:T(8,128)S(1)} %get-tuple-element.65.near, ...), custom_call_target="tpu_custom_call", output_to_operand_aliasing={{0}: (0, {})} | custom-call | tf_op jit(solution)/shard_map/near_north/pallas_call | solution.py:507
  73.7 8.9 %all-to-all-start.1 = ((f32[128,2,128]{2,1,0:T(2,128)}), f32[128,2,128]{2,1,0:T(2,128)S(1)}, u32[]{:S(2)}, u32[]{:S(2)}) async-start(f32[128,2,128]{2,1,0:T(2,128)} %bitcast.7), calls=%async_computation.1 | async-start | bytes 262144 | tf_op jit(solution)/shard_map/all_to_all | solution.py:736
  82.7 4.2 %far_north.1 = f32[3,16,16,384]{3,2,1,0:T(8,128)} custom-call(f32[3,16,16,384]{3,2,1,0:T(8,128)} %get-tuple-element.70.before, f32[3,16,8,256]{3,2,1,0:T(8,128)} %get-tuple-element.71.pack, f32[3,20,2,384]{3,2,1,0:T(2,128)} %get-tuple-element.72.ya, f32[3,20,2,384]{3,2,1,0:T(2,128)} %get-tuple-element.73.yb), custom_call_target="tpu_custom_call", output_to_operand_aliasing={{}: (0, {})} | custom-call | tf_op jit(solution)/shard_map/far_north/pallas_call | solution.py:540
  86.9 5.6 %all-to-all-done.1 = f32[128,2,128]{2,1,0:T(2,128)S(1)} async-done(((f32[128,2,128]{2,1,0:T(2,128)}), f32[128,2,128]{2,1,0:T(2,128)S(1)}, u32[]{:S(2)}, u32[]{:S(2)}) %all-to-all-start.1) | async-done | bytes 131104 | tf_op jit(solution)/shard_map/all_to_all | solution.py:736
  92.5 1.1 %responses.1 = f32[2,64,128]{2,1,0:T(8,128)} custom-call(f32[256,128]{1,0:T(8,128)S(1)} %bitcast.10, s32[1,128]{1,0:T(1,128)S(1)} %get-tuple-element.75.pos, f32[2,64,128]{2,1,0:T(8,128)S(1)} %history.1.base, f32[32,64]{1,0:T(8,128)S(1)} %bitcast.13), custom_call_target="tpu_custom_call" | custom-call | tf_op jit(solution)/shard_map/responses/pallas_call | solution.py:683
  (16 shorter events, 0.0 us)
Async XLA Ops:
  0.6 14.7 %copy-start = (f32[3,16,16,384]{3,2,1,0:T(8,128)S(1)}, f32[3,16,16,384]{3,2,1,0:T(8,128)}, u32[]{:S(2)}) copy-start(f32[3,16,16,384]{3,2,1,0:T(8,128)} %prev.5) | copy-start | bytes 3538948
  2.2 4.8 %collective-permute-start = (f32[24,16,384]{2,1,0:T(8,128)S(1)}, f32[24,16,384]{2,1,0:T(8,128)S(1)}, u32[]{:S(2)}, u32[]{:S(2)}) collective-permute-start(f32[24,16,384]{2,1,0:T(8,128)S(1)} %get-tuple-element.40), channel_id=1, source_target_pairs={{0,8},{8,0},{16,24},{24,16},{32,40},{40,32},{48,56},{56,48},{64,72... | collective-permute-start | bytes 1769480 | tf_op jit(solution)/shard_map/ppermute | solution.py:697
  3.6 18.3 %copy-start.5 = (s32[128]{0:T(128)S(1)}, s32[128]{0:T(128)}, u32[]{:S(2)}) copy-start(s32[128]{0:T(128)} %param.17) | copy-start | bytes 1540
  3.6 33.4 %copy-start.1 = (f32[31,64,128]{2,1,0:T(8,128)S(1)}, f32[31,64,128]{2,1,0:T(8,128)}, u32[]{:S(2)}) copy-start(f32[31,64,128]{2,1,0:T(8,128)} %hist.1) | copy-start | bytes 3047428
  3.6 33.4 %copy-start.2 = (f32[64,32]{0,1:T(8,128)S(1)}, f32[64,32]{0,1:T(8,128)}, u32[]{:S(2)}) copy-start(f32[64,32]{0,1:T(8,128)} %param.21) | copy-start | bytes 24580
  3.6 11.7 %collective-permute-start.1 = (f32[24,16,384]{2,1,0:T(8,128)S(1)}, f32[24,16,384]{2,1,0:T(8,128)S(1)}, u32[]{:S(2)}, u32[]{:S(2)}) collective-permute-start(f32[24,16,384]{2,1,0:T(8,128)S(1)} %get-tuple-element.41), channel_id=1, source_target_pairs={{8,16},{16,8},{24,32},{32,24},{40,48},{48,40},{56,64},{64,56},{72,... | collective-permute-start | bytes 1769480 | tf_op jit(solution)/shard_map/ppermute | solution.py:697
  16.3 30.2 %copy-start.4 = (s32[128,2]{0,1:T(2,128)S(1)}, s32[128,2]{0,1:T(2,128)}, u32[]{:S(2)}) copy-start(s32[128,2]{0,1:T(2,128)} %param.16) | copy-start | bytes 3076
  16.3 38.6 %collective-permute-start.2 = (f32[3,24,2,384]{3,2,1,0:T(2,128)}, f32[3,24,2,384]{3,2,1,0:T(2,128)}, u32[]{:S(2)}, u32[]{:S(2)}) collective-permute-start(f32[3,24,2,384]{3,2,1,0:T(2,128)} %get-tuple-element.42), channel_id=1, source_target_pairs={{0,1},{1,0},{2,3},{3,2},{4,5},{5,4},{6,7},{7,6},{8,9},{9,8},{10,11... | collective-permute-start | bytes 663560 | tf_op jit(solution)/shard_map/ppermute | solution.py:697
  20.0 34.9 %collective-permute-start.3 = (f32[3,24,2,384]{3,2,1,0:T(2,128)}, f32[3,24,2,384]{3,2,1,0:T(2,128)}, u32[]{:S(2)}, u32[]{:S(2)}) collective-permute-start(f32[3,24,2,384]{3,2,1,0:T(2,128)} %get-tuple-element.43), channel_id=1, source_target_pairs={{1,2},{2,1},{3,4},{4,3},{5,6},{6,5},{9,10},{10,9},{11,12},{12,11},... | collective-permute-start | bytes 663560 | tf_op jit(solution)/shard_map/ppermute | solution.py:697
  22.9 23.5 %all-to-all-start = ((s32[128,1,128]{2,1,0:T(1,128)}), s32[128,1,128]{2,1,0:T(1,128)S(1)}, u32[]{:S(2)}, u32[]{:S(2)}) async-start(s32[128,1,128]{2,1,0:T(1,128)} %bitcast.3), calls=%async_computation | async-start | bytes 131072 | tf_op jit(solution)/shard_map/all_to_all | solution.py:736
  46.4 0.8 copy-start.3
  59.5 9.5 %collective-permute-start.4 = (f32[3,20,2,384]{3,2,1,0:T(2,128)S(1)}, f32[3,20,2,384]{3,2,1,0:T(2,128)S(1)}, u32[]{:S(2)}, u32[]{:S(2)}) collective-permute-start(f32[3,20,2,384]{3,2,1,0:T(2,128)S(1)} %get-tuple-element.55), channel_id=1, source_target_pairs={{0,1},{1,0},{2,3},{3,2},{4,5},{5,4},{6,7},{7,6},{8,9},{9,8},{10,11... | collective-permute-start | bytes 552968 | tf_op jit(solution)/shard_map/ppermute | solution.py:697
  60.7 8.3 %collective-permute-start.5 = (f32[3,20,2,384]{3,2,1,0:T(2,128)S(1)}, f32[3,20,2,384]{3,2,1,0:T(2,128)S(1)}, u32[]{:S(2)}, u32[]{:S(2)}) collective-permute-start(f32[3,20,2,384]{3,2,1,0:T(2,128)S(1)} %get-tuple-element.56), channel_id=1, source_target_pairs={{1,2},{2,1},{3,4},{4,3},{5,6},{6,5},{9,10},{10,9},{11,12},{12,11},... | collective-permute-start | bytes 552968 | tf_op jit(solution)/shard_map/ppermute | solution.py:697
  73.7 18.7 %all-to-all-start.1 = ((f32[128,2,128]{2,1,0:T(2,128)}), f32[128,2,128]{2,1,0:T(2,128)S(1)}, u32[]{:S(2)}, u32[]{:S(2)}) async-start(f32[128,2,128]{2,1,0:T(2,128)} %bitcast.7), calls=%async_computation.1 | async-start | bytes 262144 | tf_op jit(solution)/shard_map/all_to_all | solution.py:736

commit v2 on v1

--- a/solution.py
+++ b/solution.py
@@ -162,7 +162,7 @@
         copy.wait()
 
 
-def east_pack_kernel(now, prev, buoy, mu, lam, pa, pb, sems):
+def east_pack_kernel(now, prev, buoy, mu, lam, source, pa, pb, req, pos, held, sems):
     rows = now.shape[1]
     odd = parity("gx")
     pairs = []
@@ -174,21 +174,29 @@
             pairs.append((prev.at[c, two], out.at[pl.ds(12 + 2 * c, 2)]))
         for n, field in enumerate((buoy, mu, lam)):
             pairs.append((field.at[two], out.at[pl.ds(18 + 2 * n, 2)]))
-    wait_all(started(pairs, sems))
-
-
-def east_pack(now, prev, buoy, mu, lam):
+    copies = started([(source, held)] + pairs, sems)
+    copies[0].wait()
+    build_requests(held, req, pos)
+    wait_all(copies[1:])
+
+
+def east_pack(now, prev, buoy, mu, lam, source):
     _, _, cols, depth = now.shape
     out = pltpu.VMEM((24, cols, depth), F32)
     return pl.pallas_call(
         east_pack_kernel,
-        out_shape=(out, out),
-        in_specs=[HBM_SPEC] * 5,
-        out_specs=(VMEM_SPEC,) * 2,
-        scratch_shapes=[pltpu.SemaphoreType.DMA((18,))],
+        out_shape=(
+            out,
+            out,
+            jax.ShapeDtypeStruct((LANES, LANES), jnp.int32),
+            pltpu.VMEM((1, LANES), jnp.int32),
+        ),
+        in_specs=[HBM_SPEC] * 6,
+        out_specs=(VMEM_SPEC,) * 4,
+        scratch_shapes=[pltpu.VMEM((1, LANES), jnp.int32), pltpu.SemaphoreType.DMA((19,))],
         compiler_params=pltpu.CompilerParams(vmem_limit_bytes=VMEM_BYTES),
         name="east_pack",
-    )(now, prev, buoy, mu, lam)
+    )(now, prev, buoy, mu, lam, source)
 
 
 def clear_north(vp):
@@ -281,29 +289,16 @@
     )(main, pack, ya, yb)
 
 
-def second_main_kernel(
-    prev, buoy, mu, lam, v, mid, nxt, far, near, close, vp, pv, bv, mv, lv, out, pack, byx, syz, sems
-):
+def second_main_kernel(prev, buoy, mu, lam, v, mid, out, pack, vp, pv, bv, mv, lv, byx, syz, sems):
     rows = prev.shape[1]
     total = prev.shape[3] // LANES
     copies = started([(prev, pv), (buoy, bv), (mu, mv), (lam, lv)], sems)
     stores = started([(v.at[:, pl.ds(2, rows)], mid)], sems.at[pl.ds(4, 1)])
     vp[:, :, 8:24, :] = v[...]
     clear_north(vp)
-    rest = pl.ds(LANES, prev.shape[3] - LANES)
-
-    def done(row, count):
-        part = pl.ds(row, count)
-        near[:, part] = out[:, part, :, 0:LANES]
-        stores.extend(
-            started([(out.at[:, part, :, rest], nxt.at[:, part, :, rest])], sems.at[pl.ds(4 + len(stores), 1)])
-        )
-
     step_columns(
-        vp, pv, bv, mv, lv, out, pack, byx, syz, 0, total, lambda: wait_all(copies), done
-    )
-    stores += started([(pack.at[:, :, :, rest], far)], sems.at[pl.ds(9, 1)])
-    close[...] = pack[:, :, :, 0:LANES]
+        vp, pv, bv, mv, lv, out, pack, byx, syz, 0, total, lambda: wait_all(copies), lambda row, count: None
+    )
     wait_all(stores)
 
 
@@ -315,24 +310,20 @@
         second_main_kernel,
         out_shape=(
             pltpu.HBM(prev.shape, F32),
-            pltpu.HBM(prev.shape, F32),
-            pltpu.HBM((3, rows, 8, depth - LANES), F32),
-            pltpu.VMEM((3, rows, cols, LANES), F32),
-            pltpu.VMEM((3, rows, 8, LANES), F32),
+            whole,
+            pltpu.VMEM((3, rows, 8, depth), F32),
         ),
         in_specs=[HBM_SPEC] * 4 + [VMEM_SPEC],
-        out_specs=(HBM_SPEC,) * 3 + (VMEM_SPEC,) * 2,
+        out_specs=(HBM_SPEC,) + (VMEM_SPEC,) * 2,
         scratch_shapes=[
             pltpu.VMEM((3, rows + 4, 32, depth), F32),
             whole,
             one,
             one,
             one,
-            whole,
-            pltpu.VMEM((3, rows, 8, depth), F32),
             pltpu.VMEM((rows + 4, cols, depth), F32),
             pltpu.VMEM((rows + 4, cols, depth), F32),
-            pltpu.SemaphoreType.DMA((10,)),
+            pltpu.SemaphoreType.DMA((5,)),
         ],
         compiler_params=pltpu.CompilerParams(vmem_limit_bytes=VMEM_BYTES),
         name="second_main",
@@ -356,11 +347,12 @@
         rim[:, :, 16:18, :] = yb[:, :, :, :wide]
 
 
-def add_north(rim, pack, main, out, ex, ey, first, last, ready=None, total=3):
+def add_north(rim, pack, main, out, ex, ey, first, last, base=0, done=None, parts=1):
     rows = rim.shape[1] - 4
+    total = 3
     span = range(first, last)
     lanes = lambda k: pl.ds(k * LANES, LANES)
-    local = lambda k: pl.ds((k - first) * LANES, LANES)
+    local = lambda k: pl.ds((k - base) * LANES, LANES)
     below, above = max(first - 1, 0), min(last + 1, total)
 
     def y_four(c, r, k):
@@ -373,18 +365,20 @@
             get(last) if last < total else None,
         )
 
-    def inner(r, carry):
+    def inner(r):
         for k in range(below, above):
             ey[r, :, lanes(k)] = first_of(*y_four(1, r, k))
         for k in span:
             ex[r, :, lanes(k)] = first_of(*y_four(0, r, k))
+
+    def inner_two(pair, carry):
+        inner(2 * pair)
+        inner(2 * pair + 1)
         return carry
 
-    lax.fori_loop(0, rows + 4, inner, 0)
-    if ready is not None:
-        ready()
-
-    def outer(i, carry):
+    lax.fori_loop(0, (rows + 4) // 2, inner_two, 0)
+
+    def outer(i):
         r = i + 2
         yz = z_first(*ends(lambda k: first_of(*y_four(2, r, k))))
         xy = z_first(*ends(lambda k: ey[r, :, lanes(k)]))
@@ -404,9 +398,17 @@
                 update = scale * (shear * q + both * along)
                 out[c, i, 0:8, local(k)] = main[c, i, 0:8, local(k)] + jnp.where(low, update, 0.0)
                 out[c, i, 8:16, local(k)] = main[c, i, 8:16, local(k)] + jnp.where(low, 0.0, update)
+
+    def outer_two(pair, carry):
+        outer(2 * pair)
+        outer(2 * pair + 1)
         return carry
 
-    lax.fori_loop(0, rows, outer, 0)
+    count = rows // 2 // parts
+    for part in range(parts):
+        lax.fori_loop(part * count, (part + 1) * count, outer_two, 0)
+        if done is not None:
+            done(2 * part * count, 2 * count)
 
 
 def window_tables(flat, windows):
@@ -488,75 +490,62 @@
     )(top, chosen, weights)
 
 
-def near_north_kernel(
-    before, near, pack, ya, yb, chosen, weights, early, nxt, yao, ybo, ans, rim, out, ex, ey, windows, sems
-):
-    stores = started([(ya, yao), (yb, ybo)], sems)
+def near_north_kernel(main, pack, ya, yb, chosen, weights, early, near, ans, rim, ex, ey, windows):
     fill_north(rim, ya, yb)
-    add_north(rim, pack, near, out, ex, ey, 0, 1)
-    stores += started([(out, nxt.at[:, :, :, pl.ds(0, LANES)])], sems.at[pl.ds(2, 1)])
-    forces = corner_forces(surface_rows(out, 0), weights, windows)
+    add_north(rim, pack, main, near, ex, ey, 0, 1)
+    forces = corner_forces(surface_rows(near, 0), weights, windows)
     late = jnp.dot(chosen[...], forces, precision=HIGHEST, preferred_element_type=F32)
     ans[...] = jnp.concatenate([early[...], late], axis=1)
-    wait_all(stores)
-
-
-def near_north(nxt, near, pack, ya, yb, chosen, weights, early):
-    _, rows, cols, _ = nxt.shape
-    rim = pltpu.HBM(ya.shape, F32)
+
+
+def near_north(main, pack, ya, yb, chosen, weights, early):
+    _, rows, cols, _ = main.shape
     return pl.pallas_call(
         near_north_kernel,
-        out_shape=(pltpu.HBM(nxt.shape, F32), rim, rim, jax.ShapeDtypeStruct((2 * LANES, LANES), F32)),
-        in_specs=[HBM_SPEC] + [VMEM_SPEC] * 7,
-        out_specs=(HBM_SPEC,) * 3 + (VMEM_SPEC,),
-        input_output_aliases={0: 0},
+        out_shape=(pltpu.VMEM((3, rows, cols, LANES), F32), pltpu.VMEM((2 * LANES, LANES), F32)),
+        in_specs=[VMEM_SPEC] * 7,
+        out_specs=(VMEM_SPEC,) * 2,
         scratch_shapes=[
             pltpu.VMEM((3, rows + 4, 24, 2 * LANES), F32),
-            pltpu.VMEM((3, rows, cols, LANES), F32),
             pltpu.VMEM((rows + 4, 8, 2 * LANES), F32),
             pltpu.VMEM((rows + 4, 8, 2 * LANES), F32),
             pltpu.VMEM((8 * LANES, LANES), F32),
-            pltpu.SemaphoreType.DMA((3,)),
         ],
         compiler_params=pltpu.CompilerParams(vmem_limit_bytes=VMEM_BYTES),
         name="near_north",
-    )(nxt, near, pack, ya, yb, chosen, weights, early)
-
-
-def far_north_kernel(before, pack, ya, yb, nxt, rim, yav, ybv, pv, main, out, ex, ey, sems):
-    count = out.shape[3]
-    columns = pl.ds(LANES, count)
-    copies = started([(ya, yav), (yb, ybv), (before.at[:, :, :, columns], main), (pack, pv)], sems)
-    wait_all(copies[:2])
-    fill_north(rim, yav, ybv)
-    add_north(rim, pv, main, out, ex, ey, 1, 1 + count // LANES, lambda: wait_all(copies[2:]))
-    wait_all(started([(out, nxt.at[:, :, :, columns])], sems.at[pl.ds(4, 1)]))
-
-
-def far_north(nxt, pack, ya, yb):
-    _, rows, cols, depth = nxt.shape
-    rest = depth - LANES
-    part = pltpu.VMEM((3, rows, cols, rest), F32)
+    )(main, pack, ya, yb, chosen, weights, early)
+
+
+def far_north_kernel(main, pack, near, ya, yb, nxt, rim, out, ex, ey, sems):
+    stores = started([(near, nxt.at[:, :, :, pl.ds(0, LANES)])], sems.at[pl.ds(0, 1)])
+    columns = pl.ds(LANES, out.shape[3] - LANES)
+
+    def done(row, count):
+        part = (slice(None), pl.ds(row, count), slice(None), columns)
+        stores.extend(started([(out.at[part], nxt.at[part])], sems.at[pl.ds(len(stores), 1)]))
+
+    fill_north(rim, ya, yb)
+    add_north(rim, pack, main, out, ex, ey, 1, out.shape[3] // LANES, done=done, parts=4)
+    wait_all(stores)
+
+
+def far_north(main, pack, near, ya, yb):
+    _, rows, _, depth = main.shape
     return pl.pallas_call(
         far_north_kernel,
-        out_shape=jax.ShapeDtypeStruct(nxt.shape, F32),
-        in_specs=[HBM_SPEC] * 4,
+        out_shape=pltpu.HBM(main.shape, F32),
+        in_specs=[VMEM_SPEC] * 5,
         out_specs=HBM_SPEC,
-        input_output_aliases={0: 0},
         scratch_shapes=[
             pltpu.VMEM((3, rows + 4, 24, depth), F32),
-            pltpu.VMEM(ya.shape, F32),
-            pltpu.VMEM(ya.shape, F32),
-            pltpu.VMEM(pack.shape, F32),
-            part,
-            part,
+            pltpu.VMEM(main.shape, F32),
             pltpu.VMEM((rows + 4, 8, depth), F32),
             pltpu.VMEM((rows + 4, 8, depth), F32),
             pltpu.SemaphoreType.DMA((5,)),
         ],
         compiler_params=pltpu.CompilerParams(vmem_limit_bytes=VMEM_BYTES),
         name="far_north",
-    )(nxt, pack, ya, yb)
+    )(main, pack, near, ya, yb)
 
 
 def north_kernel(now, xa, xb, ya, yb):
@@ -595,37 +584,21 @@
     )(now, xa, xb)
 
 
-def request_kernel(source, count, req, pos):
+def build_requests(source, req, pos):
     shape = (LANES, LANES)
     src = source[...]
-    slot = iota((1, LANES), 1)
-    live = slot < count[0]
     tile = src // LANES
     local = (src % LANES).astype(F32)
-    mine = jnp.where((iota(shape, 0) == tile) & live, 1.0, 0.0)
+    mine = jnp.where(iota(shape, 0) == tile, 1.0, 0.0)
     earlier = jnp.where(iota(shape, 0) < iota(shape, 1), 1.0, 0.0)
     before = jnp.dot(mine, earlier, preferred_element_type=F32)
     rank = jnp.sum(before * mine, axis=0, keepdims=True)
     wanted = mine * local
     lane = iota(shape, 1)
-    first = jnp.sum(jnp.where(rank < 0.5, wanted, 0.0), axis=1, keepdims=True)
-    second = jnp.sum(jnp.where(rank > 0.5, wanted, 0.0), axis=1, keepdims=True)
+    first = jnp.sum(jnp.where(rank == 0.0, wanted, 0.0), axis=1, keepdims=True)
+    second = jnp.sum(jnp.where(rank == 1.0, wanted, 0.0), axis=1, keepdims=True)
     req[...] = jnp.where(lane == 0, first, jnp.where(lane == 1, second, 0.0)).astype(jnp.int32)
-    pos[...] = jnp.where(live, tile * 2 + rank.astype(jnp.int32), -1)
-
-
-def make_requests(source, count):
-    return pl.pallas_call(
-        request_kernel,
-        out_shape=(
-            jax.ShapeDtypeStruct((LANES, LANES), jnp.int32),
-            jax.ShapeDtypeStruct((1, LANES), jnp.int32),
-        ),
-        in_specs=[VMEM_SPEC, SMEM_SPEC],
-        out_specs=(VMEM_SPEC, VMEM_SPEC),
-        compiler_params=pltpu.CompilerParams(vmem_limit_bytes=VMEM_BYTES),
-        name="requests",
-    )(source.reshape(1, LANES), count)
+    pos[...] = tile * 2 + jnp.minimum(rank, 1.0).astype(jnp.int32)
 
 
 def columns_of(ker):
@@ -657,7 +630,7 @@
 def history_part(hist, ker):
     return pl.pallas_call(
         history_kernel,
-        out_shape=jax.ShapeDtypeStruct((2,) + hist.shape[1:], F32),
+        out_shape=pltpu.VMEM((2,) + hist.shape[1:], F32),
         in_specs=[VMEM_SPEC, VMEM_SPEC],
         out_specs=VMEM_SPEC,
         compiler_params=pltpu.CompilerParams(vmem_limit_bytes=VMEM_BYTES),
@@ -665,7 +638,7 @@
     )(hist, ker)
 
 
-def response_kernel(ans, pos, base, ker, out):
+def response_kernel(ans, pos, count, base, ker, out):
     at = pos[...]
     chosen = jnp.where(iota((2 * LANES, LANES), 0) == at, 1.0, 0.0)
     forces = lax.dot_general(
@@ -674,20 +647,20 @@
     k = columns_of(ker)
     modes = k.shape[0]
     early, late = forces[:modes], forces[modes:]
-    live = at >= 0
+    live = iota((1, LANES), 1) < count[...]
     out[0] = jnp.where(live, base[0] + k[:, 0:1] * early, 0.0)
     out[1] = jnp.where(live, base[1] + k[:, 0:1] * late + k[:, 1:2] * early, 0.0)
 
 
-def make_responses(ans, pos, base, ker):
+def make_responses(ans, pos, count, base, ker):
     return pl.pallas_call(
         response_kernel,
         out_shape=jax.ShapeDtypeStruct(base.shape, F32),
-        in_specs=[VMEM_SPEC] * 4,
+        in_specs=[VMEM_SPEC] * 5,
         out_specs=VMEM_SPEC,
         compiler_params=pltpu.CompilerParams(vmem_limit_bytes=VMEM_BYTES),
         name="responses",
-    )(ans, pos, base, ker)
+    )(ans, pos, count.reshape(1, 1), base, ker)
 
 
 def swap(array, axis, first):
@@ -739,25 +712,26 @@
 
 def steps(prev, now, medium, offset, source, count, history, part, kernels):
     held = in_vmem(now)
-    east = east_pack(in_hbm(now), in_hbm(prev), *medium)
-    east = east_swaps(*east)
-    req, pos = make_requests(source, count)
+    pa, pb, req, pos = east_pack(
+        in_hbm(now), in_hbm(prev), *medium, in_hbm(source.reshape(1, LANES))
+    )
+    east = east_swaps(in_vmem(pa), in_vmem(pb))
     asked = exchange(req)
     north = north_edges(held, *east)
     north = north_swaps(*north)
-    base = history_part(history, kernels)
     prepared = prepare(in_vmem(asked), offset, part)
     main = first_main(held, *east, in_hbm(prev), *medium)
-    north, main, base, prepared = lax.optimization_barrier((north, main, base, prepared))
+    north, main, prepared = lax.optimization_barrier((north, main, prepared))
     mid, ya, yb, top = first_north(*main, *north)
     north = north_swaps(ya, yb)
     early = early_forces(top, *prepared)
-    disp_mid, rest, far, near, close = second_main(mid, in_hbm(now), *medium)
-    north, rest, far, near, close, early = lax.optimization_barrier((north, rest, far, near, close, early))
-    disp_next, ya, yb, ans = near_north(in_hbm(rest), near, close, *north, *prepared, early)
+    disp_mid, main, pack = second_main(mid, in_hbm(now), *medium)
+    north, main, pack, early = lax.optimization_barrier((north, main, pack, early))
+    near, ans = near_north(main, pack, *north, *prepared, early)
     back = exchange(ans)
-    disp_next = far_north(in_hbm(disp_next), in_hbm(far), in_hbm(ya), in_hbm(yb))
-    responses = make_responses(back, pos, base, kernels)
+    base = in_vmem(history_part(history, kernels))
+    disp_next = far_north(in_vmem(main), in_vmem(pack), in_vmem(near), *(in_vmem(a) for a in north))
+    responses = make_responses(back, in_vmem(pos), count, base, kernels)
     return disp_mid, disp_next, responses
 
 

time: 93.9 us -> 87.7 us (0.934)
  blocking collectives: 0 us -> 24.5 us
  starting transfers between devices: 34.8 us -> 20.3 us
  waiting for transfers between devices: 22.7 us -> 14.1 us
  Pallas kernels: 33.8 us -> 26.2 us
    all_to_all x0 -> x1, blocking collectives: none -> 24.5 us  [exchange(): lax.all_to_all(rows, ('gx', 'gy'), split_axis=0, concat_axis=0, tiled=True)]
    all_to_all x2 -> x1, starting transfers between devices: 23.1 us -> 8.92 us  [exchange(): lax.all_to_all(rows, ('gx', 'gy'), split_axis=0, concat_axis=0, tiled=True)]
    all_to_all x2 -> x1, waiting for transfers between devices: 14.3 us -> 6.09 us  [exchange(): lax.all_to_all(rows, ('gx', 'gy'), split_axis=0, concat_axis=0, tiled=True)]
    pallas_call x5 -> x4, Pallas kernels: 12 us -> 8.13 us  [the longest x1 3.62 us: near_north(): pl.pallas_call(near_north_kernel, out_shape=(pltpu.VMEM((3, rows, cols, L...]
    pallas_call x1, Pallas kernels: 4.63 us -> 2.62 us  [first_north(): pl.pallas_call(first_north_kernel, out_shape=(pltpu.VMEM(main.shape, F32)...]
  transfers between devices with their start and end apart: 8 -> 7, of which waited for: 3 -> 2; matrix products, arithmetic and copies ran while one was open for 0% -> 0% of each run, Pallas kernels for 22% -> 20%
where the time goes in v2:
time: 87.7 us; the launch traced here: 87.4 us
  Pallas kernels  26.2 us (30%)
  blocking collectives  24.5 us (28%)
  starting transfers between devices  20.3 us (23%)
  waiting for transfers between devices  14.1 us (16%)
  between operations  1.52 us (2%)
    all_to_all x1, blocking collectives, exchange(): lax.all_to_all(rows, ('gx', 'gy'), split_axis=0, concat_axis=0, tiled=True)  24.5 us
    ppermute x6, starting transfers between devices, swap(): return in_vmem(lax.ppermute(array, axis, pairs))  11.4 us
    all_to_all x1, starting transfers between devices, exchange(): lax.all_to_all(rows, ('gx', 'gy'), split_axis=0, concat_axis=0, tiled=True)  8.92 us
    ppermute x6, waiting for transfers between devices, swap(): return in_vmem(lax.ppermute(array, axis, pairs))  8.04 us
    pallas_call x1, Pallas kernels, first_main(): pl.pallas_call(first_main_kernel, out_shape=(pltpu.VMEM((3, wide, cols, d...  7.08 us
    all_to_all x1, waiting for transfers between devices, exchange(): lax.all_to_all(rows, ('gx', 'gy'), split_axis=0, concat_axis=0, tiled=True)  6.09 us
    pallas_call x1, Pallas kernels, second_main(): pl.pallas_call(second_main_kernel, out_shape=(pltpu.HBM(prev.shape, F32),...  5.74 us
    pallas_call x1, Pallas kernels, near_north(): pl.pallas_call(near_north_kernel, out_shape=(pltpu.VMEM((3, rows, cols, L...  3.62 us
  transfers between devices with their start and end apart: 7, of which 2 were waited for; matrix products, arithmetic and copies ran while one was open for 0% of the time, Pallas kernels for 20%

profile of v2, /device:TPU:1, one launch (start us, length us, event | category | flops | bytes accessed | tf_op | source)
XLA Modules:
  0.0 87.4 jit_solution(8602245475246366938)
XLA Ops:
  0.6 0.0 copy-start
  0.6 1.5 %east_pack.1 = (f32[24,16,384]{2,1,0:T(8,128)S(1)}, f32[24,16,384]{2,1,0:T(8,128)S(1)}, s32[128,128]{1,0:T(8,128)S(1)}, s32[1,128]{1,0:T(1,128)S(1)}) custom-call(f32[3,16,16,384]{3,2,1,0:T(8,128)} %prev.5, f32[3,16,16,384]{3,2,1,0:T(8,128)} %prev.4, f32[16,16,384]{2,1,0:T(8,128)} %buoy.5, f32[16,16,384]{2,1,0:T(8,128)} %mu.5, f32[16,16,384]{2,1,0:T(8,128)} %lam.5, ...), custom_call_target="tpu_custom_call" | custom-call | tf_op jit(solution)/shard_map/east_pack/pallas_call | solution.py:186
  2.2 1.5 %collective-permute-start = (f32[24,16,384]{2,1,0:T(8,128)S(1)}, f32[24,16,384]{2,1,0:T(8,128)S(1)}, u32[]{:S(2)}, u32[]{:S(2)}) collective-permute-start(f32[24,16,384]{2,1,0:T(8,128)S(1)} %get-tuple-element.33), channel_id=1, source_target_pairs={{0,8},{8,0},{16,24},{24,16},{32,40},{40,32},{48,56},{56,48},{64,72... | collective-permute-start | bytes 1769480 | tf_op jit(solution)/shard_map/ppermute | solution.py:670
  3.7 3.3 %collective-permute-start.1 = (f32[24,16,384]{2,1,0:T(8,128)S(1)}, f32[24,16,384]{2,1,0:T(8,128)S(1)}, u32[]{:S(2)}, u32[]{:S(2)}) collective-permute-start(f32[24,16,384]{2,1,0:T(8,128)S(1)} %get-tuple-element.34), channel_id=1, source_target_pairs={{8,16},{16,8},{24,32},{32,24},{40,48},{48,40},{56,64},{64,56},{72,... | collective-permute-start | bytes 1769480 | tf_op jit(solution)/shard_map/ppermute | solution.py:670
  7.0 8.0 %collective-permute-done.1.xb = f32[24,16,384]{2,1,0:T(8,128)S(1)} collective-permute-done((f32[24,16,384]{2,1,0:T(8,128)S(1)}, f32[24,16,384]{2,1,0:T(8,128)S(1)}, u32[]{:S(2)}, u32[]{:S(2)}) %collective-permute-start.1) | collective-permute-done | bytes 589856 | tf_op jit(solution)/shard_map/ppermute | solution.py:670
  15.0 0.1 north_edges.1
  15.1 4.1 %collective-permute-start.2 = (f32[3,24,2,384]{3,2,1,0:T(2,128)S(1)}, f32[3,24,2,384]{3,2,1,0:T(2,128)S(1)}, u32[]{:S(2)}, u32[]{:S(2)}) collective-permute-start(f32[3,24,2,384]{3,2,1,0:T(2,128)S(1)} %get-tuple-element.35), channel_id=1, source_target_pairs={{0,1},{1,0},{2,3},{3,2},{4,5},{5,4},{6,7},{7,6},{8,9},{9,8},{10,11... | collective-permute-start | bytes 663560 | tf_op jit(solution)/shard_map/ppermute | solution.py:670
  19.2 0.7 collective-permute-start.3
  19.9 24.5 %all_to_all.10 = s32[128,1,128]{2,1,0:T(1,128)S(1)} all-to-all(s32[128,1,128]{2,1,0:T(1,128)S(1)} %bitcast.17), channel_id=1, replica_groups=mesh['gx'=16,'gy'=8] {'gx','gy'}, dimensions={0} | all-to-all | bytes 131072 | tf_op jit(solution)/shard_map/all_to_all | solution.py:709
  44.4 0.5 prepare.1
  44.9 7.1 %first_main.1 = (f32[3,20,16,384]{3,2,1,0:T(8,128)S(1)}, f32[3,20,8,384]{3,2,1,0:T(8,128)S(1)}) custom-call(f32[3,16,16,384]{3,2,1,0:T(8,128)} %prev.4, f32[16,16,384]{2,1,0:T(8,128)} %buoy.5, f32[16,16,384]{2,1,0:T(8,128)} %mu.5, f32[16,16,384]{2,1,0:T(8,128)} %lam.5, f32[3,16,16,384]{3,2,1,0:T(8,128)S(1)} %copy-done, ...), custom_call_target="tpu_custom_call" | custom-call | tf_op jit(solution)/shard_map/first_main/pallas_call | solution.py:235
  52.0 2.6 %first_north.1 = (f32[3,20,16,384]{3,2,1,0:T(8,128)S(1)}, f32[3,20,2,384]{3,2,1,0:T(2,128)S(1)}, f32[3,20,2,384]{3,2,1,0:T(2,128)S(1)}, f32[8,256]{1,0:T(8,128)S(1)}) custom-call(f32[3,20,16,384]{3,2,1,0:T(8,128)S(1)} %get-tuple-element.42.main, f32[3,20,8,384]{3,2,1,0:T(8,128)S(1)} %get-tuple-element.43.pack, ...), custom_call_target="tpu_custom_call" | custom-call | tf_op jit(solution)/shard_map/first_north/pallas_call | solution.py:277
  54.6 1.2 %collective-permute-start.4 = (f32[3,20,2,384]{3,2,1,0:T(2,128)S(1)}, f32[3,20,2,384]{3,2,1,0:T(2,128)S(1)}, u32[]{:S(2)}, u32[]{:S(2)}) collective-permute-start(f32[3,20,2,384]{3,2,1,0:T(2,128)S(1)} %get-tuple-element.48), channel_id=1, source_target_pairs={{0,1},{1,0},{2,3},{3,2},{4,5},{5,4},{6,7},{7,6},{8,9},{9,8},{10,11... | collective-permute-start | bytes 552968 | tf_op jit(solution)/shard_map/ppermute | solution.py:670
  55.9 0.7 collective-permute-start.5
  56.5 5.7 %second_main.1 = (f32[3,16,16,384]{3,2,1,0:T(8,128)}, f32[3,16,16,384]{3,2,1,0:T(8,128)S(1)}, f32[3,16,8,384]{3,2,1,0:T(8,128)S(1)}) custom-call(f32[3,16,16,384]{3,2,1,0:T(8,128)} %prev.5, f32[16,16,384]{2,1,0:T(8,128)} %buoy.5, f32[16,16,384]{2,1,0:T(8,128)} %mu.5, f32[16,16,384]{2,1,0:T(8,128)} %lam.5, f32[3,20,16,384]{3,2,1,0:T(8,128)S(1)} %get-tuple-element.46.v), custom_call_target="tpu_custom_call" | custom-call | tf_op jit(solution)/shard_map/second_main/pallas_call | solution.py:309
  62.3 0.9 %early_forces.1.early = f32[256,64]{1,0:T(8,128)S(1)} custom-call(f32[8,256]{1,0:T(8,128)S(1)} %get-tuple-element.52.top, f32[256,128]{1,0:T(8,128)S(1)} %get-tuple-element.53.chosen, f32[3,128,64]{2,1,0:T(8,128)S(1)} %get-tuple-element.54.weights), custom_call_target="tpu_custom_call" | custom-call | tf_op jit(solution)/shard_map/early_forces/pallas_call | solution.py:482
  63.2 0.0 copy-start.1
  63.3 3.6 %near_north.1 = (f32[3,16,16,128]{3,2,1,0:T(8,128)S(1)}, f32[256,128]{1,0:T(8,128)}) custom-call(f32[3,16,16,384]{3,2,1,0:T(8,128)S(1)} %get-tuple-element.55.main, f32[3,16,8,384]{3,2,1,0:T(8,128)S(1)} %get-tuple-element.56.pack, f32[3,20,2,384]{3,2,1,0:T(2,128)S(1)} %collective-permute-done.4.ya, f32[3,20,2,384]{3,2,1,0:T(2,128)S(1)} %collective-permute-done.5.yb, ...), custom_call_target="tpu_custom_call" | custom-call | tf_op jit(solution)/shard_map/near_north/pallas_call | solution.py:503
  66.9 0.7 copy-done.2
  67.6 8.9 %all-to-all-start.1 = ((f32[128,2,128]{2,1,0:T(2,128)}), f32[128,2,128]{2,1,0:T(2,128)S(1)}, u32[]{:S(2)}, u32[]{:S(2)}) async-start(f32[128,2,128]{2,1,0:T(2,128)} %bitcast.6), calls=%async_computation.1 | async-start | bytes 262144 | tf_op jit(solution)/shard_map/all_to_all | solution.py:709
  77.3 0.7 history.1.base
  78.0 2.3 %far_north.1 = f32[3,16,16,384]{3,2,1,0:T(8,128)} custom-call(f32[3,16,16,384]{3,2,1,0:T(8,128)S(1)} %get-tuple-element.55.main, f32[3,16,8,384]{3,2,1,0:T(8,128)S(1)} %get-tuple-element.56.pack, f32[3,16,16,128]{3,2,1,0:T(8,128)S(1)} %copy-done.3, f32[3,20,2,384]{3,2,1,0:T(2,128)S(1)} %collective-permute-done.4.ya, ...), custom_call_target="tpu_custom_call" | custom-call | tf_op jit(solution)/shard_map/far_north/pallas_call | solution.py:534
  80.3 6.1 %all-to-all-done.1 = f32[128,2,128]{2,1,0:T(2,128)S(1)} async-done(((f32[128,2,128]{2,1,0:T(2,128)}), f32[128,2,128]{2,1,0:T(2,128)S(1)}, u32[]{:S(2)}, u32[]{:S(2)}) %all-to-all-start.1) | async-done | bytes 131104 | tf_op jit(solution)/shard_map/all_to_all | solution.py:709
  86.4 1.1 %responses.1 = f32[2,64,128]{2,1,0:T(8,128)} custom-call(f32[256,128]{1,0:T(8,128)S(1)} %bitcast.12, s32[1,128]{1,0:T(1,128)S(1)} %get-tuple-element.62.pos, s32[1,1]{1,0:T(1,128)} %bitcast.11.count, f32[2,64,128]{2,1,0:T(8,128)S(1)} %history.1.base, f32[32,64]{1,0:T(8,128)S(1)} %bitcast.15), custom_call_target="tpu_custom_call" | custom-call | tf_op jit(solution)/shard_map/responses/pallas_call | solution.py:656
  (16 shorter events, 0.0 us)
Async XLA Ops:
  0.6 14.4 %copy-start = (f32[3,16,16,384]{3,2,1,0:T(8,128)S(1)}, f32[3,16,16,384]{3,2,1,0:T(8,128)}, u32[]{:S(2)}) copy-start(f32[3,16,16,384]{3,2,1,0:T(8,128)} %prev.5) | copy-start | bytes 3538948
  2.2 4.8 %collective-permute-start = (f32[24,16,384]{2,1,0:T(8,128)S(1)}, f32[24,16,384]{2,1,0:T(8,128)S(1)}, u32[]{:S(2)}, u32[]{:S(2)}) collective-permute-start(f32[24,16,384]{2,1,0:T(8,128)S(1)} %get-tuple-element.33), channel_id=1, source_target_pairs={{0,8},{8,0},{16,24},{24,16},{32,40},{40,32},{48,56},{56,48},{64,72... | collective-permute-start | bytes 1769480 | tf_op jit(solution)/shard_map/ppermute | solution.py:670
  3.7 40.7 %copy-start.5 = (f32[192,64]{0,1:T(8,128)S(1)}, f32[192,64]{0,1:T(8,128)}, u32[]{:S(2)}) copy-start(f32[192,64]{0,1:T(8,128)} %param.20) | copy-start | bytes 147460
  3.7 40.7 %copy-start.6 = (s32[128,2]{0,1:T(2,128)S(1)}, s32[128,2]{0,1:T(2,128)}, u32[]{:S(2)}) copy-start(s32[128,2]{0,1:T(2,128)} %param.16) | copy-start | bytes 3076
  3.7 11.3 %collective-permute-start.1 = (f32[24,16,384]{2,1,0:T(8,128)S(1)}, f32[24,16,384]{2,1,0:T(8,128)S(1)}, u32[]{:S(2)}, u32[]{:S(2)}) collective-permute-start(f32[24,16,384]{2,1,0:T(8,128)S(1)} %get-tuple-element.34), channel_id=1, source_target_pairs={{8,16},{16,8},{24,32},{32,24},{40,48},{48,40},{56,64},{64,56},{72,... | collective-permute-start | bytes 1769480 | tf_op jit(solution)/shard_map/ppermute | solution.py:670
  15.1 36.9 %collective-permute-start.2 = (f32[3,24,2,384]{3,2,1,0:T(2,128)S(1)}, f32[3,24,2,384]{3,2,1,0:T(2,128)S(1)}, u32[]{:S(2)}, u32[]{:S(2)}) collective-permute-start(f32[3,24,2,384]{3,2,1,0:T(2,128)S(1)} %get-tuple-element.35), channel_id=1, source_target_pairs={{0,1},{1,0},{2,3},{3,2},{4,5},{5,4},{6,7},{7,6},{8,9},{9,8},{10,11... | collective-permute-start | bytes 663560 | tf_op jit(solution)/shard_map/ppermute | solution.py:670
  19.2 32.8 %collective-permute-start.3 = (f32[3,24,2,384]{3,2,1,0:T(2,128)S(1)}, f32[3,24,2,384]{3,2,1,0:T(2,128)S(1)}, u32[]{:S(2)}, u32[]{:S(2)}) collective-permute-start(f32[3,24,2,384]{3,2,1,0:T(2,128)S(1)} %get-tuple-element.36), channel_id=1, source_target_pairs={{1,2},{2,1},{3,4},{4,3},{5,6},{6,5},{9,10},{10,9},{11,12},{12,11},... | collective-permute-start | bytes 663560 | tf_op jit(solution)/shard_map/ppermute | solution.py:670
  54.6 8.6 %collective-permute-start.4 = (f32[3,20,2,384]{3,2,1,0:T(2,128)S(1)}, f32[3,20,2,384]{3,2,1,0:T(2,128)S(1)}, u32[]{:S(2)}, u32[]{:S(2)}) collective-permute-start(f32[3,20,2,384]{3,2,1,0:T(2,128)S(1)} %get-tuple-element.48), channel_id=1, source_target_pairs={{0,1},{1,0},{2,3},{3,2},{4,5},{5,4},{6,7},{7,6},{8,9},{9,8},{10,11... | collective-permute-start | bytes 552968 | tf_op jit(solution)/shard_map/ppermute | solution.py:670
  55.9 7.4 %collective-permute-start.5 = (f32[3,20,2,384]{3,2,1,0:T(2,128)S(1)}, f32[3,20,2,384]{3,2,1,0:T(2,128)S(1)}, u32[]{:S(2)}, u32[]{:S(2)}) collective-permute-start(f32[3,20,2,384]{3,2,1,0:T(2,128)S(1)} %get-tuple-element.49), channel_id=1, source_target_pairs={{1,2},{2,1},{3,4},{4,3},{5,6},{6,5},{9,10},{10,9},{11,12},{12,11},... | collective-permute-start | bytes 552968 | tf_op jit(solution)/shard_map/ppermute | solution.py:670
  63.2 14.0 %copy-start.1 = (f32[31,64,128]{2,1,0:T(8,128)S(1)}, f32[31,64,128]{2,1,0:T(8,128)}, u32[]{:S(2)}) copy-start(f32[31,64,128]{2,1,0:T(8,128)} %hist.1) | copy-start | bytes 3047428
  63.3 14.0 %copy-start.4 = (f32[64,32]{0,1:T(8,128)S(1)}, f32[64,32]{0,1:T(8,128)}, u32[]{:S(2)}) copy-start(f32[64,32]{0,1:T(8,128)} %param.21) | copy-start | bytes 24580
  66.9 0.7 copy-start.2
  67.6 18.7 %all-to-all-start.1 = ((f32[128,2,128]{2,1,0:T(2,128)}), f32[128,2,128]{2,1,0:T(2,128)S(1)}, u32[]{:S(2)}, u32[]{:S(2)}) async-start(f32[128,2,128]{2,1,0:T(2,128)} %bitcast.6), calls=%async_computation.1 | async-start | bytes 262144 | tf_op jit(solution)/shard_map/all_to_all | solution.py:709
  76.6 1.4 %copy-start.3 = (f32[3,16,16,128]{3,2,1,0:T(8,128)S(1)}, f32[3,16,16,128]{3,2,1,0:T(8,128)}, u32[]{:S(2)}) copy-start(f32[3,16,16,128]{3,2,1,0:T(8,128)} %copy-done.2) | copy-start | bytes 1179652

commit v3 on v2

--- a/solution.py
+++ b/solution.py
@@ -65,74 +65,106 @@
     return [first_of(*four) for four in z_four(below, columns, above)]
 
 
-def step_columns(vp, prev, buoy, mu, lam, out, pack, byx, syz, first, last, ready, done):
+def north_four(lower, upper):
+    sub = iota(lower.shape, 0)
+    zero = jnp.zeros_like(lower)
+    out = ([], [])
+    for s in (1, -1, 2, -2):
+        first, second = [pltpu.roll(tile, (-s) % 8, axis=0) for tile in (lower, upper)]
+        if s > 0:
+            out[0].append(jnp.where(sub < 8 - s, first, second))
+            out[1].append(jnp.where(sub < 8 - s, second, zero))
+        else:
+            out[0].append(jnp.where(sub >= -s, first, zero))
+            out[1].append(jnp.where(sub >= -s, second, first))
+    return out
+
+
+def run_step(vp, prev, buoy, mu, lam, out, pack, work, ready):
+    byx, syz, dyy, dyz, qyx, qyy, qyz, qzz = work
     rows = vp.shape[1] - 4
-    total = vp.shape[3] // LANES
-    span = range(first, last)
+    span = range(vp.shape[3] // LANES)
     lanes = lambda k: pl.ds(k * LANES, LANES)
-
-    def y_four(c, r, h, k):
-        return [vp[c, r, pl.ds(8 + 8 * h + d, 8), lanes(k)] for d in (1, -1, 2, -2)]
-
-    def ends(get):
-        below = get(first - 1) if first > 0 else None
-        above = get(last) if last < total else None
-        return below, [get(k) for k in span], above
-
-    def inner(r, carry):
+    tile = lambda h: pl.ds(8 * h, 8)
+
+    def inner(r, full):
+        i = r - 2
         for h in range(2):
-            here = pl.ds(8 * h, 8)
-            core = pl.ds(8 + 8 * h, 8)
-            dz = z_first(*ends(lambda k: vp[2, r, core, lanes(k)]))
-            for n, k in enumerate(span):
-                byx[r, here, lanes(k - first)] = first_of(*y_four(0, r, h, k))
-                syz[r, here, lanes(k - first)] = first_of(*y_four(1, r, h, k)) + dz[n]
-        return carry
-
-    lax.fori_loop(0, rows + 4, inner, 0)
+            four = z_four(None, [vp[2, r, tile(h), lanes(k)] for k in span], None)
+            for k in span:
+                syz[r, tile(h), lanes(k)] = first_of(*four[k])
+                if full:
+                    qzz[i, tile(h), lanes(k)] = second_of(*four[k])
+        for k in span:
+            for c in range(3 if full else 2):
+                four = north_four(*[vp[c, r, tile(h), lanes(k)] for h in range(2)])
+                for h in range(2):
+                    slope = first_of(*four[h])
+                    if c == 0:
+                        byx[r, tile(h), lanes(k)] = slope
+                    elif c == 1:
+                        syz[r, tile(h), lanes(k)] = syz[r, tile(h), lanes(k)] + slope
+                    if full:
+                        if c > 0:
+                            (dyy, dyz)[c - 1][i, tile(h), lanes(k)] = slope
+                        (qyx, qyy, qyz)[c][i, tile(h), lanes(k)] = second_of(*four[h])
+
+    def each(start, stop, full):
+        def trip(r, carry):
+            inner(r, full)
+            return carry
+
+        lax.fori_loop(start, stop, trip, 0)
+
+    each(0, 2, False)
+    each(2, rows + 2, True)
+    each(rows + 2, rows + 4, False)
+    ready()
 
     def outer(i, carry):
         r = i + 2
         low = iota((8, LANES), 0) < 4
         lower = {}
         for h in range(2):
-            here = pl.ds(8 * h, 8)
-            core = pl.ds(8 + 8 * h, 8)
+            here = tile(h)
 
             def x_four(c, k):
-                return [vp[c, r + d, core, lanes(k)] for d in (1, -1, 2, -2)]
+                return [vp[c, r + d, here, lanes(k)] for d in (1, -1, 2, -2)]
 
             def derived(ref, k):
-                return first_of(*[ref[r + d, here, lanes(k - first)] for d in (1, -1, 2, -2)])
-
-            yz = z_first(*ends(lambda k: first_of(*y_four(2, r, h, k))))
-            xy = z_first(*ends(lambda k: first_of(*x_four(0, k)) + first_of(*y_four(1, r, h, k))))
-            along_z = [z_four(*ends(lambda k: vp[c, r, core, lanes(k)])) for c in range(3)]
-            for n, k in enumerate(span):
-                shear = mu[i, here, lanes(k - first)]
-                both = lam[i, here, lanes(k - first)] + shear
-                scale = buoy[i, here, lanes(k - first)] * 0.12
+                return first_of(*[ref[r + d, here, lanes(k)] for d in (1, -1, 2, -2)])
+
+            yz = z_first(None, [dyz[i, here, lanes(k)] for k in span], None)
+            xy = z_first(None, [first_of(*x_four(0, k)) + dyy[i, here, lanes(k)] for k in span], None)
+            along_z = [z_four(None, [vp[c, r, here, lanes(k)] for k in span], None) for c in range(2)]
+            for k in span:
+                shear = mu[i, here, lanes(k)]
+                both = lam[i, here, lanes(k)] + shear
+                scale = buoy[i, here, lanes(k)] * 0.12
                 for which, factor in enumerate((shear, both, scale)):
                     if h == 0:
                         lower[which, k] = factor
                     else:
-                        pack[which, i, :, lanes(k - first)] = jnp.where(low, lower[which, k], factor)
-                mixed = [derived(syz, k), derived(byx, k) + yz[n], xy[n]]
+                        pack[which, i, :, lanes(k)] = jnp.where(low, lower[which, k], factor)
+                mixed = [derived(syz, k), derived(byx, k) + yz[k], xy[k]]
                 for c in range(3):
-                    centre = vp[c, r, core, lanes(k)]
-                    q = [second_of(*x_four(c, k)), second_of(*y_four(c, r, h, k)), second_of(*along_z[c][n])]
+                    centre = vp[c, r, here, lanes(k)]
+                    q = [
+                        second_of(*x_four(c, k)),
+                        (qyx, qyy, qyz)[c][i, here, lanes(k)],
+                        second_of(*along_z[c][k]) if c < 2 else qzz[i, here, lanes(k)],
+                    ]
                     laplace = (q[0] + q[1]) + (q[2] - centre * 5.625)
                     along = (q[c] - centre * 1.875) + mixed[c] * (1.0 / 3.0)
                     update = shear * laplace + both * along
-                    out[c, i, here, lanes(k - first)] = (
-                        2.0 * centre - prev[c, i, here, lanes(k - first)]
-                    ) + scale * update
+                    out[c, i, here, lanes(k)] = (2.0 * centre - prev[c, i, here, lanes(k)]) + scale * update
         return carry
 
-    ready()
-    for start in range(0, rows, rows // 4):
-        lax.fori_loop(start, start + rows // 4, outer, 0)
-        done(start, rows // 4)
+    lax.fori_loop(0, rows, outer, 0)
+
+
+def step_work(rows, cols, depth):
+    return [pltpu.VMEM((rows + 4, cols, depth), F32)] * 2 + [pltpu.VMEM((rows, cols, depth), F32)] * 6
 
 
 def surface_rows(field, first):
@@ -199,33 +231,24 @@
     )(now, prev, buoy, mu, lam, source)
 
 
-def clear_north(vp):
-    none = jnp.zeros((vp.shape[0], vp.shape[1], 2, vp.shape[3]), F32)
-    vp[:, :, 6:8, :] = none
-    vp[:, :, 24:26, :] = none
-
-
-def first_main_kernel(prev, buoy, mu, lam, now, xa, xb, out, pack, vp, pv, bv, mv, lv, byx, syz, sems):
+def first_main_kernel(prev, buoy, mu, lam, now, xa, xb, out, pack, vp, pv, bv, mv, lv, *work):
     rows = now.shape[1]
     own = pl.ds(2, rows)
     copies = started(
-        [(prev, pv.at[:, own])] + [(src, dst.at[own]) for src, dst in ((buoy, bv), (mu, mv), (lam, lv))], sems
+        [(prev, pv.at[:, own])] + [(src, dst.at[own]) for src, dst in ((buoy, bv), (mu, mv), (lam, lv))],
+        work[-1],
     )
     odd = parity("gx")
-    vp[:, 4 : rows + 4, 8:24, :] = now[...]
+    vp[:, 4 : rows + 4] = now[...]
     for edge, side in ((xa, 1 - odd), (xb, odd)):
         four = pl.ds((rows + 4) * side, 4)
         two = pl.ds((rows + 2) * side, 2)
         for c in range(3):
-            vp[c, four, 8:24, :] = edge[4 * c : 4 * c + 4]
+            vp[c, four] = edge[4 * c : 4 * c + 4]
             pv[c, two] = edge[12 + 2 * c : 14 + 2 * c]
         for n, field in enumerate((bv, mv, lv)):
             field[two] = edge[18 + 2 * n : 20 + 2 * n]
-    clear_north(vp)
-    step_columns(
-        vp, pv, bv, mv, lv, out, pack, byx, syz, 0, now.shape[3] // LANES,
-        lambda: wait_all(copies), lambda row, count: None,
-    )
+    run_step(vp, pv, bv, mv, lv, out, pack, work[:-1], lambda: wait_all(copies))
 
 
 def first_main(now, xa, xb, prev, buoy, mu, lam):
@@ -238,13 +261,12 @@
         in_specs=[HBM_SPEC] * 4 + [VMEM_SPEC] * 3,
         out_specs=(VMEM_SPEC,) * 2,
         scratch_shapes=[
-            pltpu.VMEM((3, wide + 4, 32, depth), F32),
+            pltpu.VMEM((3, wide + 4, cols, depth), F32),
             pltpu.VMEM((3, wide, cols, depth), F32),
             one,
             one,
             one,
-            pltpu.VMEM((wide + 4, cols, depth), F32),
-            pltpu.VMEM((wide + 4, cols, depth), F32),
+            *step_work(wide, cols, depth),
             pltpu.SemaphoreType.DMA((4,)),
         ],
         compiler_params=pltpu.CompilerParams(vmem_limit_bytes=VMEM_BYTES),
@@ -289,16 +311,12 @@
     )(main, pack, ya, yb)
 
 
-def second_main_kernel(prev, buoy, mu, lam, v, mid, out, pack, vp, pv, bv, mv, lv, byx, syz, sems):
+def second_main_kernel(prev, buoy, mu, lam, vp, mid, out, pack, pv, bv, mv, lv, *work):
+    sems = work[-1]
     rows = prev.shape[1]
-    total = prev.shape[3] // LANES
     copies = started([(prev, pv), (buoy, bv), (mu, mv), (lam, lv)], sems)
-    stores = started([(v.at[:, pl.ds(2, rows)], mid)], sems.at[pl.ds(4, 1)])
-    vp[:, :, 8:24, :] = v[...]
-    clear_north(vp)
-    step_columns(
-        vp, pv, bv, mv, lv, out, pack, byx, syz, 0, total, lambda: wait_all(copies), lambda row, count: None
-    )
+    stores = started([(vp.at[:, pl.ds(2, rows)], mid)], sems.at[pl.ds(4, 1)])
+    run_step(vp, pv, bv, mv, lv, out, pack, work[:-1], lambda: wait_all(copies))
     wait_all(stores)
 
 
@@ -308,21 +326,15 @@
     one = pltpu.VMEM((rows, cols, depth), F32)
     return pl.pallas_call(
         second_main_kernel,
-        out_shape=(
-            pltpu.HBM(prev.shape, F32),
-            whole,
-            pltpu.VMEM((3, rows, 8, depth), F32),
-        ),
+        out_shape=(pltpu.HBM(prev.shape, F32), whole, pltpu.VMEM((3, rows, 8, depth), F32)),
         in_specs=[HBM_SPEC] * 4 + [VMEM_SPEC],
         out_specs=(HBM_SPEC,) + (VMEM_SPEC,) * 2,
         scratch_shapes=[
-            pltpu.VMEM((3, rows + 4, 32, depth), F32),
             whole,
             one,
             one,
             one,
-            pltpu.VMEM((rows + 4, cols, depth), F32),
-            pltpu.VMEM((rows + 4, cols, depth), F32),
+            *step_work(rows, cols, depth),
             pltpu.SemaphoreType.DMA((5,)),
         ],
         compiler_params=pltpu.CompilerParams(vmem_limit_bytes=VMEM_BYTES),
@@ -704,9 +716,9 @@
     )
 
 
-def exchange(array):
-    rows = array.reshape(LANES, -1, LANES)
-    out = lax.all_to_all(rows, ("gx", "gy"), split_axis=0, concat_axis=0, tiled=True)
+def exchange(array, place=lambda rows: rows):
+    rows = place(array.reshape(LANES, -1, LANES))
+    out = lax.all_to_all(rows, ("gx", "gy"), split_axis=0, concat_axis=0)
     return out.reshape(array.shape)
 
 

time: 87.7 us -> 86.4 us (0.985)
  Pallas kernels: 26.2 us -> 24.3 us
    pallas_call x1, Pallas kernels: 7.08 us -> 6.05 us  [first_main(): pl.pallas_call(first_main_kernel, out_shape=(pltpu.VMEM((3, wide, cols, d...]
  transfers between devices with their start and end apart: 7 -> 7, of which waited for: 2 -> 2; matrix products, arithmetic and copies ran while one was open for 0% -> 0% of each run, Pallas kernels for 20% -> 18%
where the time goes in v3:
time: 86.4 us; the launch traced here: 86 us
  blocking collectives  24.5 us (28%)
  Pallas kernels  24.3 us (28%)
  starting transfers between devices  20.8 us (24%)
  waiting for transfers between devices  14.1 us (16%)
  between operations  1.52 us (2%)
    all_to_all x1, blocking collectives, exchange(): out = lax.all_to_all(rows, ('gx', 'gy'), split_axis=0, concat_axis=0)  24.5 us
    ppermute x6, starting transfers between devices, swap(): return in_vmem(lax.ppermute(array, axis, pairs))  11.4 us
    all_to_all x1, starting transfers between devices, exchange(): out = lax.all_to_all(rows, ('gx', 'gy'), split_axis=0, concat_axis=0)  9.4 us
    ppermute x6, waiting for transfers between devices, swap(): return in_vmem(lax.ppermute(array, axis, pairs))  8.04 us
    all_to_all x1, waiting for transfers between devices, exchange(): out = lax.all_to_all(rows, ('gx', 'gy'), split_axis=0, concat_axis=0)  6.09 us
    pallas_call x1, Pallas kernels, first_main(): pl.pallas_call(first_main_kernel, out_shape=(pltpu.VMEM((3, wide, cols, d...  6.05 us
    pallas_call x1, Pallas kernels, second_main(): pl.pallas_call(second_main_kernel, out_shape=(pltpu.HBM(prev.shape, F32),...  4.91 us
    pallas_call x1, Pallas kernels, near_north(): pl.pallas_call(near_north_kernel, out_shape=(pltpu.VMEM((3, rows, cols, L...  3.62 us
  transfers between devices with their start and end apart: 7, of which 2 were waited for; matrix products, arithmetic and copies ran while one was open for 0% of the time, Pallas kernels for 18%

profile of v3, /device:TPU:1, one launch (start us, length us, event | category | flops | bytes accessed | tf_op | source)
XLA Modules:
  0.0 86.0 jit_solution(17450386050155072439)
XLA Ops:
  0.6 0.0 copy-start
  0.6 1.5 %east_pack.1 = (f32[24,16,384]{2,1,0:T(8,128)S(1)}, f32[24,16,384]{2,1,0:T(8,128)S(1)}, s32[128,128]{1,0:T(8,128)S(1)}, s32[1,128]{1,0:T(1,128)S(1)}) custom-call(f32[3,16,16,384]{3,2,1,0:T(8,128)} %prev.5, f32[3,16,16,384]{3,2,1,0:T(8,128)} %prev.4, f32[16,16,384]{2,1,0:T(8,128)} %buoy.5, f32[16,16,384]{2,1,0:T(8,128)} %mu.5, f32[16,16,384]{2,1,0:T(8,128)} %lam.5, ...), custom_call_target="tpu_custom_call" | custom-call | tf_op jit(solution)/shard_map/east_pack/pallas_call | solution.py:218
  2.2 1.5 %collective-permute-start = (f32[24,16,384]{2,1,0:T(8,128)S(1)}, f32[24,16,384]{2,1,0:T(8,128)S(1)}, u32[]{:S(2)}, u32[]{:S(2)}) collective-permute-start(f32[24,16,384]{2,1,0:T(8,128)S(1)} %get-tuple-element.33), channel_id=1, source_target_pairs={{0,8},{8,0},{16,24},{24,16},{32,40},{40,32},{48,56},{56,48},{64,72... | collective-permute-start | bytes 1769480 | tf_op jit(solution)/shard_map/ppermute | solution.py:682
  3.7 3.3 %collective-permute-start.1 = (f32[24,16,384]{2,1,0:T(8,128)S(1)}, f32[24,16,384]{2,1,0:T(8,128)S(1)}, u32[]{:S(2)}, u32[]{:S(2)}) collective-permute-start(f32[24,16,384]{2,1,0:T(8,128)S(1)} %get-tuple-element.34), channel_id=1, source_target_pairs={{8,16},{16,8},{24,32},{32,24},{40,48},{48,40},{56,64},{64,56},{72,... | collective-permute-start | bytes 1769480 | tf_op jit(solution)/shard_map/ppermute | solution.py:682
  7.0 8.0 %collective-permute-done.1.xb = f32[24,16,384]{2,1,0:T(8,128)S(1)} collective-permute-done((f32[24,16,384]{2,1,0:T(8,128)S(1)}, f32[24,16,384]{2,1,0:T(8,128)S(1)}, u32[]{:S(2)}, u32[]{:S(2)}) %collective-permute-start.1) | collective-permute-done | bytes 589856 | tf_op jit(solution)/shard_map/ppermute | solution.py:682
  15.0 0.1 north_edges.1
  15.1 4.1 %collective-permute-start.2 = (f32[3,24,2,384]{3,2,1,0:T(2,128)S(1)}, f32[3,24,2,384]{3,2,1,0:T(2,128)S(1)}, u32[]{:S(2)}, u32[]{:S(2)}) collective-permute-start(f32[3,24,2,384]{3,2,1,0:T(2,128)S(1)} %get-tuple-element.35), channel_id=1, source_target_pairs={{0,1},{1,0},{2,3},{3,2},{4,5},{5,4},{6,7},{7,6},{8,9},{9,8},{10,11... | collective-permute-start | bytes 663560 | tf_op jit(solution)/shard_map/ppermute | solution.py:682
  19.2 0.7 collective-permute-start.3
  19.9 24.5 %all_to_all.10 = s32[128,1,128]{2,1,0:T(1,128)S(1)} all-to-all(s32[128,1,128]{2,1,0:T(1,128)S(1)} %bitcast.17), channel_id=1, replica_groups=mesh['gx'=16,'gy'=8] {'gx','gy'}, dimensions={0} | all-to-all | bytes 131072 | tf_op jit(solution)/shard_map/all_to_all | solution.py:721
  44.4 0.5 prepare.1
  44.9 6.0 %first_main.1 = (f32[3,20,16,384]{3,2,1,0:T(8,128)S(1)}, f32[3,20,8,384]{3,2,1,0:T(8,128)S(1)}) custom-call(f32[3,16,16,384]{3,2,1,0:T(8,128)} %prev.4, f32[16,16,384]{2,1,0:T(8,128)} %buoy.5, f32[16,16,384]{2,1,0:T(8,128)} %mu.5, f32[16,16,384]{2,1,0:T(8,128)} %lam.5, f32[3,16,16,384]{3,2,1,0:T(8,128)S(1)} %copy-done, ...), custom_call_target="tpu_custom_call" | custom-call | tf_op jit(solution)/shard_map/first_main/pallas_call | solution.py:258
  51.0 2.6 %first_north.1 = (f32[3,20,16,384]{3,2,1,0:T(8,128)S(1)}, f32[3,20,2,384]{3,2,1,0:T(2,128)S(1)}, f32[3,20,2,384]{3,2,1,0:T(2,128)S(1)}, f32[8,256]{1,0:T(8,128)S(1)}) custom-call(f32[3,20,16,384]{3,2,1,0:T(8,128)S(1)} %get-tuple-element.42.main, f32[3,20,8,384]{3,2,1,0:T(8,128)S(1)} %get-tuple-element.43.pack, ...), custom_call_target="tpu_custom_call" | custom-call | tf_op jit(solution)/shard_map/first_north/pallas_call | solution.py:299
  53.6 1.2 %collective-permute-start.4 = (f32[3,20,2,384]{3,2,1,0:T(2,128)S(1)}, f32[3,20,2,384]{3,2,1,0:T(2,128)S(1)}, u32[]{:S(2)}, u32[]{:S(2)}) collective-permute-start(f32[3,20,2,384]{3,2,1,0:T(2,128)S(1)} %get-tuple-element.48), channel_id=1, source_target_pairs={{0,1},{1,0},{2,3},{3,2},{4,5},{5,4},{6,7},{7,6},{8,9},{9,8},{10,11... | collective-permute-start | bytes 552968 | tf_op jit(solution)/shard_map/ppermute | solution.py:682
  54.8 0.7 collective-permute-start.5
  55.5 4.9 %second_main.1 = (f32[3,16,16,384]{3,2,1,0:T(8,128)}, f32[3,16,16,384]{3,2,1,0:T(8,128)S(1)}, f32[3,16,8,384]{3,2,1,0:T(8,128)S(1)}) custom-call(f32[3,16,16,384]{3,2,1,0:T(8,128)} %prev.5, f32[16,16,384]{2,1,0:T(8,128)} %buoy.5, f32[16,16,384]{2,1,0:T(8,128)} %mu.5, f32[16,16,384]{2,1,0:T(8,128)} %lam.5, f32[3,20,16,384]{3,2,1,0:T(8,128)S(1)} %get-tuple-element.46.vp), custom_call_target="tpu_custom_call" | custom-call | tf_op jit(solution)/shard_map/second_main/pallas_call | solution.py:327
  60.4 0.9 %early_forces.1.early = f32[256,64]{1,0:T(8,128)S(1)} custom-call(f32[8,256]{1,0:T(8,128)S(1)} %get-tuple-element.52.top, f32[256,128]{1,0:T(8,128)S(1)} %get-tuple-element.53.chosen, f32[3,128,64]{2,1,0:T(8,128)S(1)} %get-tuple-element.54.weights), custom_call_target="tpu_custom_call" | custom-call | tf_op jit(solution)/shard_map/early_forces/pallas_call | solution.py:494
  61.4 0.0 copy-start.4
  61.4 3.6 %near_north.1 = (f32[3,16,16,128]{3,2,1,0:T(8,128)S(1)}, f32[256,128]{1,0:T(8,128)}) custom-call(f32[3,16,16,384]{3,2,1,0:T(8,128)S(1)} %get-tuple-element.55.main, f32[3,16,8,384]{3,2,1,0:T(8,128)S(1)} %get-tuple-element.56.pack, f32[3,20,2,384]{3,2,1,0:T(2,128)S(1)} %collective-permute-done.4.ya, f32[3,20,2,384]{3,2,1,0:T(2,128)S(1)} %collective-permute-done.5.yb, ...), custom_call_target="tpu_custom_call" | custom-call | tf_op jit(solution)/shard_map/near_north/pallas_call | solution.py:515
  65.0 0.7 copy-done.2
  65.8 9.4 %all-to-all-start.1 = ((f32[128,2,128]{2,1,0:T(2,128)}), f32[128,2,128]{2,1,0:T(2,128)S(1)}, u32[]{:S(2)}, u32[]{:S(2)}) async-start(f32[128,2,128]{2,1,0:T(2,128)} %bitcast.6), calls=%async_computation.1 | async-start | bytes 262144 | tf_op jit(solution)/shard_map/all_to_all | solution.py:721
  75.9 0.7 history.1.base
  76.6 2.3 %far_north.1 = f32[3,16,16,384]{3,2,1,0:T(8,128)} custom-call(f32[3,16,16,384]{3,2,1,0:T(8,128)S(1)} %get-tuple-element.55.main, f32[3,16,8,384]{3,2,1,0:T(8,128)S(1)} %get-tuple-element.56.pack, f32[3,16,16,128]{3,2,1,0:T(8,128)S(1)} %copy-done.3, f32[3,20,2,384]{3,2,1,0:T(2,128)S(1)} %collective-permute-done.4.ya, ...), custom_call_target="tpu_custom_call" | custom-call | tf_op jit(solution)/shard_map/far_north/pallas_call | solution.py:546
  78.9 6.1 %all-to-all-done.1 = f32[128,2,128]{2,1,0:T(2,128)S(1)} async-done(((f32[128,2,128]{2,1,0:T(2,128)}), f32[128,2,128]{2,1,0:T(2,128)S(1)}, u32[]{:S(2)}, u32[]{:S(2)}) %all-to-all-start.1) | async-done | bytes 131104 | tf_op jit(solution)/shard_map/all_to_all | solution.py:721
  85.0 1.1 %responses.1 = f32[2,64,128]{2,1,0:T(8,128)} custom-call(f32[256,128]{1,0:T(8,128)S(1)} %bitcast.12, s32[1,128]{1,0:T(1,128)S(1)} %get-tuple-element.62.pos, s32[1,1]{1,0:T(1,128)} %bitcast.11.count, f32[2,64,128]{2,1,0:T(8,128)S(1)} %history.1.base, f32[32,64]{1,0:T(8,128)S(1)} %bitcast.15), custom_call_target="tpu_custom_call" | custom-call | tf_op jit(solution)/shard_map/responses/pallas_call | solution.py:668
  (16 shorter events, 0.0 us)
Async XLA Ops:
  0.6 14.4 %copy-start = (f32[3,16,16,384]{3,2,1,0:T(8,128)S(1)}, f32[3,16,16,384]{3,2,1,0:T(8,128)}, u32[]{:S(2)}) copy-start(f32[3,16,16,384]{3,2,1,0:T(8,128)} %prev.5) | copy-start | bytes 3538948
  2.2 4.8 %collective-permute-start = (f32[24,16,384]{2,1,0:T(8,128)S(1)}, f32[24,16,384]{2,1,0:T(8,128)S(1)}, u32[]{:S(2)}, u32[]{:S(2)}) collective-permute-start(f32[24,16,384]{2,1,0:T(8,128)S(1)} %get-tuple-element.33), channel_id=1, source_target_pairs={{0,8},{8,0},{16,24},{24,16},{32,40},{40,32},{48,56},{56,48},{64,72... | collective-permute-start | bytes 1769480 | tf_op jit(solution)/shard_map/ppermute | solution.py:682
  3.7 40.7 %copy-start.5 = (f32[192,64]{0,1:T(8,128)S(1)}, f32[192,64]{0,1:T(8,128)}, u32[]{:S(2)}) copy-start(f32[192,64]{0,1:T(8,128)} %param.20) | copy-start | bytes 147460
  3.7 40.7 %copy-start.6 = (s32[128,2]{0,1:T(2,128)S(1)}, s32[128,2]{0,1:T(2,128)}, u32[]{:S(2)}) copy-start(s32[128,2]{0,1:T(2,128)} %param.16) | copy-start | bytes 3076
  3.7 11.3 %collective-permute-start.1 = (f32[24,16,384]{2,1,0:T(8,128)S(1)}, f32[24,16,384]{2,1,0:T(8,128)S(1)}, u32[]{:S(2)}, u32[]{:S(2)}) collective-permute-start(f32[24,16,384]{2,1,0:T(8,128)S(1)} %get-tuple-element.34), channel_id=1, source_target_pairs={{8,16},{16,8},{24,32},{32,24},{40,48},{48,40},{56,64},{64,56},{72,... | collective-permute-start | bytes 1769480 | tf_op jit(solution)/shard_map/ppermute | solution.py:682
  15.1 35.9 %collective-permute-start.2 = (f32[3,24,2,384]{3,2,1,0:T(2,128)S(1)}, f32[3,24,2,384]{3,2,1,0:T(2,128)S(1)}, u32[]{:S(2)}, u32[]{:S(2)}) collective-permute-start(f32[3,24,2,384]{3,2,1,0:T(2,128)S(1)} %get-tuple-element.35), channel_id=1, source_target_pairs={{0,1},{1,0},{2,3},{3,2},{4,5},{5,4},{6,7},{7,6},{8,9},{9,8},{10,11... | collective-permute-start | bytes 663560 | tf_op jit(solution)/shard_map/ppermute | solution.py:682
  19.2 31.8 %collective-permute-start.3 = (f32[3,24,2,384]{3,2,1,0:T(2,128)S(1)}, f32[3,24,2,384]{3,2,1,0:T(2,128)S(1)}, u32[]{:S(2)}, u32[]{:S(2)}) collective-permute-start(f32[3,24,2,384]{3,2,1,0:T(2,128)S(1)} %get-tuple-element.36), channel_id=1, source_target_pairs={{1,2},{2,1},{3,4},{4,3},{5,6},{6,5},{9,10},{10,9},{11,12},{12,11},... | collective-permute-start | bytes 663560 | tf_op jit(solution)/shard_map/ppermute | solution.py:682
  53.6 7.7 %collective-permute-start.4 = (f32[3,20,2,384]{3,2,1,0:T(2,128)S(1)}, f32[3,20,2,384]{3,2,1,0:T(2,128)S(1)}, u32[]{:S(2)}, u32[]{:S(2)}) collective-permute-start(f32[3,20,2,384]{3,2,1,0:T(2,128)S(1)} %get-tuple-element.48), channel_id=1, source_target_pairs={{0,1},{1,0},{2,3},{3,2},{4,5},{5,4},{6,7},{7,6},{8,9},{9,8},{10,11... | collective-permute-start | bytes 552968 | tf_op jit(solution)/shard_map/ppermute | solution.py:682
  54.8 6.5 %collective-permute-start.5 = (f32[3,20,2,384]{3,2,1,0:T(2,128)S(1)}, f32[3,20,2,384]{3,2,1,0:T(2,128)S(1)}, u32[]{:S(2)}, u32[]{:S(2)}) collective-permute-start(f32[3,20,2,384]{3,2,1,0:T(2,128)S(1)} %get-tuple-element.49), channel_id=1, source_target_pairs={{1,2},{2,1},{3,4},{4,3},{5,6},{6,5},{9,10},{10,9},{11,12},{12,11},... | collective-permute-start | bytes 552968 | tf_op jit(solution)/shard_map/ppermute | solution.py:682
  61.4 14.5 %copy-start.1 = (f32[31,64,128]{2,1,0:T(8,128)S(1)}, f32[31,64,128]{2,1,0:T(8,128)}, u32[]{:S(2)}) copy-start(f32[31,64,128]{2,1,0:T(8,128)} %hist.1) | copy-start | bytes 3047428
  61.4 14.5 %copy-start.4 = (f32[64,32]{0,1:T(8,128)S(1)}, f32[64,32]{0,1:T(8,128)}, u32[]{:S(2)}) copy-start(f32[64,32]{0,1:T(8,128)} %param.21) | copy-start | bytes 24580
  65.0 0.7 copy-start.2
  65.8 19.2 %all-to-all-start.1 = ((f32[128,2,128]{2,1,0:T(2,128)}), f32[128,2,128]{2,1,0:T(2,128)S(1)}, u32[]{:S(2)}, u32[]{:S(2)}) async-start(f32[128,2,128]{2,1,0:T(2,128)} %bitcast.6), calls=%async_computation.1 | async-start | bytes 262144 | tf_op jit(solution)/shard_map/all_to_all | solution.py:721
  75.2 1.4 %copy-start.3 = (f32[3,16,16,128]{3,2,1,0:T(8,128)S(1)}, f32[3,16,16,128]{3,2,1,0:T(8,128)}, u32[]{:S(2)}) copy-start(f32[3,16,16,128]{3,2,1,0:T(8,128)} %copy-done.2) | copy-start | bytes 1179652

commit v4 on v3

--- a/solution.py
+++ b/solution.py
@@ -194,7 +194,7 @@
         copy.wait()
 
 
-def east_pack_kernel(now, prev, buoy, mu, lam, source, pa, pb, req, pos, held, sems):
+def east_pack_kernel(now, prev, buoy, mu, lam, source, pa, pb, held, sems):
     rows = now.shape[1]
     odd = parity("gx")
     pairs = []
@@ -206,10 +206,7 @@
             pairs.append((prev.at[c, two], out.at[pl.ds(12 + 2 * c, 2)]))
         for n, field in enumerate((buoy, mu, lam)):
             pairs.append((field.at[two], out.at[pl.ds(18 + 2 * n, 2)]))
-    copies = started([(source, held)] + pairs, sems)
-    copies[0].wait()
-    build_requests(held, req, pos)
-    wait_all(copies[1:])
+    wait_all(started(pairs + [(source, held)], sems))
 
 
 def east_pack(now, prev, buoy, mu, lam, source):
@@ -220,12 +217,11 @@
         out_shape=(
             out,
             out,
-            jax.ShapeDtypeStruct((LANES, LANES), jnp.int32),
             pltpu.VMEM((1, LANES), jnp.int32),
         ),
         in_specs=[HBM_SPEC] * 6,
-        out_specs=(VMEM_SPEC,) * 4,
-        scratch_shapes=[pltpu.VMEM((1, LANES), jnp.int32), pltpu.SemaphoreType.DMA((19,))],
+        out_specs=(VMEM_SPEC,) * 3,
+        scratch_shapes=[pltpu.SemaphoreType.DMA((19,))],
         compiler_params=pltpu.CompilerParams(vmem_limit_bytes=VMEM_BYTES),
         name="east_pack",
     )(now, prev, buoy, mu, lam, source)
@@ -596,7 +592,7 @@
     )(now, xa, xb)
 
 
-def build_requests(source, req, pos):
+def request_kernel(source, req, pos):
     shape = (LANES, LANES)
     src = source[...]
     tile = src // LANES
@@ -611,6 +607,17 @@
     second = jnp.sum(jnp.where(rank == 1.0, wanted, 0.0), axis=1, keepdims=True)
     req[...] = jnp.where(lane == 0, first, jnp.where(lane == 1, second, 0.0)).astype(jnp.int32)
     pos[...] = tile * 2 + jnp.minimum(rank, 1.0).astype(jnp.int32)
+
+
+def make_requests(source):
+    return pl.pallas_call(
+        request_kernel,
+        out_shape=(pltpu.VMEM((LANES, LANES), jnp.int32), pltpu.VMEM((1, LANES), jnp.int32)),
+        in_specs=[VMEM_SPEC],
+        out_specs=(VMEM_SPEC,) * 2,
+        compiler_params=pltpu.CompilerParams(vmem_limit_bytes=VMEM_BYTES),
+        name="requests",
+    )(source)
 
 
 def columns_of(ker):
@@ -724,18 +731,19 @@
 
 def steps(prev, now, medium, offset, source, count, history, part, kernels):
     held = in_vmem(now)
-    pa, pb, req, pos = east_pack(
+    pa, pb, slots = east_pack(
         in_hbm(now), in_hbm(prev), *medium, in_hbm(source.reshape(1, LANES))
     )
     east = east_swaps(in_vmem(pa), in_vmem(pb))
+    req, pos = make_requests(in_vmem(slots))
     asked = exchange(req)
     north = north_edges(held, *east)
     north = north_swaps(*north)
-    prepared = prepare(in_vmem(asked), offset, part)
     main = first_main(held, *east, in_hbm(prev), *medium)
-    north, main, prepared = lax.optimization_barrier((north, main, prepared))
+    north, main = lax.optimization_barrier((north, main))
     mid, ya, yb, top = first_north(*main, *north)
     north = north_swaps(ya, yb)
+    prepared = prepare(in_vmem(asked), offset, part)
     early = early_forces(top, *prepared)
     disp_mid, main, pack = second_main(mid, in_hbm(now), *medium)
     north, main, pack, early = lax.optimization_barrier((north, main, pack, early))

time: 86.4 us -> 84 us (0.972)
  blocking collectives: 24.5 us -> 22.9 us
  starting transfers between devices: 20.8 us -> 19.7 us
    all_to_all x1, starting transfers between devices: 9.4 us -> 4.45 us  [exchange(): out = lax.all_to_all(rows, ('gx', 'gy'), split_axis=0, concat_axis=0)]
    ppermute x6, starting transfers between devices: 11.4 us -> 15.2 us  [swap(): return in_vmem(lax.ppermute(array, axis, pairs))]
    all_to_all x1, blocking collectives: 24.5 us -> 22.9 us  [exchange(): out = lax.all_to_all(rows, ('gx', 'gy'), split_axis=0, concat_axis=0)]
    pallas_call x1 -> x2, Pallas kernels: 1.54 us -> 1.8 us  [the longest x1 1.54 us: east_pack(): pl.pallas_call(east_pack_kernel, out_shape=(out, out, pltpu.VMEM((1, LANE...]
  transfers between devices with their start and end apart: 7 -> 7, of which waited for: 2 -> 2; matrix products, arithmetic and copies ran while one was open for 0% -> 0% of each run, Pallas kernels for 18% -> 19%
where the time goes in v4:
time: 84 us; the launch traced here: 83.8 us
  Pallas kernels  24.6 us (29%)
  blocking collectives  22.9 us (27%)
  starting transfers between devices  19.7 us (23%)
  waiting for transfers between devices  14.3 us (17%)
  between operations  1.54 us (2%)
    all_to_all x1, blocking collectives, exchange(): out = lax.all_to_all(rows, ('gx', 'gy'), split_axis=0, concat_axis=0)  22.9 us
    ppermute x6, starting transfers between devices, swap(): return in_vmem(lax.ppermute(array, axis, pairs))  15.2 us
    ppermute x6, waiting for transfers between devices, swap(): return in_vmem(lax.ppermute(array, axis, pairs))  8.06 us
    all_to_all x1, waiting for transfers between devices, exchange(): out = lax.all_to_all(rows, ('gx', 'gy'), split_axis=0, concat_axis=0)  6.2 us
    pallas_call x1, Pallas kernels, first_main(): pl.pallas_call(first_main_kernel, out_shape=(pltpu.VMEM((3, wide, cols, d...  6.04 us
    pallas_call x1, Pallas kernels, second_main(): pl.pallas_call(second_main_kernel, out_shape=(pltpu.HBM(prev.shape, F32),...  4.91 us
    all_to_all x1, starting transfers between devices, exchange(): out = lax.all_to_all(rows, ('gx', 'gy'), split_axis=0, concat_axis=0)  4.45 us
    pallas_call x1, Pallas kernels, near_north(): pl.pallas_call(near_north_kernel, out_shape=(pltpu.VMEM((3, rows, cols, L...  3.63 us
  transfers between devices with their start and end apart: 7, of which 2 were waited for; matrix products, arithmetic and copies ran while one was open for 0% of the time, Pallas kernels for 19%

profile of v4, /device:TPU:1, one launch (start us, length us, event | category | flops | bytes accessed | tf_op | source)
XLA Modules:
  0.0 83.8 jit_solution(8430875478368691569)
XLA Ops:
  0.6 0.0 copy-start
  0.6 1.5 %east_pack.1 = (f32[24,16,384]{2,1,0:T(8,128)S(1)}, f32[24,16,384]{2,1,0:T(8,128)S(1)}, s32[1,128]{1,0:T(1,128)S(1)}) custom-call(f32[3,16,16,384]{3,2,1,0:T(8,128)} %prev.5, f32[3,16,16,384]{3,2,1,0:T(8,128)} %prev.4, f32[16,16,384]{2,1,0:T(8,128)} %buoy.5, f32[16,16,384]{2,1,0:T(8,128)} %mu.5, f32[16,16,384]{2,1,0:T(8,128)} %lam.5, s32[1,128]{1,0:T(1,128)} %bitcast.19), custom_call_target="tpu_custom_call" | custom-call | tf_op jit(solution)/shard_map/east_pack/pallas_call | solution.py:215
  2.2 1.5 %collective-permute-start = (f32[24,16,384]{2,1,0:T(8,128)S(1)}, f32[24,16,384]{2,1,0:T(8,128)S(1)}, u32[]{:S(2)}, u32[]{:S(2)}) collective-permute-start(f32[24,16,384]{2,1,0:T(8,128)S(1)} %get-tuple-element.32), channel_id=1, source_target_pairs={{0,8},{8,0},{16,24},{24,16},{32,40},{40,32},{48,56},{56,48},{64,72... | collective-permute-start | bytes 1769480 | tf_op jit(solution)/shard_map/ppermute | solution.py:689
  3.7 3.1 %collective-permute-start.1 = (f32[24,16,384]{2,1,0:T(8,128)S(1)}, f32[24,16,384]{2,1,0:T(8,128)S(1)}, u32[]{:S(2)}, u32[]{:S(2)}) collective-permute-start(f32[24,16,384]{2,1,0:T(8,128)S(1)} %get-tuple-element.33), channel_id=1, source_target_pairs={{8,16},{16,8},{24,32},{32,24},{40,48},{48,40},{56,64},{64,56},{72,... | collective-permute-start | bytes 1769480 | tf_op jit(solution)/shard_map/ppermute | solution.py:689
  6.8 8.0 %collective-permute-done.1.xb = f32[24,16,384]{2,1,0:T(8,128)S(1)} collective-permute-done((f32[24,16,384]{2,1,0:T(8,128)S(1)}, f32[24,16,384]{2,1,0:T(8,128)S(1)}, u32[]{:S(2)}, u32[]{:S(2)}) %collective-permute-start.1) | collective-permute-done | bytes 589856 | tf_op jit(solution)/shard_map/ppermute | solution.py:689
  14.8 0.1 north_edges.1
  15.0 4.1 %collective-permute-start.2 = (f32[3,24,2,384]{3,2,1,0:T(2,128)S(1)}, f32[3,24,2,384]{3,2,1,0:T(2,128)S(1)}, u32[]{:S(2)}, u32[]{:S(2)}) collective-permute-start(f32[3,24,2,384]{3,2,1,0:T(2,128)S(1)} %get-tuple-element.34), channel_id=1, source_target_pairs={{0,1},{1,0},{2,3},{3,2},{4,5},{5,4},{6,7},{7,6},{8,9},{9,8},{10,11... | collective-permute-start | bytes 663560 | tf_op jit(solution)/shard_map/ppermute | solution.py:689
  19.1 0.7 collective-permute-start.3
  19.7 6.0 %first_main.1 = (f32[3,20,16,384]{3,2,1,0:T(8,128)S(1)}, f32[3,20,8,384]{3,2,1,0:T(8,128)S(1)}) custom-call(f32[3,16,16,384]{3,2,1,0:T(8,128)} %prev.4, f32[16,16,384]{2,1,0:T(8,128)} %buoy.5, f32[16,16,384]{2,1,0:T(8,128)} %mu.5, f32[16,16,384]{2,1,0:T(8,128)} %lam.5, f32[3,16,16,384]{3,2,1,0:T(8,128)S(1)} %copy-done, ...), custom_call_target="tpu_custom_call" | custom-call | tf_op jit(solution)/shard_map/first_main/pallas_call | solution.py:254
  25.8 2.6 %first_north.1 = (f32[3,20,16,384]{3,2,1,0:T(8,128)S(1)}, f32[3,20,2,384]{3,2,1,0:T(2,128)S(1)}, f32[3,20,2,384]{3,2,1,0:T(2,128)S(1)}, f32[8,256]{1,0:T(8,128)S(1)}) custom-call(f32[3,20,16,384]{3,2,1,0:T(8,128)S(1)} %get-tuple-element.38.main, f32[3,20,8,384]{3,2,1,0:T(8,128)S(1)} %get-tuple-element.39.pack, ...), custom_call_target="tpu_custom_call" | custom-call | tf_op jit(solution)/shard_map/first_north/pallas_call | solution.py:295
  28.4 5.2 %collective-permute-start.4 = (f32[3,20,2,384]{3,2,1,0:T(2,128)S(1)}, f32[3,20,2,384]{3,2,1,0:T(2,128)S(1)}, u32[]{:S(2)}, u32[]{:S(2)}) collective-permute-start(f32[3,20,2,384]{3,2,1,0:T(2,128)S(1)} %get-tuple-element.44), channel_id=1, source_target_pairs={{0,1},{1,0},{2,3},{3,2},{4,5},{5,4},{6,7},{7,6},{8,9},{9,8},{10,11... | collective-permute-start | bytes 552968 | tf_op jit(solution)/shard_map/ppermute | solution.py:689
  33.7 0.7 collective-permute-start.5
  34.3 0.3 requests.1
  34.6 22.9 %all_to_all.10 = s32[128,1,128]{2,1,0:T(1,128)S(1)} all-to-all(s32[128,1,128]{2,1,0:T(1,128)S(1)} %bitcast.17), channel_id=1, replica_groups=mesh['gx'=16,'gy'=8] {'gx','gy'}, dimensions={0} | all-to-all | bytes 131072 | tf_op jit(solution)/shard_map/all_to_all | solution.py:728
  57.5 0.5 prepare.1
  58.0 4.9 %second_main.1 = (f32[3,16,16,384]{3,2,1,0:T(8,128)}, f32[3,16,16,384]{3,2,1,0:T(8,128)S(1)}, f32[3,16,8,384]{3,2,1,0:T(8,128)S(1)}) custom-call(f32[3,16,16,384]{3,2,1,0:T(8,128)} %prev.5, f32[16,16,384]{2,1,0:T(8,128)} %buoy.5, f32[16,16,384]{2,1,0:T(8,128)} %mu.5, f32[16,16,384]{2,1,0:T(8,128)} %lam.5, f32[3,20,16,384]{3,2,1,0:T(8,128)S(1)} %get-tuple-element.42.vp), custom_call_target="tpu_custom_call" | custom-call | tf_op jit(solution)/shard_map/second_main/pallas_call | solution.py:323
  62.9 0.9 %early_forces.1.early = f32[256,64]{1,0:T(8,128)S(1)} custom-call(f32[8,256]{1,0:T(8,128)S(1)} %get-tuple-element.48.top, f32[256,128]{1,0:T(8,128)S(1)} %get-tuple-element.51.chosen, f32[3,128,64]{2,1,0:T(8,128)S(1)} %get-tuple-element.52.weights), custom_call_target="tpu_custom_call" | custom-call | tf_op jit(solution)/shard_map/early_forces/pallas_call | solution.py:490
  63.9 3.6 %near_north.1 = (f32[3,16,16,128]{3,2,1,0:T(8,128)S(1)}, f32[256,128]{1,0:T(8,128)}) custom-call(f32[3,16,16,384]{3,2,1,0:T(8,128)S(1)} %get-tuple-element.53.main, f32[3,16,8,384]{3,2,1,0:T(8,128)S(1)} %get-tuple-element.54.pack, f32[3,20,2,384]{3,2,1,0:T(2,128)S(1)} %collective-permute-done.4.ya, f32[3,20,2,384]{3,2,1,0:T(2,128)S(1)} %collective-permute-done.5.yb, ...), custom_call_target="tpu_custom_call" | custom-call | tf_op jit(solution)/shard_map/near_north/pallas_call | solution.py:511
  67.6 0.7 copy-done.2
  68.3 4.5 %all-to-all-start.1 = ((f32[128,2,128]{2,1,0:T(2,128)}), f32[128,2,128]{2,1,0:T(2,128)S(1)}, u32[]{:S(2)}, u32[]{:S(2)}) async-start(f32[128,2,128]{2,1,0:T(2,128)} %bitcast.6), calls=%async_computation.1 | async-start | bytes 262144 | tf_op jit(solution)/shard_map/all_to_all | solution.py:728
  73.5 0.7 history.1.base
  74.2 2.3 %far_north.1 = f32[3,16,16,384]{3,2,1,0:T(8,128)} custom-call(f32[3,16,16,384]{3,2,1,0:T(8,128)S(1)} %get-tuple-element.53.main, f32[3,16,8,384]{3,2,1,0:T(8,128)S(1)} %get-tuple-element.54.pack, f32[3,16,16,128]{3,2,1,0:T(8,128)S(1)} %copy-done.3, f32[3,20,2,384]{3,2,1,0:T(2,128)S(1)} %collective-permute-done.4.ya, ...), custom_call_target="tpu_custom_call" | custom-call | tf_op jit(solution)/shard_map/far_north/pallas_call | solution.py:542
  76.5 6.2 %all-to-all-done.1 = f32[128,2,128]{2,1,0:T(2,128)S(1)} async-done(((f32[128,2,128]{2,1,0:T(2,128)}), f32[128,2,128]{2,1,0:T(2,128)S(1)}, u32[]{:S(2)}, u32[]{:S(2)}) %all-to-all-start.1) | async-done | bytes 131104 | tf_op jit(solution)/shard_map/all_to_all | solution.py:728
  82.7 1.1 %responses.1 = f32[2,64,128]{2,1,0:T(8,128)} custom-call(f32[256,128]{1,0:T(8,128)S(1)} %bitcast.12, s32[1,128]{1,0:T(1,128)S(1)} %get-tuple-element.60.pos, s32[1,1]{1,0:T(1,128)} %bitcast.11.count, f32[2,64,128]{2,1,0:T(8,128)S(1)} %history.1.base, f32[32,64]{1,0:T(8,128)S(1)} %bitcast.15), custom_call_target="tpu_custom_call" | custom-call | tf_op jit(solution)/shard_map/responses/pallas_call | solution.py:675
  (17 shorter events, 0.0 us)
Async XLA Ops:
  0.6 14.2 %copy-start = (f32[3,16,16,384]{3,2,1,0:T(8,128)S(1)}, f32[3,16,16,384]{3,2,1,0:T(8,128)}, u32[]{:S(2)}) copy-start(f32[3,16,16,384]{3,2,1,0:T(8,128)} %prev.5) | copy-start | bytes 3538948
  2.2 4.6 %collective-permute-start = (f32[24,16,384]{2,1,0:T(8,128)S(1)}, f32[24,16,384]{2,1,0:T(8,128)S(1)}, u32[]{:S(2)}, u32[]{:S(2)}) collective-permute-start(f32[24,16,384]{2,1,0:T(8,128)S(1)} %get-tuple-element.32), channel_id=1, source_target_pairs={{0,8},{8,0},{16,24},{24,16},{32,40},{40,32},{48,56},{56,48},{64,72... | collective-permute-start | bytes 1769480 | tf_op jit(solution)/shard_map/ppermute | solution.py:689
  3.7 11.2 %collective-permute-start.1 = (f32[24,16,384]{2,1,0:T(8,128)S(1)}, f32[24,16,384]{2,1,0:T(8,128)S(1)}, u32[]{:S(2)}, u32[]{:S(2)}) collective-permute-start(f32[24,16,384]{2,1,0:T(8,128)S(1)} %get-tuple-element.33), channel_id=1, source_target_pairs={{8,16},{16,8},{24,32},{32,24},{40,48},{48,40},{56,64},{64,56},{72,... | collective-permute-start | bytes 1769480 | tf_op jit(solution)/shard_map/ppermute | solution.py:689
  15.0 10.8 %collective-permute-start.2 = (f32[3,24,2,384]{3,2,1,0:T(2,128)S(1)}, f32[3,24,2,384]{3,2,1,0:T(2,128)S(1)}, u32[]{:S(2)}, u32[]{:S(2)}) collective-permute-start(f32[3,24,2,384]{3,2,1,0:T(2,128)S(1)} %get-tuple-element.34), channel_id=1, source_target_pairs={{0,1},{1,0},{2,3},{3,2},{4,5},{5,4},{6,7},{7,6},{8,9},{9,8},{10,11... | collective-permute-start | bytes 663560 | tf_op jit(solution)/shard_map/ppermute | solution.py:689
  19.1 6.7 %collective-permute-start.3 = (f32[3,24,2,384]{3,2,1,0:T(2,128)S(1)}, f32[3,24,2,384]{3,2,1,0:T(2,128)S(1)}, u32[]{:S(2)}, u32[]{:S(2)}) collective-permute-start(f32[3,24,2,384]{3,2,1,0:T(2,128)S(1)} %get-tuple-element.35), channel_id=1, source_target_pairs={{1,2},{2,1},{3,4},{4,3},{5,6},{6,5},{9,10},{10,9},{11,12},{12,11},... | collective-permute-start | bytes 663560 | tf_op jit(solution)/shard_map/ppermute | solution.py:689
  25.8 31.7 %copy-start.5 = (f32[192,64]{0,1:T(8,128)S(1)}, f32[192,64]{0,1:T(8,128)}, u32[]{:S(2)}) copy-start(f32[192,64]{0,1:T(8,128)} %param.20) | copy-start | bytes 147460
  25.8 31.7 %copy-start.6 = (s32[128,2]{0,1:T(2,128)S(1)}, s32[128,2]{0,1:T(2,128)}, u32[]{:S(2)}) copy-start(s32[128,2]{0,1:T(2,128)} %param.16) | copy-start | bytes 3076
  28.4 35.5 %collective-permute-start.4 = (f32[3,20,2,384]{3,2,1,0:T(2,128)S(1)}, f32[3,20,2,384]{3,2,1,0:T(2,128)S(1)}, u32[]{:S(2)}, u32[]{:S(2)}) collective-permute-start(f32[3,20,2,384]{3,2,1,0:T(2,128)S(1)} %get-tuple-element.44), channel_id=1, source_target_pairs={{0,1},{1,0},{2,3},{3,2},{4,5},{5,4},{6,7},{7,6},{8,9},{9,8},{10,11... | collective-permute-start | bytes 552968 | tf_op jit(solution)/shard_map/ppermute | solution.py:689
  33.7 30.2 %collective-permute-start.5 = (f32[3,20,2,384]{3,2,1,0:T(2,128)S(1)}, f32[3,20,2,384]{3,2,1,0:T(2,128)S(1)}, u32[]{:S(2)}, u32[]{:S(2)}) collective-permute-start(f32[3,20,2,384]{3,2,1,0:T(2,128)S(1)} %get-tuple-element.45), channel_id=1, source_target_pairs={{1,2},{2,1},{3,4},{4,3},{5,6},{6,5},{9,10},{10,9},{11,12},{12,11},... | collective-permute-start | bytes 552968 | tf_op jit(solution)/shard_map/ppermute | solution.py:689
  63.9 9.6 %copy-start.1 = (f32[31,64,128]{2,1,0:T(8,128)S(1)}, f32[31,64,128]{2,1,0:T(8,128)}, u32[]{:S(2)}) copy-start(f32[31,64,128]{2,1,0:T(8,128)} %hist.1) | copy-start | bytes 3047428
  63.9 9.6 %copy-start.4 = (f32[64,32]{0,1:T(8,128)S(1)}, f32[64,32]{0,1:T(8,128)}, u32[]{:S(2)}) copy-start(f32[64,32]{0,1:T(8,128)} %param.21) | copy-start | bytes 24580
  67.6 0.7 copy-start.2
  68.3 14.4 %all-to-all-start.1 = ((f32[128,2,128]{2,1,0:T(2,128)}), f32[128,2,128]{2,1,0:T(2,128)S(1)}, u32[]{:S(2)}, u32[]{:S(2)}) async-start(f32[128,2,128]{2,1,0:T(2,128)} %bitcast.6), calls=%async_computation.1 | async-start | bytes 262144 | tf_op jit(solution)/shard_map/all_to_all | solution.py:728
  72.8 1.4 %copy-start.3 = (f32[3,16,16,128]{3,2,1,0:T(8,128)S(1)}, f32[3,16,16,128]{3,2,1,0:T(8,128)}, u32[]{:S(2)}) copy-start(f32[3,16,16,128]{3,2,1,0:T(8,128)} %copy-done.2) | copy-start | bytes 1179652

commit v5 on v3

--- a/solution.py
+++ b/solution.py
@@ -194,7 +194,7 @@
         copy.wait()
 
 
-def east_pack_kernel(now, prev, buoy, mu, lam, source, pa, pb, req, pos, held, sems):
+def east_pack_kernel(now, prev, buoy, mu, lam, source, pa, pb, low, high, req, pos, held, sems):
     rows = now.shape[1]
     odd = parity("gx")
     pairs = []
@@ -206,6 +206,9 @@
             pairs.append((prev.at[c, two], out.at[pl.ds(12 + 2 * c, 2)]))
         for n, field in enumerate((buoy, mu, lam)):
             pairs.append((field.at[two], out.at[pl.ds(18 + 2 * n, 2)]))
+    cols = now.shape[2]
+    pairs.append((now.at[:, :, pl.ds(0, 2)], low))
+    pairs.append((now.at[:, :, pl.ds(cols - 2, 2)], high))
     copies = started([(source, held)] + pairs, sems)
     copies[0].wait()
     build_requests(held, req, pos)
@@ -213,19 +216,22 @@
 
 
 def east_pack(now, prev, buoy, mu, lam, source):
-    _, _, cols, depth = now.shape
+    _, rows, cols, depth = now.shape
     out = pltpu.VMEM((24, cols, depth), F32)
+    side = pltpu.VMEM((3, rows, 2, depth), F32)
     return pl.pallas_call(
         east_pack_kernel,
         out_shape=(
             out,
             out,
+            side,
+            side,
             jax.ShapeDtypeStruct((LANES, LANES), jnp.int32),
             pltpu.VMEM((1, LANES), jnp.int32),
         ),
         in_specs=[HBM_SPEC] * 6,
-        out_specs=(VMEM_SPEC,) * 4,
-        scratch_shapes=[pltpu.VMEM((1, LANES), jnp.int32), pltpu.SemaphoreType.DMA((19,))],
+        out_specs=(VMEM_SPEC,) * 6,
+        scratch_shapes=[pltpu.VMEM((1, LANES), jnp.int32), pltpu.SemaphoreType.DMA((21,))],
         compiler_params=pltpu.CompilerParams(vmem_limit_bytes=VMEM_BYTES),
         name="east_pack",
     )(now, prev, buoy, mu, lam, source)
@@ -235,11 +241,10 @@
     rows = now.shape[1]
     own = pl.ds(2, rows)
     copies = started(
-        [(prev, pv.at[:, own])] + [(src, dst.at[own]) for src, dst in ((buoy, bv), (mu, mv), (lam, lv))],
+        [(now, vp.at[:, pl.ds(4, rows)]), (prev, pv.at[:, own])] + [(src, dst.at[own]) for src, dst in ((buoy, bv), (mu, mv), (lam, lv))],
         work[-1],
     )
     odd = parity("gx")
-    vp[:, 4 : rows + 4] = now[...]
     for edge, side in ((xa, 1 - odd), (xb, odd)):
         four = pl.ds((rows + 4) * side, 4)
         two = pl.ds((rows + 2) * side, 2)
@@ -248,7 +253,8 @@
             pv[c, two] = edge[12 + 2 * c : 14 + 2 * c]
         for n, field in enumerate((bv, mv, lv)):
             field[two] = edge[18 + 2 * n : 20 + 2 * n]
-    run_step(vp, pv, bv, mv, lv, out, pack, work[:-1], lambda: wait_all(copies))
+    copies[0].wait()
+    run_step(vp, pv, bv, mv, lv, out, pack, work[:-1], lambda: wait_all(copies[1:]))
 
 
 def first_main(now, xa, xb, prev, buoy, mu, lam):
@@ -258,7 +264,7 @@
     return pl.pallas_call(
         first_main_kernel,
         out_shape=(pltpu.VMEM((3, wide, cols, depth), F32), pltpu.VMEM((3, wide, 8, depth), F32)),
-        in_specs=[HBM_SPEC] * 4 + [VMEM_SPEC] * 3,
+        in_specs=[HBM_SPEC] * 5 + [VMEM_SPEC] * 2,
         out_specs=(VMEM_SPEC,) * 2,
         scratch_shapes=[
             pltpu.VMEM((3, wide + 4, cols, depth), F32),
@@ -267,7 +273,7 @@
             one,
             one,
             *step_work(wide, cols, depth),
-            pltpu.SemaphoreType.DMA((4,)),
+            pltpu.SemaphoreType.DMA((5,)),
         ],
         compiler_params=pltpu.CompilerParams(vmem_limit_bytes=VMEM_BYTES),
         name="first_main",
@@ -560,40 +566,40 @@
     )(main, pack, near, ya, yb)
 
 
-def north_kernel(now, xa, xb, ya, yb):
-    rows = now.shape[1]
+def north_kernel(low, high, xa, xb, ya, yb):
+    rows = low.shape[1]
     odd_x, odd_y = parity("gx"), parity("gy")
 
-    def gather(out, edge):
-        out[:, 4 : rows + 4] = now[:, :, edge : edge + 2, :]
+    def gather(out, own, edge):
+        out[:, 4 : rows + 4] = own[...]
         for rim, side in ((xa, 1 - odd_x), (xb, odd_x)):
             for c in range(3):
                 out[c, pl.ds((rows + 4) * side, 4)] = rim[4 * c : 4 * c + 4, edge : edge + 2, :]
 
-    high = SIDE - 2
+    last = SIDE - 2
 
     @pl.when(odd_y == 0)
     def _():
-        gather(ya, high)
-        gather(yb, 0)
+        gather(ya, high, last)
+        gather(yb, low, 0)
 
     @pl.when(odd_y == 1)
     def _():
-        gather(ya, 0)
-        gather(yb, high)
-
-
-def north_edges(now, xa, xb):
-    _, rows, _, depth = now.shape
-    out = pltpu.VMEM((3, rows + 8, 2, depth), F32)
+        gather(ya, low, 0)
+        gather(yb, high, last)
+
+
+def north_edges(low, high, xa, xb):
+    _, rows, two, depth = low.shape
+    out = pltpu.VMEM((3, rows + 8, two, depth), F32)
     return pl.pallas_call(
         north_kernel,
         out_shape=(out, out),
-        in_specs=[VMEM_SPEC] * 3,
+        in_specs=[VMEM_SPEC] * 4,
         out_specs=(VMEM_SPEC, VMEM_SPEC),
         compiler_params=pltpu.CompilerParams(vmem_limit_bytes=VMEM_BYTES),
         name="north_edges",
-    )(now, xa, xb)
+    )(low, high, xa, xb)
 
 
 def build_requests(source, req, pos):
@@ -723,19 +729,18 @@
 
 
 def steps(prev, now, medium, offset, source, count, history, part, kernels):
-    held = in_vmem(now)
-    pa, pb, req, pos = east_pack(
+    pa, pb, low, high, req, pos = east_pack(
         in_hbm(now), in_hbm(prev), *medium, in_hbm(source.reshape(1, LANES))
     )
     east = east_swaps(in_vmem(pa), in_vmem(pb))
     asked = exchange(req)
-    north = north_edges(held, *east)
+    north = north_edges(in_vmem(low), in_vmem(high), *east)
     north = north_swaps(*north)
-    prepared = prepare(in_vmem(asked), offset, part)
-    main = first_main(held, *east, in_hbm(prev), *medium)
-    north, main, prepared = lax.optimization_barrier((north, main, prepared))
+    main = first_main(in_hbm(now), *east, in_hbm(prev), *medium)
+    north, main = lax.optimization_barrier((north, main))
     mid, ya, yb, top = first_north(*main, *north)
     north = north_swaps(ya, yb)
+    prepared = prepare(in_vmem(asked), offset, part)
     early = early_forces(top, *prepared)
     disp_mid, main, pack = second_main(mid, in_hbm(now), *medium)
     north, main, pack, early = lax.optimization_barrier((north, main, pack, early))

time: 86.4 us -> 85 us (0.984)
  blocking collectives: 24.5 us -> 22.9 us
  Pallas kernels: 24.3 us -> 25.5 us
  starting transfers between devices: 20.8 us -> 19.7 us
    all_to_all x1, starting transfers between devices: 9.4 us -> 4.46 us  [exchange(): out = lax.all_to_all(rows, ('gx', 'gy'), split_axis=0, concat_axis=0)]
    ppermute x6, starting transfers between devices: 11.4 us -> 15.2 us  [swap(): return in_vmem(lax.ppermute(array, axis, pairs))]
    all_to_all x1, blocking collectives: 24.5 us -> 22.9 us  [exchange(): out = lax.all_to_all(rows, ('gx', 'gy'), split_axis=0, concat_axis=0)]
    pallas_call x1, Pallas kernels: 6.05 us -> 7.17 us  [first_main(): pl.pallas_call(first_main_kernel, out_shape=(pltpu.VMEM((3, wide, cols, d...]
  transfers between devices with their start and end apart: 7 -> 7, of which waited for: 2 -> 2; matrix products, arithmetic and copies ran while one was open for 0% -> 0% of each run, Pallas kernels for 18% -> 19%
where the time goes in v5:
time: 85 us; the launch traced here: 84.7 us
  Pallas kernels  25.5 us (30%)
  blocking collectives  22.9 us (27%)
  starting transfers between devices  19.7 us (23%)
  waiting for transfers between devices  14.3 us (17%)
  between operations  1.53 us (2%)
    all_to_all x1, blocking collectives, exchange(): out = lax.all_to_all(rows, ('gx', 'gy'), split_axis=0, concat_axis=0)  22.9 us
    ppermute x6, starting transfers between devices, swap(): return in_vmem(lax.ppermute(array, axis, pairs))  15.2 us
    ppermute x6, waiting for transfers between devices, swap(): return in_vmem(lax.ppermute(array, axis, pairs))  8.06 us
    pallas_call x1, Pallas kernels, first_main(): pl.pallas_call(first_main_kernel, out_shape=(pltpu.VMEM((3, wide, cols, d...  7.17 us
    all_to_all x1, waiting for transfers between devices, exchange(): out = lax.all_to_all(rows, ('gx', 'gy'), split_axis=0, concat_axis=0)  6.23 us
    pallas_call x1, Pallas kernels, second_main(): pl.pallas_call(second_main_kernel, out_shape=(pltpu.HBM(prev.shape, F32),...  4.91 us
    all_to_all x1, starting transfers between devices, exchange(): out = lax.all_to_all(rows, ('gx', 'gy'), split_axis=0, concat_axis=0)  4.46 us
    pallas_call x1, Pallas kernels, near_north(): pl.pallas_call(near_north_kernel, out_shape=(pltpu.VMEM((3, rows, cols, L...  3.63 us
  transfers between devices with their start and end apart: 7, of which 2 were waited for; matrix products, arithmetic and copies ran while one was open for 0% of the time, Pallas kernels for 19%

profile of v5, /device:TPU:1, one launch (start us, length us, event | category | flops | bytes accessed | tf_op | source)
XLA Modules:
  0.0 84.7 jit_solution(15120254120909513450)
XLA Ops:
  0.6 1.6 %east_pack.1 = (f32[24,16,384]{2,1,0:T(8,128)S(1)}, f32[24,16,384]{2,1,0:T(8,128)S(1)}, f32[3,16,2,384]{3,2,1,0:T(2,128)S(1)}, f32[3,16,2,384]{3,2,1,0:T(2,128)S...) custom-call(f32[3,16,16,384]{3,2,1,0:T(8,128)} %prev.5, f32[3,16,16,384]{3,2,1,0:T(8,128)} %prev.4, ...), custom_call_target="tpu_custom_call" | custom-call | tf_op jit(solution)/shard_map/east_pack/pallas_call | solution.py:222
  2.3 1.5 %collective-permute-start = (f32[24,16,384]{2,1,0:T(8,128)S(1)}, f32[24,16,384]{2,1,0:T(8,128)S(1)}, u32[]{:S(2)}, u32[]{:S(2)}) collective-permute-start(f32[24,16,384]{2,1,0:T(8,128)S(1)} %get-tuple-element.35), channel_id=1, source_target_pairs={{0,8},{8,0},{16,24},{24,16},{32,40},{40,32},{48,56},{56,48},{64,72... | collective-permute-start | bytes 1769480 | tf_op jit(solution)/shard_map/ppermute | solution.py:688
  3.7 3.1 %collective-permute-start.1 = (f32[24,16,384]{2,1,0:T(8,128)S(1)}, f32[24,16,384]{2,1,0:T(8,128)S(1)}, u32[]{:S(2)}, u32[]{:S(2)}) collective-permute-start(f32[24,16,384]{2,1,0:T(8,128)S(1)} %get-tuple-element.36), channel_id=1, source_target_pairs={{8,16},{16,8},{24,32},{32,24},{40,48},{48,40},{56,64},{64,56},{72,... | collective-permute-start | bytes 1769480 | tf_op jit(solution)/shard_map/ppermute | solution.py:688
  6.9 8.0 %collective-permute-done.1.xb = f32[24,16,384]{2,1,0:T(8,128)S(1)} collective-permute-done((f32[24,16,384]{2,1,0:T(8,128)S(1)}, f32[24,16,384]{2,1,0:T(8,128)S(1)}, u32[]{:S(2)}, u32[]{:S(2)}) %collective-permute-start.1) | collective-permute-done | bytes 589856 | tf_op jit(solution)/shard_map/ppermute | solution.py:688
  14.9 0.1 north_edges.1
  15.0 4.1 %collective-permute-start.2 = (f32[3,24,2,384]{3,2,1,0:T(2,128)S(1)}, f32[3,24,2,384]{3,2,1,0:T(2,128)S(1)}, u32[]{:S(2)}, u32[]{:S(2)}) collective-permute-start(f32[3,24,2,384]{3,2,1,0:T(2,128)S(1)} %get-tuple-element.37), channel_id=1, source_target_pairs={{0,1},{1,0},{2,3},{3,2},{4,5},{5,4},{6,7},{7,6},{8,9},{9,8},{10,11... | collective-permute-start | bytes 663560 | tf_op jit(solution)/shard_map/ppermute | solution.py:688
  19.1 0.7 collective-permute-start.3
  19.8 7.2 %first_main.1 = (f32[3,20,16,384]{3,2,1,0:T(8,128)S(1)}, f32[3,20,8,384]{3,2,1,0:T(8,128)S(1)}) custom-call(f32[3,16,16,384]{3,2,1,0:T(8,128)} %prev.4, f32[16,16,384]{2,1,0:T(8,128)} %buoy.5, f32[16,16,384]{2,1,0:T(8,128)} %mu.5, f32[16,16,384]{2,1,0:T(8,128)} %lam.5, f32[3,16,16,384]{3,2,1,0:T(8,128)} %prev.5, f32[24,16,384]{2,1,0:T(8,128)S(1)} %collective-permute-done.xa, ...), custom_call_target="tpu_custom_call" | custom-call | tf_op jit(solution)/shard_map/first_main/pallas_call | solution.py:264
  27.0 0.0 copy-start.4
  27.0 2.6 %first_north.1 = (f32[3,20,16,384]{3,2,1,0:T(8,128)S(1)}, f32[3,20,2,384]{3,2,1,0:T(2,128)S(1)}, f32[3,20,2,384]{3,2,1,0:T(2,128)S(1)}, f32[8,256]{1,0:T(8,128)S(1)}) custom-call(f32[3,20,16,384]{3,2,1,0:T(8,128)S(1)} %get-tuple-element.41.main, f32[3,20,8,384]{3,2,1,0:T(8,128)S(1)} %get-tuple-element.42.pack, ...), custom_call_target="tpu_custom_call" | custom-call | tf_op jit(solution)/shard_map/first_north/pallas_call | solution.py:305
  29.6 5.2 %collective-permute-start.4 = (f32[3,20,2,384]{3,2,1,0:T(2,128)S(1)}, f32[3,20,2,384]{3,2,1,0:T(2,128)S(1)}, u32[]{:S(2)}, u32[]{:S(2)}) collective-permute-start(f32[3,20,2,384]{3,2,1,0:T(2,128)S(1)} %get-tuple-element.47), channel_id=1, source_target_pairs={{0,1},{1,0},{2,3},{3,2},{4,5},{5,4},{6,7},{7,6},{8,9},{9,8},{10,11... | collective-permute-start | bytes 552968 | tf_op jit(solution)/shard_map/ppermute | solution.py:688
  34.8 0.7 collective-permute-start.5
  35.5 22.9 %all_to_all.10 = s32[128,1,128]{2,1,0:T(1,128)S(1)} all-to-all(s32[128,1,128]{2,1,0:T(1,128)S(1)} %bitcast.17), channel_id=1, replica_groups=mesh['gx'=16,'gy'=8] {'gx','gy'}, dimensions={0} | all-to-all | bytes 131072 | tf_op jit(solution)/shard_map/all_to_all | solution.py:727
  58.4 0.5 prepare.1
  58.9 4.9 %second_main.1 = (f32[3,16,16,384]{3,2,1,0:T(8,128)}, f32[3,16,16,384]{3,2,1,0:T(8,128)S(1)}, f32[3,16,8,384]{3,2,1,0:T(8,128)S(1)}) custom-call(f32[3,16,16,384]{3,2,1,0:T(8,128)} %prev.5, f32[16,16,384]{2,1,0:T(8,128)} %buoy.5, f32[16,16,384]{2,1,0:T(8,128)} %mu.5, f32[16,16,384]{2,1,0:T(8,128)} %lam.5, f32[3,20,16,384]{3,2,1,0:T(8,128)S(1)} %get-tuple-element.45.vp), custom_call_target="tpu_custom_call" | custom-call | tf_op jit(solution)/shard_map/second_main/pallas_call | solution.py:333
  63.8 0.9 %early_forces.1.early = f32[256,64]{1,0:T(8,128)S(1)} custom-call(f32[8,256]{1,0:T(8,128)S(1)} %get-tuple-element.51.top, f32[256,128]{1,0:T(8,128)S(1)} %get-tuple-element.53.chosen, f32[3,128,64]{2,1,0:T(8,128)S(1)} %get-tuple-element.54.weights), custom_call_target="tpu_custom_call" | custom-call | tf_op jit(solution)/shard_map/early_forces/pallas_call | solution.py:500
  64.8 0.0 copy-start
  64.8 3.6 %near_north.1 = (f32[3,16,16,128]{3,2,1,0:T(8,128)S(1)}, f32[256,128]{1,0:T(8,128)}) custom-call(f32[3,16,16,384]{3,2,1,0:T(8,128)S(1)} %get-tuple-element.55.main, f32[3,16,8,384]{3,2,1,0:T(8,128)S(1)} %get-tuple-element.56.pack, f32[3,20,2,384]{3,2,1,0:T(2,128)S(1)} %collective-permute-done.4.ya, f32[3,20,2,384]{3,2,1,0:T(2,128)S(1)} %collective-permute-done.5.yb, ...), custom_call_target="tpu_custom_call" | custom-call | tf_op jit(solution)/shard_map/near_north/pallas_call | solution.py:521
  68.5 0.7 copy-done.1
  69.2 4.5 %all-to-all-start.1 = ((f32[128,2,128]{2,1,0:T(2,128)}), f32[128,2,128]{2,1,0:T(2,128)S(1)}, u32[]{:S(2)}, u32[]{:S(2)}) async-start(f32[128,2,128]{2,1,0:T(2,128)} %bitcast.6), calls=%async_computation.1 | async-start | bytes 262144 | tf_op jit(solution)/shard_map/all_to_all | solution.py:727
  74.4 0.7 history.1.base
  75.1 2.3 %far_north.1 = f32[3,16,16,384]{3,2,1,0:T(8,128)} custom-call(f32[3,16,16,384]{3,2,1,0:T(8,128)S(1)} %get-tuple-element.55.main, f32[3,16,8,384]{3,2,1,0:T(8,128)S(1)} %get-tuple-element.56.pack, f32[3,16,16,128]{3,2,1,0:T(8,128)S(1)} %copy-done.2, f32[3,20,2,384]{3,2,1,0:T(2,128)S(1)} %collective-permute-done.4.ya, ...), custom_call_target="tpu_custom_call" | custom-call | tf_op jit(solution)/shard_map/far_north/pallas_call | solution.py:552
  77.4 6.2 %all-to-all-done.1 = f32[128,2,128]{2,1,0:T(2,128)S(1)} async-done(((f32[128,2,128]{2,1,0:T(2,128)}), f32[128,2,128]{2,1,0:T(2,128)S(1)}, u32[]{:S(2)}, u32[]{:S(2)}) %all-to-all-start.1) | async-done | bytes 131104 | tf_op jit(solution)/shard_map/all_to_all | solution.py:727
  83.6 1.1 %responses.1 = f32[2,64,128]{2,1,0:T(8,128)} custom-call(f32[256,128]{1,0:T(8,128)S(1)} %bitcast.12, s32[1,128]{1,0:T(1,128)S(1)} %get-tuple-element.62.pos, s32[1,1]{1,0:T(1,128)} %bitcast.11.count, f32[2,64,128]{2,1,0:T(8,128)S(1)} %history.1.base, f32[32,64]{1,0:T(8,128)S(1)} %bitcast.15), custom_call_target="tpu_custom_call" | custom-call | tf_op jit(solution)/shard_map/responses/pallas_call | solution.py:674
  (14 shorter events, 0.0 us)
Async XLA Ops:
  2.3 4.6 %collective-permute-start = (f32[24,16,384]{2,1,0:T(8,128)S(1)}, f32[24,16,384]{2,1,0:T(8,128)S(1)}, u32[]{:S(2)}, u32[]{:S(2)}) collective-permute-start(f32[24,16,384]{2,1,0:T(8,128)S(1)} %get-tuple-element.35), channel_id=1, source_target_pairs={{0,8},{8,0},{16,24},{24,16},{32,40},{40,32},{48,56},{56,48},{64,72... | collective-permute-start | bytes 1769480 | tf_op jit(solution)/shard_map/ppermute | solution.py:688
  3.7 11.2 %collective-permute-start.1 = (f32[24,16,384]{2,1,0:T(8,128)S(1)}, f32[24,16,384]{2,1,0:T(8,128)S(1)}, u32[]{:S(2)}, u32[]{:S(2)}) collective-permute-start(f32[24,16,384]{2,1,0:T(8,128)S(1)} %get-tuple-element.36), channel_id=1, source_target_pairs={{8,16},{16,8},{24,32},{32,24},{40,48},{48,40},{56,64},{64,56},{72,... | collective-permute-start | bytes 1769480 | tf_op jit(solution)/shard_map/ppermute | solution.py:688
  15.0 11.9 %collective-permute-start.2 = (f32[3,24,2,384]{3,2,1,0:T(2,128)S(1)}, f32[3,24,2,384]{3,2,1,0:T(2,128)S(1)}, u32[]{:S(2)}, u32[]{:S(2)}) collective-permute-start(f32[3,24,2,384]{3,2,1,0:T(2,128)S(1)} %get-tuple-element.37), channel_id=1, source_target_pairs={{0,1},{1,0},{2,3},{3,2},{4,5},{5,4},{6,7},{7,6},{8,9},{9,8},{10,11... | collective-permute-start | bytes 663560 | tf_op jit(solution)/shard_map/ppermute | solution.py:688
  19.1 7.9 %collective-permute-start.3 = (f32[3,24,2,384]{3,2,1,0:T(2,128)S(1)}, f32[3,24,2,384]{3,2,1,0:T(2,128)S(1)}, u32[]{:S(2)}, u32[]{:S(2)}) collective-permute-start(f32[3,24,2,384]{3,2,1,0:T(2,128)S(1)} %get-tuple-element.38), channel_id=1, source_target_pairs={{1,2},{2,1},{3,4},{4,3},{5,6},{6,5},{9,10},{10,9},{11,12},{12,11},... | collective-permute-start | bytes 663560 | tf_op jit(solution)/shard_map/ppermute | solution.py:688
  27.0 31.4 %copy-start.4 = (f32[192,64]{0,1:T(8,128)S(1)}, f32[192,64]{0,1:T(8,128)}, u32[]{:S(2)}) copy-start(f32[192,64]{0,1:T(8,128)} %param.20) | copy-start | bytes 147460
  27.0 31.4 %copy-start.5 = (s32[128,2]{0,1:T(2,128)S(1)}, s32[128,2]{0,1:T(2,128)}, u32[]{:S(2)}) copy-start(s32[128,2]{0,1:T(2,128)} %param.16) | copy-start | bytes 3076
  29.6 35.2 %collective-permute-start.4 = (f32[3,20,2,384]{3,2,1,0:T(2,128)S(1)}, f32[3,20,2,384]{3,2,1,0:T(2,128)S(1)}, u32[]{:S(2)}, u32[]{:S(2)}) collective-permute-start(f32[3,20,2,384]{3,2,1,0:T(2,128)S(1)} %get-tuple-element.47), channel_id=1, source_target_pairs={{0,1},{1,0},{2,3},{3,2},{4,5},{5,4},{6,7},{7,6},{8,9},{9,8},{10,11... | collective-permute-start | bytes 552968 | tf_op jit(solution)/shard_map/ppermute | solution.py:688
  34.8 30.0 %collective-permute-start.5 = (f32[3,20,2,384]{3,2,1,0:T(2,128)S(1)}, f32[3,20,2,384]{3,2,1,0:T(2,128)S(1)}, u32[]{:S(2)}, u32[]{:S(2)}) collective-permute-start(f32[3,20,2,384]{3,2,1,0:T(2,128)S(1)} %get-tuple-element.48), channel_id=1, source_target_pairs={{1,2},{2,1},{3,4},{4,3},{5,6},{6,5},{9,10},{10,9},{11,12},{12,11},... | collective-permute-start | bytes 552968 | tf_op jit(solution)/shard_map/ppermute | solution.py:688
  64.8 9.6 %copy-start = (f32[31,64,128]{2,1,0:T(8,128)S(1)}, f32[31,64,128]{2,1,0:T(8,128)}, u32[]{:S(2)}) copy-start(f32[31,64,128]{2,1,0:T(8,128)} %hist.1) | copy-start | bytes 3047428
  64.8 9.6 %copy-start.3 = (f32[64,32]{0,1:T(8,128)S(1)}, f32[64,32]{0,1:T(8,128)}, u32[]{:S(2)}) copy-start(f32[64,32]{0,1:T(8,128)} %param.21) | copy-start | bytes 24580
  68.5 0.7 copy-start.1
  69.2 14.4 %all-to-all-start.1 = ((f32[128,2,128]{2,1,0:T(2,128)}), f32[128,2,128]{2,1,0:T(2,128)S(1)}, u32[]{:S(2)}, u32[]{:S(2)}) async-start(f32[128,2,128]{2,1,0:T(2,128)} %bitcast.6), calls=%async_computation.1 | async-start | bytes 262144 | tf_op jit(solution)/shard_map/all_to_all | solution.py:727
  73.7 1.4 %copy-start.2 = (f32[3,16,16,128]{3,2,1,0:T(8,128)S(1)}, f32[3,16,16,128]{3,2,1,0:T(8,128)}, u32[]{:S(2)}) copy-start(f32[3,16,16,128]{3,2,1,0:T(8,128)} %copy-done.1) | copy-start | bytes 1179652

commit v6 on v5

--- a/solution.py
+++ b/solution.py
@@ -286,29 +286,37 @@
     add_north(rim, pack, main, mid, ex, ey, 0, main.shape[3] // LANES)
     odd = parity("gy")
 
+    wide = rows + 4
+
+    def gather(edge, first):
+        cells = slice(first, first + 2)
+        edge[0:wide] = mid[0, :, cells, :]
+        edge[wide : 2 * wide] = mid[1, :, cells, :]
+        edge[2 * wide :] = mid[2, 2 : wide - 2, cells, :]
+
     @pl.when(odd == 0)
     def _():
-        ma[...] = mid[:, :, 14:16, :]
-        mb[...] = mid[:, :, 0:2, :]
+        gather(ma, 14)
+        gather(mb, 0)
 
     @pl.when(odd == 1)
     def _():
-        ma[...] = mid[:, :, 0:2, :]
-        mb[...] = mid[:, :, 14:16, :]
+        gather(ma, 0)
+        gather(mb, 14)
 
     top[...] = surface_rows(mid.at[:, pl.ds(2, rows)], 0)
 
 
 def first_north(main, pack, ya, yb):
     _, wide, _, depth = main.shape
-    edge = pltpu.VMEM((3, wide, 2, depth), F32)
+    edge = pltpu.VMEM((3 * wide - 4, 2, depth), F32)
     return pl.pallas_call(
         first_north_kernel,
         out_shape=(pltpu.VMEM(main.shape, F32), edge, edge, pltpu.VMEM((8, SIDE * SIDE), F32)),
         in_specs=[VMEM_SPEC] * 4,
         out_specs=(VMEM_SPEC,) * 4,
         scratch_shapes=[
-            pltpu.VMEM((3, wide + 4, 24, depth), F32),
+            pltpu.VMEM((3, wide + 4, 8, depth), F32),
             pltpu.VMEM((wide + 4, 8, depth), F32),
             pltpu.VMEM((wide + 4, 8, depth), F32),
         ],
@@ -350,19 +358,24 @@
 
 def fill_north(rim, ya, yb):
     odd_y = parity("gy")
-    rim[:, :, 8:16, :] = jnp.zeros((rim.shape[0], rim.shape[1], 8, rim.shape[3]), F32)
-
-    wide = rim.shape[3]
+    rows, wide = rim.shape[1], rim.shape[3]
+    rim[:, :, 2:6, :] = jnp.zeros((rim.shape[0], rows, 4, wide), F32)
+
+    def place(edge, first):
+        cells = slice(first, first + 2)
+        rim[0, :, cells, :] = edge[0:rows, :, :wide]
+        rim[1, :, cells, :] = edge[rows : 2 * rows, :, :wide]
+        rim[2, 2 : rows - 2, cells, :] = edge[2 * rows :, :, :wide]
 
     @pl.when(odd_y == 0)
     def _():
-        rim[:, :, 6:8, :] = yb[:, :, :, :wide]
-        rim[:, :, 16:18, :] = ya[:, :, :, :wide]
+        place(yb, 0)
+        place(ya, 6)
 
     @pl.when(odd_y == 1)
     def _():
-        rim[:, :, 6:8, :] = ya[:, :, :, :wide]
-        rim[:, :, 16:18, :] = yb[:, :, :, :wide]
+        place(ya, 0)
+        place(yb, 6)
 
 
 def add_north(rim, pack, main, out, ex, ey, first, last, base=0, done=None, parts=1):
@@ -373,8 +386,22 @@
     local = lambda k: pl.ds((k - base) * LANES, LANES)
     below, above = max(first - 1, 0), min(last + 1, total)
 
-    def y_four(c, r, k):
-        return [rim[c, r, pl.ds(8 + d, 8), lanes(k)] for d in (1, -1, 2, -2)]
+    sub = iota((8, LANES), 0)
+    low = sub < 4
+
+    def rim_parts(c, r, k):
+        two = rim[c, r, :, lanes(k)]
+        one = jnp.where(sub == 7, pltpu.roll(two, 1, axis=0), 0.0)
+        return jnp.where(sub == 0, pltpu.roll(two, 7, axis=0), one), two
+
+    def slope(c, r, k):
+        one, two = rim_parts(c, r, k)
+        change = one - two * 0.125
+        return jnp.where(low, -change, change)
+
+    def bend(c, r, k):
+        one, two = rim_parts(c, r, k)
+        return one - two * 0.0625
 
     def ends(get):
         return (
@@ -385,9 +412,9 @@
 
     def inner(r):
         for k in range(below, above):
-            ey[r, :, lanes(k)] = first_of(*y_four(1, r, k))
+            ey[r, :, lanes(k)] = slope(1, r, k)
         for k in span:
-            ex[r, :, lanes(k)] = first_of(*y_four(0, r, k))
+            ex[r, :, lanes(k)] = slope(0, r, k)
 
     def inner_two(pair, carry):
         inner(2 * pair)
@@ -398,9 +425,8 @@
 
     def outer(i):
         r = i + 2
-        yz = z_first(*ends(lambda k: first_of(*y_four(2, r, k))))
+        yz = z_first(*ends(lambda k: slope(2, r, k)))
         xy = z_first(*ends(lambda k: ey[r, :, lanes(k)]))
-        low = iota((8, LANES), 0) < 4
         for n, k in enumerate(span):
 
             def derived(ref):
@@ -409,7 +435,7 @@
             shear, both, scale = [pack[which, i, :, local(k)] for which in range(3)]
             mixed = [derived(ey), derived(ex) + yz[n], xy[n]]
             for c in range(3):
-                q = second_of(*y_four(c, r, k))
+                q = bend(c, r, k)
                 along = mixed[c] * (1.0 / 3.0)
                 if c == 1:
                     along = along + q
@@ -524,7 +550,7 @@
         in_specs=[VMEM_SPEC] * 7,
         out_specs=(VMEM_SPEC,) * 2,
         scratch_shapes=[
-            pltpu.VMEM((3, rows + 4, 24, 2 * LANES), F32),
+            pltpu.VMEM((3, rows + 4, 8, 2 * LANES), F32),
             pltpu.VMEM((rows + 4, 8, 2 * LANES), F32),
             pltpu.VMEM((rows + 4, 8, 2 * LANES), F32),
             pltpu.VMEM((8 * LANES, LANES), F32),
@@ -555,7 +581,7 @@
         in_specs=[VMEM_SPEC] * 5,
         out_specs=HBM_SPEC,
         scratch_shapes=[
-            pltpu.VMEM((3, rows + 4, 24, depth), F32),
+            pltpu.VMEM((3, rows + 4, 8, depth), F32),
             pltpu.VMEM(main.shape, F32),
             pltpu.VMEM((rows + 4, 8, depth), F32),
             pltpu.VMEM((rows + 4, 8, depth), F32),
@@ -570,11 +596,17 @@
     rows = low.shape[1]
     odd_x, odd_y = parity("gx"), parity("gy")
 
+    wide = rows + 8
+
     def gather(out, own, edge):
-        out[:, 4 : rows + 4] = own[...]
+        cells = slice(edge, edge + 2)
+        for c in range(3):
+            start = c * wide + (2 if c == 2 else 4)
+            out[start : start + rows] = own[c]
         for rim, side in ((xa, 1 - odd_x), (xb, odd_x)):
-            for c in range(3):
-                out[c, pl.ds((rows + 4) * side, 4)] = rim[4 * c : 4 * c + 4, edge : edge + 2, :]
+            for c in range(2):
+                out[pl.ds(c * wide + (rows + 4) * side, 4)] = rim[4 * c : 4 * c + 4, cells, :]
+            out[pl.ds(2 * wide + (rows + 2) * side, 2)] = rim[pl.ds(10 - 2 * side, 2), cells, :]
 
     last = SIDE - 2
 
@@ -591,7 +623,7 @@
 
 def north_edges(low, high, xa, xb):
     _, rows, two, depth = low.shape
-    out = pltpu.VMEM((3, rows + 8, two, depth), F32)
+    out = pltpu.VMEM((3 * (rows + 8) - 4, two, depth), F32)
     return pl.pallas_call(
         north_kernel,
         out_shape=(out, out),

time: 85 us -> 84.4 us (level)
  no operation moved by 1% of the time
where the time goes in v6:
time: 84.4 us; the launch traced here: 84.1 us
  Pallas kernels  24.8 us (29%)
  blocking collectives  22.8 us (27%)
  starting transfers between devices  19.7 us (23%)
  waiting for transfers between devices  14.6 us (17%)
  between operations  1.53 us (2%)
    all_to_all x1, blocking collectives, exchange(): out = lax.all_to_all(rows, ('gx', 'gy'), split_axis=0, concat_axis=0)  22.8 us
    ppermute x6, starting transfers between devices, swap(): return in_vmem(lax.ppermute(array, axis, pairs))  15.2 us
    ppermute x6, waiting for transfers between devices, swap(): return in_vmem(lax.ppermute(array, axis, pairs))  8.06 us
    pallas_call x1, Pallas kernels, first_main(): pl.pallas_call(first_main_kernel, out_shape=(pltpu.VMEM((3, wide, cols, d...  7.17 us
    all_to_all x1, waiting for transfers between devices, exchange(): out = lax.all_to_all(rows, ('gx', 'gy'), split_axis=0, concat_axis=0)  6.5 us
    pallas_call x1, Pallas kernels, second_main(): pl.pallas_call(second_main_kernel, out_shape=(pltpu.HBM(prev.shape, F32),...  5.02 us
    all_to_all x1, starting transfers between devices, exchange(): out = lax.all_to_all(rows, ('gx', 'gy'), split_axis=0, concat_axis=0)  4.46 us
    pallas_call x1, Pallas kernels, near_north(): pl.pallas_call(near_north_kernel, out_shape=(pltpu.VMEM((3, rows, cols, L...  3.43 us
  transfers between devices with their start and end apart: 7, of which 2 were waited for; matrix products, arithmetic and copies ran while one was open for 0% of the time, Pallas kernels for 19%

profile of v6, /device:TPU:1, one launch (start us, length us, event | category | flops | bytes accessed | tf_op | source)
XLA Modules:
  0.0 84.1 jit_solution(6883776501052925412)
XLA Ops:
  0.6 1.6 %east_pack.1 = (f32[24,16,384]{2,1,0:T(8,128)S(1)}, f32[24,16,384]{2,1,0:T(8,128)S(1)}, f32[3,16,2,384]{3,2,1,0:T(2,128)S(1)}, f32[3,16,2,384]{3,2,1,0:T(2,128)S...) custom-call(f32[3,16,16,384]{3,2,1,0:T(8,128)} %prev.5, f32[3,16,16,384]{3,2,1,0:T(8,128)} %prev.4, ...), custom_call_target="tpu_custom_call" | custom-call | tf_op jit(solution)/shard_map/east_pack/pallas_call | solution.py:222
  2.3 1.5 %collective-permute-start = (f32[24,16,384]{2,1,0:T(8,128)S(1)}, f32[24,16,384]{2,1,0:T(8,128)S(1)}, u32[]{:S(2)}, u32[]{:S(2)}) collective-permute-start(f32[24,16,384]{2,1,0:T(8,128)S(1)} %get-tuple-element.35), channel_id=1, source_target_pairs={{0,8},{8,0},{16,24},{24,16},{32,40},{40,32},{48,56},{56,48},{64,72... | collective-permute-start | bytes 1769480 | tf_op jit(solution)/shard_map/ppermute | solution.py:720
  3.7 3.1 %collective-permute-start.1 = (f32[24,16,384]{2,1,0:T(8,128)S(1)}, f32[24,16,384]{2,1,0:T(8,128)S(1)}, u32[]{:S(2)}, u32[]{:S(2)}) collective-permute-start(f32[24,16,384]{2,1,0:T(8,128)S(1)} %get-tuple-element.36), channel_id=1, source_target_pairs={{8,16},{16,8},{24,32},{32,24},{40,48},{48,40},{56,64},{64,56},{72,... | collective-permute-start | bytes 1769480 | tf_op jit(solution)/shard_map/ppermute | solution.py:720
  6.9 8.0 %collective-permute-done.1.xb = f32[24,16,384]{2,1,0:T(8,128)S(1)} collective-permute-done((f32[24,16,384]{2,1,0:T(8,128)S(1)}, f32[24,16,384]{2,1,0:T(8,128)S(1)}, u32[]{:S(2)}, u32[]{:S(2)}) %collective-permute-start.1) | collective-permute-done | bytes 589856 | tf_op jit(solution)/shard_map/ppermute | solution.py:720
  14.9 0.1 north_edges.1
  15.0 4.1 %collective-permute-start.2 = (f32[68,2,384]{2,1,0:T(2,128)S(1)}, f32[68,2,384]{2,1,0:T(2,128)S(1)}, u32[]{:S(2)}, u32[]{:S(2)}) collective-permute-start(f32[68,2,384]{2,1,0:T(2,128)S(1)} %get-tuple-element.37), channel_id=1, source_target_pairs={{0,1},{1,0},{2,3},{3,2},{4,5},{5,4},{6,7},{7,6},{8,9},{9,8},{10,11... | collective-permute-start | bytes 626696 | tf_op jit(solution)/shard_map/ppermute | solution.py:720
  19.1 0.7 collective-permute-start.3
  19.8 7.2 %first_main.1 = (f32[3,20,16,384]{3,2,1,0:T(8,128)S(1)}, f32[3,20,8,384]{3,2,1,0:T(8,128)S(1)}) custom-call(f32[3,16,16,384]{3,2,1,0:T(8,128)} %prev.4, f32[16,16,384]{2,1,0:T(8,128)} %buoy.5, f32[16,16,384]{2,1,0:T(8,128)} %mu.5, f32[16,16,384]{2,1,0:T(8,128)} %lam.5, f32[3,16,16,384]{3,2,1,0:T(8,128)} %prev.5, f32[24,16,384]{2,1,0:T(8,128)S(1)} %collective-permute-done.xa, ...), custom_call_target="tpu_custom_call" | custom-call | tf_op jit(solution)/shard_map/first_main/pallas_call | solution.py:264
  27.0 0.0 copy-start.5
  27.0 2.2 %first_north.1 = (f32[3,20,16,384]{3,2,1,0:T(8,128)S(1)}, f32[56,2,384]{2,1,0:T(2,128)S(1)}, f32[56,2,384]{2,1,0:T(2,128)S(1)}, f32[8,256]{1,0:T(8,128)S(1)}) custom-call(f32[3,20,16,384]{3,2,1,0:T(8,128)S(1)} %get-tuple-element.41.main, f32[3,20,8,384]{3,2,1,0:T(8,128)S(1)} %get-tuple-element.42.pack, f32[68,2,384]{2,1,0:T(2,128)S(1)} %collective-permute-done.2.ya, ...), custom_call_target="tpu_custom_call" | custom-call | tf_op jit(solution)/shard_map/first_north/pallas_call | solution.py:313
  29.2 5.2 %collective-permute-start.4 = (f32[56,2,384]{2,1,0:T(2,128)S(1)}, f32[56,2,384]{2,1,0:T(2,128)S(1)}, u32[]{:S(2)}, u32[]{:S(2)}) collective-permute-start(f32[56,2,384]{2,1,0:T(2,128)S(1)} %get-tuple-element.47), channel_id=1, source_target_pairs={{0,1},{1,0},{2,3},{3,2},{4,5},{5,4},{6,7},{7,6},{8,9},{9,8},{10,11... | collective-permute-start | bytes 516104 | tf_op jit(solution)/shard_map/ppermute | solution.py:720
  34.5 0.7 collective-permute-start.5
  35.1 22.8 %all_to_all.10 = s32[128,1,128]{2,1,0:T(1,128)S(1)} all-to-all(s32[128,1,128]{2,1,0:T(1,128)S(1)} %bitcast.17), channel_id=1, replica_groups=mesh['gx'=16,'gy'=8] {'gx','gy'}, dimensions={0} | all-to-all | bytes 131072 | tf_op jit(solution)/shard_map/all_to_all | solution.py:759
  57.9 0.5 prepare.1
  58.4 5.0 %second_main.1 = (f32[3,16,16,384]{3,2,1,0:T(8,128)}, f32[3,16,16,384]{3,2,1,0:T(8,128)S(1)}, f32[3,16,8,384]{3,2,1,0:T(8,128)S(1)}) custom-call(f32[3,16,16,384]{3,2,1,0:T(8,128)} %prev.5, f32[16,16,384]{2,1,0:T(8,128)} %buoy.5, f32[16,16,384]{2,1,0:T(8,128)} %mu.5, f32[16,16,384]{2,1,0:T(8,128)} %lam.5, f32[3,20,16,384]{3,2,1,0:T(8,128)S(1)} %get-tuple-element.45.vp), custom_call_target="tpu_custom_call" | custom-call | tf_op jit(solution)/shard_map/second_main/pallas_call | solution.py:341
  63.4 0.9 %early_forces.1.early = f32[256,64]{1,0:T(8,128)S(1)} custom-call(f32[8,256]{1,0:T(8,128)S(1)} %get-tuple-element.51.top, f32[256,128]{1,0:T(8,128)S(1)} %get-tuple-element.53.chosen, f32[3,128,64]{2,1,0:T(8,128)S(1)} %get-tuple-element.54.weights), custom_call_target="tpu_custom_call" | custom-call | tf_op jit(solution)/shard_map/early_forces/pallas_call | solution.py:526
  64.4 0.0 copy-start
  64.4 3.4 %near_north.1 = (f32[3,16,16,128]{3,2,1,0:T(8,128)S(1)}, f32[256,128]{1,0:T(8,128)}) custom-call(f32[3,16,16,384]{3,2,1,0:T(8,128)S(1)} %get-tuple-element.55.main, f32[3,16,8,384]{3,2,1,0:T(8,128)S(1)} %get-tuple-element.56.pack, f32[56,2,384]{2,1,0:T(2,128)S(1)} %collective-permute-done.4.ya, f32[56,2,384]{2,1,0:T(2,128)S(1)} %collective-permute-done.5.yb, ...), custom_call_target="tpu_custom_call" | custom-call | tf_op jit(solution)/shard_map/near_north/pallas_call | solution.py:547
  67.9 0.7 copy-done.1
  68.6 4.5 %all-to-all-start.1 = ((f32[128,2,128]{2,1,0:T(2,128)}), f32[128,2,128]{2,1,0:T(2,128)S(1)}, u32[]{:S(2)}, u32[]{:S(2)}) async-start(f32[128,2,128]{2,1,0:T(2,128)} %bitcast.6), calls=%async_computation.1 | async-start | bytes 262144 | tf_op jit(solution)/shard_map/all_to_all | solution.py:759
  73.8 0.7 history.1.base
  74.5 2.0 %far_north.1 = f32[3,16,16,384]{3,2,1,0:T(8,128)} custom-call(f32[3,16,16,384]{3,2,1,0:T(8,128)S(1)} %get-tuple-element.55.main, f32[3,16,8,384]{3,2,1,0:T(8,128)S(1)} %get-tuple-element.56.pack, f32[3,16,16,128]{3,2,1,0:T(8,128)S(1)} %copy-done.2, f32[56,2,384]{2,1,0:T(2,128)S(1)} %collective-permute-done.4.ya, f32[56,2,384]{2,1,0:T(2,128)S(1)} %collective-permute-done.5.yb), custom_call_target="tpu_custom_call" | custom-call | tf_op jit(solution)/shard_map/far_north/pallas_call | solution.py:578
  76.5 6.5 %all-to-all-done.1 = f32[128,2,128]{2,1,0:T(2,128)S(1)} async-done(((f32[128,2,128]{2,1,0:T(2,128)}), f32[128,2,128]{2,1,0:T(2,128)S(1)}, u32[]{:S(2)}, u32[]{:S(2)}) %all-to-all-start.1) | async-done | bytes 131104 | tf_op jit(solution)/shard_map/all_to_all | solution.py:759
  83.0 1.1 %responses.1 = f32[2,64,128]{2,1,0:T(8,128)} custom-call(f32[256,128]{1,0:T(8,128)S(1)} %bitcast.12, s32[1,128]{1,0:T(1,128)S(1)} %get-tuple-element.62.pos, s32[1,1]{1,0:T(1,128)} %bitcast.11.count, f32[2,64,128]{2,1,0:T(8,128)S(1)} %history.1.base, f32[32,64]{1,0:T(8,128)S(1)} %bitcast.15), custom_call_target="tpu_custom_call" | custom-call | tf_op jit(solution)/shard_map/responses/pallas_call | solution.py:706
  (14 shorter events, 0.0 us)
Async XLA Ops:
  2.3 4.6 %collective-permute-start = (f32[24,16,384]{2,1,0:T(8,128)S(1)}, f32[24,16,384]{2,1,0:T(8,128)S(1)}, u32[]{:S(2)}, u32[]{:S(2)}) collective-permute-start(f32[24,16,384]{2,1,0:T(8,128)S(1)} %get-tuple-element.35), channel_id=1, source_target_pairs={{0,8},{8,0},{16,24},{24,16},{32,40},{40,32},{48,56},{56,48},{64,72... | collective-permute-start | bytes 1769480 | tf_op jit(solution)/shard_map/ppermute | solution.py:720
  3.7 11.2 %collective-permute-start.1 = (f32[24,16,384]{2,1,0:T(8,128)S(1)}, f32[24,16,384]{2,1,0:T(8,128)S(1)}, u32[]{:S(2)}, u32[]{:S(2)}) collective-permute-start(f32[24,16,384]{2,1,0:T(8,128)S(1)} %get-tuple-element.36), channel_id=1, source_target_pairs={{8,16},{16,8},{24,32},{32,24},{40,48},{48,40},{56,64},{64,56},{72,... | collective-permute-start | bytes 1769480 | tf_op jit(solution)/shard_map/ppermute | solution.py:720
  15.0 11.9 %collective-permute-start.2 = (f32[68,2,384]{2,1,0:T(2,128)S(1)}, f32[68,2,384]{2,1,0:T(2,128)S(1)}, u32[]{:S(2)}, u32[]{:S(2)}) collective-permute-start(f32[68,2,384]{2,1,0:T(2,128)S(1)} %get-tuple-element.37), channel_id=1, source_target_pairs={{0,1},{1,0},{2,3},{3,2},{4,5},{5,4},{6,7},{7,6},{8,9},{9,8},{10,11... | collective-permute-start | bytes 626696 | tf_op jit(solution)/shard_map/ppermute | solution.py:720
  19.1 7.9 %collective-permute-start.3 = (f32[68,2,384]{2,1,0:T(2,128)S(1)}, f32[68,2,384]{2,1,0:T(2,128)S(1)}, u32[]{:S(2)}, u32[]{:S(2)}) collective-permute-start(f32[68,2,384]{2,1,0:T(2,128)S(1)} %get-tuple-element.38), channel_id=1, source_target_pairs={{1,2},{2,1},{3,4},{4,3},{5,6},{6,5},{9,10},{10,9},{11,12},{12,11},... | collective-permute-start | bytes 626696 | tf_op jit(solution)/shard_map/ppermute | solution.py:720
  27.0 31.0 %copy-start.4 = (f32[192,64]{0,1:T(8,128)S(1)}, f32[192,64]{0,1:T(8,128)}, u32[]{:S(2)}) copy-start(f32[192,64]{0,1:T(8,128)} %param.20) | copy-start | bytes 147460
  27.0 30.9 %copy-start.5 = (s32[128,2]{0,1:T(2,128)S(1)}, s32[128,2]{0,1:T(2,128)}, u32[]{:S(2)}) copy-start(s32[128,2]{0,1:T(2,128)} %param.16) | copy-start | bytes 3076
  29.2 35.2 %collective-permute-start.4 = (f32[56,2,384]{2,1,0:T(2,128)S(1)}, f32[56,2,384]{2,1,0:T(2,128)S(1)}, u32[]{:S(2)}, u32[]{:S(2)}) collective-permute-start(f32[56,2,384]{2,1,0:T(2,128)S(1)} %get-tuple-element.47), channel_id=1, source_target_pairs={{0,1},{1,0},{2,3},{3,2},{4,5},{5,4},{6,7},{7,6},{8,9},{9,8},{10,11... | collective-permute-start | bytes 516104 | tf_op jit(solution)/shard_map/ppermute | solution.py:720
  34.5 29.9 %collective-permute-start.5 = (f32[56,2,384]{2,1,0:T(2,128)S(1)}, f32[56,2,384]{2,1,0:T(2,128)S(1)}, u32[]{:S(2)}, u32[]{:S(2)}) collective-permute-start(f32[56,2,384]{2,1,0:T(2,128)S(1)} %get-tuple-element.48), channel_id=1, source_target_pairs={{1,2},{2,1},{3,4},{4,3},{5,6},{6,5},{9,10},{10,9},{11,12},{12,11},... | collective-permute-start | bytes 516104 | tf_op jit(solution)/shard_map/ppermute | solution.py:720
  64.4 9.4 %copy-start = (f32[31,64,128]{2,1,0:T(8,128)S(1)}, f32[31,64,128]{2,1,0:T(8,128)}, u32[]{:S(2)}) copy-start(f32[31,64,128]{2,1,0:T(8,128)} %hist.1) | copy-start | bytes 3047428
  64.4 9.4 %copy-start.3 = (f32[64,32]{0,1:T(8,128)S(1)}, f32[64,32]{0,1:T(8,128)}, u32[]{:S(2)}) copy-start(f32[64,32]{0,1:T(8,128)} %param.21) | copy-start | bytes 24580
  67.9 0.7 copy-start.1
  68.6 14.4 %all-to-all-start.1 = ((f32[128,2,128]{2,1,0:T(2,128)}), f32[128,2,128]{2,1,0:T(2,128)S(1)}, u32[]{:S(2)}, u32[]{:S(2)}) async-start(f32[128,2,128]{2,1,0:T(2,128)} %bitcast.6), calls=%async_computation.1 | async-start | bytes 262144 | tf_op jit(solution)/shard_map/all_to_all | solution.py:759
  73.1 1.4 %copy-start.2 = (f32[3,16,16,128]{3,2,1,0:T(8,128)S(1)}, f32[3,16,16,128]{3,2,1,0:T(8,128)}, u32[]{:S(2)}) copy-start(f32[3,16,16,128]{3,2,1,0:T(8,128)} %copy-done.1) | copy-start | bytes 1179652

commit v7 on v6

--- a/solution.py
+++ b/solution.py
@@ -80,7 +80,7 @@
     return out
 
 
-def run_step(vp, prev, buoy, mu, lam, out, pack, work, ready):
+def run_step(vp, prev, buoy, mu, lam, out, pack, work, ready, arrived=None, late=0):
     byx, syz, dyy, dyz, qyx, qyy, qyz, qzz = work
     rows = vp.shape[1] - 4
     span = range(vp.shape[3] // LANES)
@@ -110,18 +110,24 @@
                         (qyx, qyy, qyz)[c][i, tile(h), lanes(k)] = second_of(*four[h])
 
     def each(start, stop, full):
-        def trip(r, carry):
-            inner(r, full)
+        def trip(pair, carry):
+            inner(start + 2 * pair, full)
+            inner(start + 2 * pair + 1, full)
             return carry
 
-        lax.fori_loop(start, stop, trip, 0)
+        lax.fori_loop(0, (stop - start) // 2, trip, 0)
 
     each(0, 2, False)
-    each(2, rows + 2, True)
     each(rows + 2, rows + 4, False)
+    if arrived is not None:
+        each(2, late, True)
+        each(rows + 4 - late, rows + 2, True)
+        arrived()
+    start = max(2, late)
+    each(start, rows + 4 - start, True)
     ready()
 
-    def outer(i, carry):
+    def outer(i):
         r = i + 2
         low = iota((8, LANES), 0) < 4
         lower = {}
@@ -158,9 +164,13 @@
                     along = (q[c] - centre * 1.875) + mixed[c] * (1.0 / 3.0)
                     update = shear * laplace + both * along
                     out[c, i, here, lanes(k)] = (2.0 * centre - prev[c, i, here, lanes(k)]) + scale * update
+
+    def outer_two(pair, carry):
+        outer(2 * pair)
+        outer(2 * pair + 1)
         return carry
 
-    lax.fori_loop(0, rows, outer, 0)
+    lax.fori_loop(0, rows // 2, outer_two, 0)
 
 
 def step_work(rows, cols, depth):
@@ -253,8 +263,9 @@
             pv[c, two] = edge[12 + 2 * c : 14 + 2 * c]
         for n, field in enumerate((bv, mv, lv)):
             field[two] = edge[18 + 2 * n : 20 + 2 * n]
-    copies[0].wait()
-    run_step(vp, pv, bv, mv, lv, out, pack, work[:-1], lambda: wait_all(copies[1:]))
+    run_step(
+        vp, pv, bv, mv, lv, out, pack, work[:-1], lambda: wait_all(copies[1:]), arrived=copies[0].wait, late=4
+    )
 
 
 def first_main(now, xa, xb, prev, buoy, mu, lam):
@@ -472,12 +483,18 @@
 
 def corner_forces(flat, weights, windows):
     window_tables(flat, windows)
-    total = jnp.zeros((LANES, weights.shape[2]), F32)
-    for c in range(3):
-        total = total + jnp.dot(
-            windows[pl.ds(c, LANES, stride=8), :], weights[c], precision=HIGHEST, preferred_element_type=F32
-        )
-    return total
+    both = []
+    for n in range(2):
+        total = jnp.zeros((LANES, weights.shape[2]), F32)
+        for c in range(3):
+            total = total + jnp.dot(
+                windows[pl.ds(3 * n + c, LANES, stride=8), :],
+                weights[c],
+                precision=HIGHEST,
+                preferred_element_type=F32,
+            )
+        both.append(total)
+    return jnp.concatenate(both, axis=1)
 
 
 def spread(part, c):
@@ -517,32 +534,14 @@
     )(asked, offset, part)
 
 
-def early_kernel(top, chosen, weights, early, windows):
-    forces = corner_forces(top[...], weights, windows)
-    early[...] = jnp.dot(chosen[...], forces, precision=HIGHEST, preferred_element_type=F32)
-
-
-def early_forces(top, chosen, weights):
-    return pl.pallas_call(
-        early_kernel,
-        out_shape=pltpu.VMEM((2 * LANES, weights.shape[2]), F32),
-        in_specs=[VMEM_SPEC] * 3,
-        out_specs=VMEM_SPEC,
-        scratch_shapes=[pltpu.VMEM((8 * LANES, LANES), F32)],
-        compiler_params=pltpu.CompilerParams(vmem_limit_bytes=VMEM_BYTES),
-        name="early_forces",
-    )(top, chosen, weights)
-
-
-def near_north_kernel(main, pack, ya, yb, chosen, weights, early, near, ans, rim, ex, ey, windows):
+def near_north_kernel(main, pack, ya, yb, top, chosen, weights, near, ans, rim, ex, ey, windows):
     fill_north(rim, ya, yb)
     add_north(rim, pack, main, near, ex, ey, 0, 1)
-    forces = corner_forces(surface_rows(near, 0), weights, windows)
-    late = jnp.dot(chosen[...], forces, precision=HIGHEST, preferred_element_type=F32)
-    ans[...] = jnp.concatenate([early[...], late], axis=1)
-
-
-def near_north(main, pack, ya, yb, chosen, weights, early):
+    forces = corner_forces(top[...] + surface_rows(near, 3), weights, windows)
+    ans[...] = jnp.dot(chosen[...], forces, precision=HIGHEST, preferred_element_type=F32)
+
+
+def near_north(main, pack, ya, yb, top, chosen, weights):
     _, rows, cols, _ = main.shape
     return pl.pallas_call(
         near_north_kernel,
@@ -557,7 +556,7 @@
         ],
         compiler_params=pltpu.CompilerParams(vmem_limit_bytes=VMEM_BYTES),
         name="near_north",
-    )(main, pack, ya, yb, chosen, weights, early)
+    )(main, pack, ya, yb, top, chosen, weights)
 
 
 def far_north_kernel(main, pack, near, ya, yb, nxt, rim, out, ex, ey, sems):
@@ -773,10 +772,9 @@
     mid, ya, yb, top = first_north(*main, *north)
     north = north_swaps(ya, yb)
     prepared = prepare(in_vmem(asked), offset, part)
-    early = early_forces(top, *prepared)
     disp_mid, main, pack = second_main(mid, in_hbm(now), *medium)
-    north, main, pack, early = lax.optimization_barrier((north, main, pack, early))
-    near, ans = near_north(main, pack, *north, *prepared, early)
+    north, main, pack, prepared = lax.optimization_barrier((north, main, pack, prepared))
+    near, ans = near_north(main, pack, *north, in_vmem(top), *prepared)
     back = exchange(ans)
     base = in_vmem(history_part(history, kernels))
     disp_next = far_north(in_vmem(main), in_vmem(pack), in_vmem(near), *(in_vmem(a) for a in north))

time: 84.4 us -> 81.2 us (0.962)
  Pallas kernels: 24.8 us -> 21.5 us
    pallas_call x1, Pallas kernels: 7.17 us -> 5.12 us  [first_main(): pl.pallas_call(first_main_kernel, out_shape=(pltpu.VMEM((3, wide, cols, d...]
    pallas_call x1 -> x0, Pallas kernels: 0.94 us -> none  [early_forces(): pl.pallas_call(early_kernel, out_shape=pltpu.VMEM((2 * LANES, weights.sha...]
  transfers between devices with their start and end apart: 7 -> 7, of which waited for: 2 -> 3; matrix products, arithmetic and copies ran while one was open for 0% -> 0% of each run, Pallas kernels for 19% -> 16%
where the time goes in v7:
time: 81.2 us; the launch traced here: 80.9 us
  blocking collectives  22.8 us (28%)
  Pallas kernels  21.5 us (26%)
  starting transfers between devices  19.4 us (24%)
  waiting for transfers between devices  14.8 us (18%)
  between operations  1.49 us (2%)
    all_to_all x1, blocking collectives, exchange(): out = lax.all_to_all(rows, ('gx', 'gy'), split_axis=0, concat_axis=0)  22.8 us
    ppermute x6, starting transfers between devices, swap(): return in_vmem(lax.ppermute(array, axis, pairs))  15 us
    ppermute x6, waiting for transfers between devices, swap(): return in_vmem(lax.ppermute(array, axis, pairs))  8.34 us
    all_to_all x1, waiting for transfers between devices, exchange(): out = lax.all_to_all(rows, ('gx', 'gy'), split_axis=0, concat_axis=0)  6.5 us
    pallas_call x1, Pallas kernels, first_main(): pl.pallas_call(first_main_kernel, out_shape=(pltpu.VMEM((3, wide, cols, d...  5.12 us
    pallas_call x1, Pallas kernels, second_main(): pl.pallas_call(second_main_kernel, out_shape=(pltpu.HBM(prev.shape, F32),...  4.54 us
    all_to_all x1, starting transfers between devices, exchange(): out = lax.all_to_all(rows, ('gx', 'gy'), split_axis=0, concat_axis=0)  4.46 us
    pallas_call x1, Pallas kernels, near_north(): pl.pallas_call(near_north_kernel, out_shape=(pltpu.VMEM((3, rows, cols, L...  3.67 us
  transfers between devices with their start and end apart: 7, of which 3 were waited for; matrix products, arithmetic and copies ran while one was open for 0% of the time, Pallas kernels for 16%

profile of v7, /device:TPU:1, one launch (start us, length us, event | category | flops | bytes accessed | tf_op | source)
XLA Modules:
  0.0 80.9 jit_solution(13147925032274118652)
XLA Ops:
  0.6 1.6 %east_pack.1 = (f32[24,16,384]{2,1,0:T(8,128)S(1)}, f32[24,16,384]{2,1,0:T(8,128)S(1)}, f32[3,16,2,384]{3,2,1,0:T(2,128)S(1)}, f32[3,16,2,384]{3,2,1,0:T(2,128)S...) custom-call(f32[3,16,16,384]{3,2,1,0:T(8,128)} %prev.5, f32[3,16,16,384]{3,2,1,0:T(8,128)} %prev.4, ...), custom_call_target="tpu_custom_call" | custom-call | tf_op jit(solution)/shard_map/east_pack/pallas_call | solution.py:232
  2.3 1.5 %collective-permute-start = (f32[24,16,384]{2,1,0:T(8,128)S(1)}, f32[24,16,384]{2,1,0:T(8,128)S(1)}, u32[]{:S(2)}, u32[]{:S(2)}) collective-permute-start(f32[24,16,384]{2,1,0:T(8,128)S(1)} %get-tuple-element.36), channel_id=1, source_target_pairs={{0,8},{8,0},{16,24},{24,16},{32,40},{40,32},{48,56},{56,48},{64,72... | collective-permute-start | bytes 1769480 | tf_op jit(solution)/shard_map/ppermute | solution.py:719
  3.7 3.1 %collective-permute-start.1 = (f32[24,16,384]{2,1,0:T(8,128)S(1)}, f32[24,16,384]{2,1,0:T(8,128)S(1)}, u32[]{:S(2)}, u32[]{:S(2)}) collective-permute-start(f32[24,16,384]{2,1,0:T(8,128)S(1)} %get-tuple-element.37), channel_id=1, source_target_pairs={{8,16},{16,8},{24,32},{32,24},{40,48},{48,40},{56,64},{64,56},{72,... | collective-permute-start | bytes 1769480 | tf_op jit(solution)/shard_map/ppermute | solution.py:719
  6.9 8.0 %collective-permute-done.1.xb = f32[24,16,384]{2,1,0:T(8,128)S(1)} collective-permute-done((f32[24,16,384]{2,1,0:T(8,128)S(1)}, f32[24,16,384]{2,1,0:T(8,128)S(1)}, u32[]{:S(2)}, u32[]{:S(2)}) %collective-permute-start.1) | collective-permute-done | bytes 589856 | tf_op jit(solution)/shard_map/ppermute | solution.py:719
  14.9 0.1 north_edges.1
  15.0 4.1 %collective-permute-start.2 = (f32[68,2,384]{2,1,0:T(2,128)S(1)}, f32[68,2,384]{2,1,0:T(2,128)S(1)}, u32[]{:S(2)}, u32[]{:S(2)}) collective-permute-start(f32[68,2,384]{2,1,0:T(2,128)S(1)} %get-tuple-element.38), channel_id=1, source_target_pairs={{0,1},{1,0},{2,3},{3,2},{4,5},{5,4},{6,7},{7,6},{8,9},{9,8},{10,11... | collective-permute-start | bytes 626696 | tf_op jit(solution)/shard_map/ppermute | solution.py:719
  19.1 0.7 collective-permute-start.3
  19.8 5.1 %first_main.1 = (f32[3,20,16,384]{3,2,1,0:T(8,128)S(1)}, f32[3,20,8,384]{3,2,1,0:T(8,128)S(1)}) custom-call(f32[3,16,16,384]{3,2,1,0:T(8,128)} %prev.4, f32[16,16,384]{2,1,0:T(8,128)} %buoy.5, f32[16,16,384]{2,1,0:T(8,128)} %mu.5, f32[16,16,384]{2,1,0:T(8,128)} %lam.5, f32[3,16,16,384]{3,2,1,0:T(8,128)} %prev.5, f32[24,16,384]{2,1,0:T(8,128)S(1)} %collective-permute-done.xa, ...), custom_call_target="tpu_custom_call" | custom-call | tf_op jit(solution)/shard_map/first_main/pallas_call | solution.py:275
  24.9 0.3 collective-permute-done.2.ya
  25.2 2.2 %first_north.1 = (f32[3,20,16,384]{3,2,1,0:T(8,128)S(1)}, f32[56,2,384]{2,1,0:T(2,128)S(1)}, f32[56,2,384]{2,1,0:T(2,128)S(1)}, f32[8,256]{1,0:T(8,128)S(1)}) custom-call(f32[3,20,16,384]{3,2,1,0:T(8,128)S(1)} %get-tuple-element.42.main, f32[3,20,8,384]{3,2,1,0:T(8,128)S(1)} %get-tuple-element.43.pack, f32[68,2,384]{2,1,0:T(2,128)S(1)} %collective-permute-done.2.ya, ...), custom_call_target="tpu_custom_call" | custom-call | tf_op jit(solution)/shard_map/first_north/pallas_call | solution.py:324
  27.4 5.0 %collective-permute-start.4 = (f32[56,2,384]{2,1,0:T(2,128)S(1)}, f32[56,2,384]{2,1,0:T(2,128)S(1)}, u32[]{:S(2)}, u32[]{:S(2)}) collective-permute-start(f32[56,2,384]{2,1,0:T(2,128)S(1)} %get-tuple-element.48), channel_id=1, source_target_pairs={{0,1},{1,0},{2,3},{3,2},{4,5},{5,4},{6,7},{7,6},{8,9},{9,8},{10,11... | collective-permute-start | bytes 516104 | tf_op jit(solution)/shard_map/ppermute | solution.py:719
  32.4 0.7 collective-permute-start.5
  33.1 22.8 %all_to_all.10 = s32[128,1,128]{2,1,0:T(1,128)S(1)} all-to-all(s32[128,1,128]{2,1,0:T(1,128)S(1)} %bitcast.17), channel_id=1, replica_groups=mesh['gx'=16,'gy'=8] {'gx','gy'}, dimensions={0} | all-to-all | bytes 131072 | tf_op jit(solution)/shard_map/all_to_all | solution.py:758
  55.9 0.5 prepare.1
  56.4 4.5 %second_main.1 = (f32[3,16,16,384]{3,2,1,0:T(8,128)}, f32[3,16,16,384]{3,2,1,0:T(8,128)S(1)}, f32[3,16,8,384]{3,2,1,0:T(8,128)S(1)}) custom-call(f32[3,16,16,384]{3,2,1,0:T(8,128)} %prev.5, f32[16,16,384]{2,1,0:T(8,128)} %buoy.5, f32[16,16,384]{2,1,0:T(8,128)} %mu.5, f32[16,16,384]{2,1,0:T(8,128)} %lam.5, f32[3,20,16,384]{3,2,1,0:T(8,128)S(1)} %get-tuple-element.46.vp), custom_call_target="tpu_custom_call" | custom-call | tf_op jit(solution)/shard_map/second_main/pallas_call | solution.py:352
  60.9 0.0 copy-start
  61.0 3.7 %near_north.1 = (f32[3,16,16,128]{3,2,1,0:T(8,128)S(1)}, f32[256,128]{1,0:T(8,128)}) custom-call(f32[3,16,16,384]{3,2,1,0:T(8,128)S(1)} %get-tuple-element.55.main, f32[3,16,8,384]{3,2,1,0:T(8,128)S(1)} %get-tuple-element.56.pack, f32[56,2,384]{2,1,0:T(2,128)S(1)} %collective-permute-done.4.ya, f32[56,2,384]{2,1,0:T(2,128)S(1)} %collective-permute-done.5.yb, ...), custom_call_target="tpu_custom_call" | custom-call | tf_op jit(solution)/shard_map/near_north/pallas_call | solution.py:546
  64.6 0.7 copy-done.1
  65.4 4.5 %all-to-all-start.1 = ((f32[128,2,128]{2,1,0:T(2,128)}), f32[128,2,128]{2,1,0:T(2,128)S(1)}, u32[]{:S(2)}, u32[]{:S(2)}) async-start(f32[128,2,128]{2,1,0:T(2,128)} %bitcast.6), calls=%async_computation.1 | async-start | bytes 262144 | tf_op jit(solution)/shard_map/all_to_all | solution.py:758
  69.9 0.0 copy-start.2
  70.6 0.7 history.1.base
  71.3 2.0 %far_north.1 = f32[3,16,16,384]{3,2,1,0:T(8,128)} custom-call(f32[3,16,16,384]{3,2,1,0:T(8,128)S(1)} %get-tuple-element.55.main, f32[3,16,8,384]{3,2,1,0:T(8,128)S(1)} %get-tuple-element.56.pack, f32[3,16,16,128]{3,2,1,0:T(8,128)S(1)} %copy-done.2, f32[56,2,384]{2,1,0:T(2,128)S(1)} %collective-permute-done.4.ya, f32[56,2,384]{2,1,0:T(2,128)S(1)} %collective-permute-done.5.yb), custom_call_target="tpu_custom_call" | custom-call | tf_op jit(solution)/shard_map/far_north/pallas_call | solution.py:577
  73.3 6.5 %all-to-all-done.1 = f32[128,2,128]{2,1,0:T(2,128)S(1)} async-done(((f32[128,2,128]{2,1,0:T(2,128)}), f32[128,2,128]{2,1,0:T(2,128)S(1)}, u32[]{:S(2)}, u32[]{:S(2)}) %all-to-all-start.1) | async-done | bytes 131104 | tf_op jit(solution)/shard_map/all_to_all | solution.py:758
  79.8 1.1 %responses.1 = f32[2,64,128]{2,1,0:T(8,128)} custom-call(f32[256,128]{1,0:T(8,128)S(1)} %bitcast.12, s32[1,128]{1,0:T(1,128)S(1)} %get-tuple-element.64.pos, s32[1,1]{1,0:T(1,128)} %bitcast.11.count, f32[2,64,128]{2,1,0:T(8,128)S(1)} %history.1.base, f32[32,64]{1,0:T(8,128)S(1)} %bitcast.15), custom_call_target="tpu_custom_call" | custom-call | tf_op jit(solution)/shard_map/responses/pallas_call | solution.py:705
  (13 shorter events, 0.0 us)
Async XLA Ops:
  2.3 4.6 %collective-permute-start = (f32[24,16,384]{2,1,0:T(8,128)S(1)}, f32[24,16,384]{2,1,0:T(8,128)S(1)}, u32[]{:S(2)}, u32[]{:S(2)}) collective-permute-start(f32[24,16,384]{2,1,0:T(8,128)S(1)} %get-tuple-element.36), channel_id=1, source_target_pairs={{0,8},{8,0},{16,24},{24,16},{32,40},{40,32},{48,56},{56,48},{64,72... | collective-permute-start | bytes 1769480 | tf_op jit(solution)/shard_map/ppermute | solution.py:719
  3.7 11.2 %collective-permute-start.1 = (f32[24,16,384]{2,1,0:T(8,128)S(1)}, f32[24,16,384]{2,1,0:T(8,128)S(1)}, u32[]{:S(2)}, u32[]{:S(2)}) collective-permute-start(f32[24,16,384]{2,1,0:T(8,128)S(1)} %get-tuple-element.37), channel_id=1, source_target_pairs={{8,16},{16,8},{24,32},{32,24},{40,48},{48,40},{56,64},{64,56},{72,... | collective-permute-start | bytes 1769480 | tf_op jit(solution)/shard_map/ppermute | solution.py:719
  15.0 10.2 %collective-permute-start.2 = (f32[68,2,384]{2,1,0:T(2,128)S(1)}, f32[68,2,384]{2,1,0:T(2,128)S(1)}, u32[]{:S(2)}, u32[]{:S(2)}) collective-permute-start(f32[68,2,384]{2,1,0:T(2,128)S(1)} %get-tuple-element.38), channel_id=1, source_target_pairs={{0,1},{1,0},{2,3},{3,2},{4,5},{5,4},{6,7},{7,6},{8,9},{9,8},{10,11... | collective-permute-start | bytes 626696 | tf_op jit(solution)/shard_map/ppermute | solution.py:719
  19.1 6.1 %collective-permute-start.3 = (f32[68,2,384]{2,1,0:T(2,128)S(1)}, f32[68,2,384]{2,1,0:T(2,128)S(1)}, u32[]{:S(2)}, u32[]{:S(2)}) collective-permute-start(f32[68,2,384]{2,1,0:T(2,128)S(1)} %get-tuple-element.39), channel_id=1, source_target_pairs={{1,2},{2,1},{3,4},{4,3},{5,6},{6,5},{9,10},{10,9},{11,12},{12,11},... | collective-permute-start | bytes 626696 | tf_op jit(solution)/shard_map/ppermute | solution.py:719
  25.2 30.7 %copy-start.4 = (f32[192,64]{0,1:T(8,128)S(1)}, f32[192,64]{0,1:T(8,128)}, u32[]{:S(2)}) copy-start(f32[192,64]{0,1:T(8,128)} %param.20) | copy-start | bytes 147460
  25.2 30.7 %copy-start.5 = (s32[128,2]{0,1:T(2,128)S(1)}, s32[128,2]{0,1:T(2,128)}, u32[]{:S(2)}) copy-start(s32[128,2]{0,1:T(2,128)} %param.16) | copy-start | bytes 3076
  27.4 33.5 %collective-permute-start.4 = (f32[56,2,384]{2,1,0:T(2,128)S(1)}, f32[56,2,384]{2,1,0:T(2,128)S(1)}, u32[]{:S(2)}, u32[]{:S(2)}) collective-permute-start(f32[56,2,384]{2,1,0:T(2,128)S(1)} %get-tuple-element.48), channel_id=1, source_target_pairs={{0,1},{1,0},{2,3},{3,2},{4,5},{5,4},{6,7},{7,6},{8,9},{9,8},{10,11... | collective-permute-start | bytes 516104 | tf_op jit(solution)/shard_map/ppermute | solution.py:719
  32.4 28.5 %collective-permute-start.5 = (f32[56,2,384]{2,1,0:T(2,128)S(1)}, f32[56,2,384]{2,1,0:T(2,128)S(1)}, u32[]{:S(2)}, u32[]{:S(2)}) collective-permute-start(f32[56,2,384]{2,1,0:T(2,128)S(1)} %get-tuple-element.49), channel_id=1, source_target_pairs={{1,2},{2,1},{3,4},{4,3},{5,6},{6,5},{9,10},{10,9},{11,12},{12,11},... | collective-permute-start | bytes 516104 | tf_op jit(solution)/shard_map/ppermute | solution.py:719
  60.9 9.6 %copy-start = (f32[31,64,128]{2,1,0:T(8,128)S(1)}, f32[31,64,128]{2,1,0:T(8,128)}, u32[]{:S(2)}) copy-start(f32[31,64,128]{2,1,0:T(8,128)} %hist.1) | copy-start | bytes 3047428
  61.0 9.6 %copy-start.3 = (f32[64,32]{0,1:T(8,128)S(1)}, f32[64,32]{0,1:T(8,128)}, u32[]{:S(2)}) copy-start(f32[64,32]{0,1:T(8,128)} %param.21) | copy-start | bytes 24580
  64.6 0.7 copy-start.1
  65.4 14.4 %all-to-all-start.1 = ((f32[128,2,128]{2,1,0:T(2,128)}), f32[128,2,128]{2,1,0:T(2,128)S(1)}, u32[]{:S(2)}, u32[]{:S(2)}) async-start(f32[128,2,128]{2,1,0:T(2,128)} %bitcast.6), calls=%async_computation.1 | async-start | bytes 262144 | tf_op jit(solution)/shard_map/all_to_all | solution.py:758
  69.9 1.4 %copy-start.2 = (f32[3,16,16,128]{3,2,1,0:T(8,128)S(1)}, f32[3,16,16,128]{3,2,1,0:T(8,128)}, u32[]{:S(2)}) copy-start(f32[3,16,16,128]{3,2,1,0:T(8,128)} %copy-done.1) | copy-start | bytes 1179652

commit v8 on v7

--- a/solution.py
+++ b/solution.py
@@ -177,18 +177,33 @@
     return [pltpu.VMEM((rows + 4, cols, depth), F32)] * 2 + [pltpu.VMEM((rows, cols, depth), F32)] * 6
 
 
+def halves(x):
+    high = x.astype(jnp.bfloat16)
+    return high, (x - high.astype(F32)).astype(jnp.bfloat16)
+
+
+def product(a, b, dims=((1,), (0,))):
+    dot = lambda p, q: lax.dot_general(p, q, (dims, ((), ())), preferred_element_type=F32)
+    if a.dtype == jnp.bfloat16:
+        high, low = halves(b)
+        return dot(a, high) + dot(a, low)
+    ah, al = halves(a)
+    if b.dtype == jnp.bfloat16:
+        return dot(ah, b) + dot(al, b)
+    bh, bl = halves(b)
+    return dot(ah, bh) + (dot(ah, bl) + dot(al, bh))
+
+
+def one_hot(mask):
+    return jnp.where(mask, 1.0, 0.0).astype(jnp.bfloat16)
+
+
 def surface_rows(field, first):
     cells = SIDE * SIDE
     flat = jnp.zeros((8, cells), F32)
     for c in range(3):
-        pick = jnp.where((iota((8, LANES), 0) == first + c) & (iota((8, LANES), 1) == 0), 1.0, 0.0)
-        flat = flat + lax.dot_general(
-            pick,
-            field[c, :, :, 0:LANES].reshape(cells, LANES),
-            (((1,), (1,)), ((), ())),
-            precision=HIGHEST,
-            preferred_element_type=F32,
-        )
+        pick = one_hot((iota((8, LANES), 0) == first + c) & (iota((8, LANES), 1) == 0))
+        flat = flat + product(pick, field[c, :, :, 0:LANES].reshape(cells, LANES), ((1,), (1,)))
     return flat
 
 
@@ -487,12 +502,7 @@
     for n in range(2):
         total = jnp.zeros((LANES, weights.shape[2]), F32)
         for c in range(3):
-            total = total + jnp.dot(
-                windows[pl.ds(3 * n + c, LANES, stride=8), :],
-                weights[c],
-                precision=HIGHEST,
-                preferred_element_type=F32,
-            )
+            total = total + product(windows[pl.ds(3 * n + c, LANES, stride=8), :], weights[c])
         both.append(total)
     return jnp.concatenate(both, axis=1)
 
@@ -538,7 +548,7 @@
     fill_north(rim, ya, yb)
     add_north(rim, pack, main, near, ex, ey, 0, 1)
     forces = corner_forces(top[...] + surface_rows(near, 3), weights, windows)
-    ans[...] = jnp.dot(chosen[...], forces, precision=HIGHEST, preferred_element_type=F32)
+    ans[...] = product(chosen[...].astype(jnp.bfloat16), forces)
 
 
 def near_north(main, pack, ya, yb, top, chosen, weights):
@@ -689,10 +699,7 @@
 
 def response_kernel(ans, pos, count, base, ker, out):
     at = pos[...]
-    chosen = jnp.where(iota((2 * LANES, LANES), 0) == at, 1.0, 0.0)
-    forces = lax.dot_general(
-        ans[...], chosen, (((0,), (0,)), ((), ())), precision=HIGHEST, preferred_element_type=F32
-    )
+    forces = product(ans[...], one_hot(iota((2 * LANES, LANES), 0) == at), ((0,), (0,)))
     k = columns_of(ker)
     modes = k.shape[0]
     early, late = forces[:modes], forces[modes:]
@@ -724,7 +731,9 @@
 
 
 def north_swaps(ya, yb):
-    return swap(ya, "gy", 0), swap(yb, "gy", 1)
+    yb = swap(yb, "gy", 1)
+    ya = swap(ya, "gy", 0)
+    return ya, yb
 
 
 def per_device(

time: 81.2 us -> 80 us (0.985)
  Pallas kernels: 21.5 us -> 20.4 us
    pallas_call x1, Pallas kernels: 3.67 us -> 2.74 us  [near_north(): pl.pallas_call(near_north_kernel, out_shape=(pltpu.VMEM((3, rows, cols, L...]
where the time goes in v8:
time: 80 us; the launch traced here: 79.7 us
  blocking collectives  22.8 us (28%)
  Pallas kernels  20.4 us (25%)
  starting transfers between devices  19.4 us (24%)
  waiting for transfers between devices  14.8 us (18%)
  between operations  1.49 us (2%)
    all_to_all x1, blocking collectives, exchange(): out = lax.all_to_all(rows, ('gx', 'gy'), split_axis=0, concat_axis=0)  22.8 us
    ppermute x6, starting transfers between devices, swap(): return in_vmem(lax.ppermute(array, axis, pairs))  15 us
    ppermute x6, waiting for transfers between devices, swap(): return in_vmem(lax.ppermute(array, axis, pairs))  8.34 us
    all_to_all x1, waiting for transfers between devices, exchange(): out = lax.all_to_all(rows, ('gx', 'gy'), split_axis=0, concat_axis=0)  6.5 us
    pallas_call x1, Pallas kernels, first_main(): pl.pallas_call(first_main_kernel, out_shape=(pltpu.VMEM((3, wide, cols, d...  5.12 us
    pallas_call x1, Pallas kernels, second_main(): pl.pallas_call(second_main_kernel, out_shape=(pltpu.HBM(prev.shape, F32),...  4.54 us
    all_to_all x1, starting transfers between devices, exchange(): out = lax.all_to_all(rows, ('gx', 'gy'), split_axis=0, concat_axis=0)  4.46 us
    pallas_call x1, Pallas kernels, near_north(): pl.pallas_call(near_north_kernel, out_shape=(pltpu.VMEM((3, rows, cols, L...  2.74 us
  transfers between devices with their start and end apart: 7, of which 3 were waited for; matrix products, arithmetic and copies ran while one was open for 0% of the time, Pallas kernels for 16%

profile of v8, /device:TPU:1, one launch (start us, length us, event | category | flops | bytes accessed | tf_op | source)
XLA Modules:
  0.0 79.7 jit_solution(14391648627085761298)
XLA Ops:
  0.6 1.6 %east_pack.1 = (f32[24,16,384]{2,1,0:T(8,128)S(1)}, f32[24,16,384]{2,1,0:T(8,128)S(1)}, f32[3,16,2,384]{3,2,1,0:T(2,128)S(1)}, f32[3,16,2,384]{3,2,1,0:T(2,128)S...) custom-call(f32[3,16,16,384]{3,2,1,0:T(8,128)} %prev.5, f32[3,16,16,384]{3,2,1,0:T(8,128)} %prev.4, ...), custom_call_target="tpu_custom_call" | custom-call | tf_op jit(solution)/shard_map/east_pack/pallas_call | solution.py:247
  2.3 1.5 %collective-permute-start = (f32[24,16,384]{2,1,0:T(8,128)S(1)}, f32[24,16,384]{2,1,0:T(8,128)S(1)}, u32[]{:S(2)}, u32[]{:S(2)}) collective-permute-start(f32[24,16,384]{2,1,0:T(8,128)S(1)} %get-tuple-element.36), channel_id=1, source_target_pairs={{0,8},{8,0},{16,24},{24,16},{32,40},{40,32},{48,56},{56,48},{64,72... | collective-permute-start | bytes 1769480 | tf_op jit(solution)/shard_map/ppermute | solution.py:726
  3.7 3.1 %collective-permute-start.1 = (f32[24,16,384]{2,1,0:T(8,128)S(1)}, f32[24,16,384]{2,1,0:T(8,128)S(1)}, u32[]{:S(2)}, u32[]{:S(2)}) collective-permute-start(f32[24,16,384]{2,1,0:T(8,128)S(1)} %get-tuple-element.37), channel_id=1, source_target_pairs={{8,16},{16,8},{24,32},{32,24},{40,48},{48,40},{56,64},{64,56},{72,... | collective-permute-start | bytes 1769480 | tf_op jit(solution)/shard_map/ppermute | solution.py:726
  6.9 8.0 %collective-permute-done.1.xb = f32[24,16,384]{2,1,0:T(8,128)S(1)} collective-permute-done((f32[24,16,384]{2,1,0:T(8,128)S(1)}, f32[24,16,384]{2,1,0:T(8,128)S(1)}, u32[]{:S(2)}, u32[]{:S(2)}) %collective-permute-start.1) | collective-permute-done | bytes 589856 | tf_op jit(solution)/shard_map/ppermute | solution.py:726
  14.9 0.1 north_edges.1
  15.0 4.1 %collective-permute-start.2 = (f32[68,2,384]{2,1,0:T(2,128)S(1)}, f32[68,2,384]{2,1,0:T(2,128)S(1)}, u32[]{:S(2)}, u32[]{:S(2)}) collective-permute-start(f32[68,2,384]{2,1,0:T(2,128)S(1)} %get-tuple-element.38), channel_id=1, source_target_pairs={{0,1},{1,0},{2,3},{3,2},{4,5},{5,4},{6,7},{7,6},{8,9},{9,8},{10,11... | collective-permute-start | bytes 626696 | tf_op jit(solution)/shard_map/ppermute | solution.py:726
  19.1 0.7 collective-permute-start.3
  19.8 5.1 %first_main.1 = (f32[3,20,16,384]{3,2,1,0:T(8,128)S(1)}, f32[3,20,8,384]{3,2,1,0:T(8,128)S(1)}) custom-call(f32[3,16,16,384]{3,2,1,0:T(8,128)} %prev.4, f32[16,16,384]{2,1,0:T(8,128)} %buoy.5, f32[16,16,384]{2,1,0:T(8,128)} %mu.5, f32[16,16,384]{2,1,0:T(8,128)} %lam.5, f32[3,16,16,384]{3,2,1,0:T(8,128)} %prev.5, f32[24,16,384]{2,1,0:T(8,128)S(1)} %collective-permute-done.xa, ...), custom_call_target="tpu_custom_call" | custom-call | tf_op jit(solution)/shard_map/first_main/pallas_call | solution.py:290
  24.9 0.3 collective-permute-done.2.ya
  25.2 2.0 %first_north.1 = (f32[3,20,16,384]{3,2,1,0:T(8,128)S(1)}, f32[56,2,384]{2,1,0:T(2,128)S(1)}, f32[56,2,384]{2,1,0:T(2,128)S(1)}, f32[8,256]{1,0:T(8,128)S(1)}) custom-call(f32[3,20,16,384]{3,2,1,0:T(8,128)S(1)} %get-tuple-element.42.main, f32[3,20,8,384]{3,2,1,0:T(8,128)S(1)} %get-tuple-element.43.pack, f32[68,2,384]{2,1,0:T(2,128)S(1)} %collective-permute-done.2.ya, ...), custom_call_target="tpu_custom_call" | custom-call | tf_op jit(solution)/shard_map/first_north/pallas_call | solution.py:339
  27.2 5.0 %collective-permute-start.4 = (f32[56,2,384]{2,1,0:T(2,128)S(1)}, f32[56,2,384]{2,1,0:T(2,128)S(1)}, u32[]{:S(2)}, u32[]{:S(2)}) collective-permute-start(f32[56,2,384]{2,1,0:T(2,128)S(1)} %get-tuple-element.48), channel_id=1, source_target_pairs={{0,1},{1,0},{2,3},{3,2},{4,5},{5,4},{6,7},{7,6},{8,9},{9,8},{10,11... | collective-permute-start | bytes 516104 | tf_op jit(solution)/shard_map/ppermute | solution.py:726
  32.2 0.7 collective-permute-start.5
  32.9 22.8 %all_to_all.10 = s32[128,1,128]{2,1,0:T(1,128)S(1)} all-to-all(s32[128,1,128]{2,1,0:T(1,128)S(1)} %bitcast.17), channel_id=1, replica_groups=mesh['gx'=16,'gy'=8] {'gx','gy'}, dimensions={0} | all-to-all | bytes 131072 | tf_op jit(solution)/shard_map/all_to_all | solution.py:767
  55.7 0.5 prepare.1
  56.2 4.5 %second_main.1 = (f32[3,16,16,384]{3,2,1,0:T(8,128)}, f32[3,16,16,384]{3,2,1,0:T(8,128)S(1)}, f32[3,16,8,384]{3,2,1,0:T(8,128)S(1)}) custom-call(f32[3,16,16,384]{3,2,1,0:T(8,128)} %prev.5, f32[16,16,384]{2,1,0:T(8,128)} %buoy.5, f32[16,16,384]{2,1,0:T(8,128)} %mu.5, f32[16,16,384]{2,1,0:T(8,128)} %lam.5, f32[3,20,16,384]{3,2,1,0:T(8,128)S(1)} %get-tuple-element.46.vp), custom_call_target="tpu_custom_call" | custom-call | tf_op jit(solution)/shard_map/second_main/pallas_call | solution.py:367
  60.7 0.0 copy-start
  60.8 0.0 copy-start.3
  60.8 2.7 %near_north.1 = (f32[3,16,16,128]{3,2,1,0:T(8,128)S(1)}, f32[256,128]{1,0:T(8,128)}) custom-call(f32[3,16,16,384]{3,2,1,0:T(8,128)S(1)} %get-tuple-element.55.main, f32[3,16,8,384]{3,2,1,0:T(8,128)S(1)} %get-tuple-element.56.pack, f32[56,2,384]{2,1,0:T(2,128)S(1)} %collective-permute-done.4.ya, f32[56,2,384]{2,1,0:T(2,128)S(1)} %collective-permute-done.5.yb, ...), custom_call_target="tpu_custom_call" | custom-call | tf_op jit(solution)/shard_map/near_north/pallas_call | solution.py:556
  63.5 0.7 copy-done.1
  64.3 4.5 %all-to-all-start.1 = ((f32[128,2,128]{2,1,0:T(2,128)}), f32[128,2,128]{2,1,0:T(2,128)S(1)}, u32[]{:S(2)}, u32[]{:S(2)}) async-start(f32[128,2,128]{2,1,0:T(2,128)} %bitcast.6), calls=%async_computation.1 | async-start | bytes 262144 | tf_op jit(solution)/shard_map/all_to_all | solution.py:767
  69.5 0.7 history.1.base
  70.2 2.0 %far_north.1 = f32[3,16,16,384]{3,2,1,0:T(8,128)} custom-call(f32[3,16,16,384]{3,2,1,0:T(8,128)S(1)} %get-tuple-element.55.main, f32[3,16,8,384]{3,2,1,0:T(8,128)S(1)} %get-tuple-element.56.pack, f32[3,16,16,128]{3,2,1,0:T(8,128)S(1)} %copy-done.2, f32[56,2,384]{2,1,0:T(2,128)S(1)} %collective-permute-done.4.ya, f32[56,2,384]{2,1,0:T(2,128)S(1)} %collective-permute-done.5.yb), custom_call_target="tpu_custom_call" | custom-call | tf_op jit(solution)/shard_map/far_north/pallas_call | solution.py:587
  72.2 6.5 %all-to-all-done.1 = f32[128,2,128]{2,1,0:T(2,128)S(1)} async-done(((f32[128,2,128]{2,1,0:T(2,128)}), f32[128,2,128]{2,1,0:T(2,128)S(1)}, u32[]{:S(2)}, u32[]{:S(2)}) %all-to-all-start.1) | async-done | bytes 131104 | tf_op jit(solution)/shard_map/all_to_all | solution.py:767
  78.7 1.0 %responses.1 = f32[2,64,128]{2,1,0:T(8,128)} custom-call(f32[256,128]{1,0:T(8,128)S(1)} %bitcast.12, s32[1,128]{1,0:T(1,128)S(1)} %get-tuple-element.64.pos, s32[1,1]{1,0:T(1,128)} %bitcast.11.count, f32[2,64,128]{2,1,0:T(8,128)S(1)} %history.1.base, f32[32,64]{1,0:T(8,128)S(1)} %bitcast.15), custom_call_target="tpu_custom_call" | custom-call | tf_op jit(solution)/shard_map/responses/pallas_call | solution.py:712
  (13 shorter events, 0.0 us)
Async XLA Ops:
  2.3 4.6 %collective-permute-start = (f32[24,16,384]{2,1,0:T(8,128)S(1)}, f32[24,16,384]{2,1,0:T(8,128)S(1)}, u32[]{:S(2)}, u32[]{:S(2)}) collective-permute-start(f32[24,16,384]{2,1,0:T(8,128)S(1)} %get-tuple-element.36), channel_id=1, source_target_pairs={{0,8},{8,0},{16,24},{24,16},{32,40},{40,32},{48,56},{56,48},{64,72... | collective-permute-start | bytes 1769480 | tf_op jit(solution)/shard_map/ppermute | solution.py:726
  3.7 11.2 %collective-permute-start.1 = (f32[24,16,384]{2,1,0:T(8,128)S(1)}, f32[24,16,384]{2,1,0:T(8,128)S(1)}, u32[]{:S(2)}, u32[]{:S(2)}) collective-permute-start(f32[24,16,384]{2,1,0:T(8,128)S(1)} %get-tuple-element.37), channel_id=1, source_target_pairs={{8,16},{16,8},{24,32},{32,24},{40,48},{48,40},{56,64},{64,56},{72,... | collective-permute-start | bytes 1769480 | tf_op jit(solution)/shard_map/ppermute | solution.py:726
  15.0 10.2 %collective-permute-start.2 = (f32[68,2,384]{2,1,0:T(2,128)S(1)}, f32[68,2,384]{2,1,0:T(2,128)S(1)}, u32[]{:S(2)}, u32[]{:S(2)}) collective-permute-start(f32[68,2,384]{2,1,0:T(2,128)S(1)} %get-tuple-element.38), channel_id=1, source_target_pairs={{0,1},{1,0},{2,3},{3,2},{4,5},{5,4},{6,7},{7,6},{8,9},{9,8},{10,11... | collective-permute-start | bytes 626696 | tf_op jit(solution)/shard_map/ppermute | solution.py:726
  19.1 6.1 %collective-permute-start.3 = (f32[68,2,384]{2,1,0:T(2,128)S(1)}, f32[68,2,384]{2,1,0:T(2,128)S(1)}, u32[]{:S(2)}, u32[]{:S(2)}) collective-permute-start(f32[68,2,384]{2,1,0:T(2,128)S(1)} %get-tuple-element.39), channel_id=1, source_target_pairs={{1,2},{2,1},{3,4},{4,3},{5,6},{6,5},{9,10},{10,9},{11,12},{12,11},... | collective-permute-start | bytes 626696 | tf_op jit(solution)/shard_map/ppermute | solution.py:726
  25.2 30.5 %copy-start.4 = (f32[192,64]{0,1:T(8,128)S(1)}, f32[192,64]{0,1:T(8,128)}, u32[]{:S(2)}) copy-start(f32[192,64]{0,1:T(8,128)} %param.20) | copy-start | bytes 147460
  25.2 30.5 %copy-start.5 = (s32[128,2]{0,1:T(2,128)S(1)}, s32[128,2]{0,1:T(2,128)}, u32[]{:S(2)}) copy-start(s32[128,2]{0,1:T(2,128)} %param.16) | copy-start | bytes 3076
  27.2 33.5 %collective-permute-start.4 = (f32[56,2,384]{2,1,0:T(2,128)S(1)}, f32[56,2,384]{2,1,0:T(2,128)S(1)}, u32[]{:S(2)}, u32[]{:S(2)}) collective-permute-start(f32[56,2,384]{2,1,0:T(2,128)S(1)} %get-tuple-element.48), channel_id=1, source_target_pairs={{0,1},{1,0},{2,3},{3,2},{4,5},{5,4},{6,7},{7,6},{8,9},{9,8},{10,11... | collective-permute-start | bytes 516104 | tf_op jit(solution)/shard_map/ppermute | solution.py:726
  32.2 28.5 %collective-permute-start.5 = (f32[56,2,384]{2,1,0:T(2,128)S(1)}, f32[56,2,384]{2,1,0:T(2,128)S(1)}, u32[]{:S(2)}, u32[]{:S(2)}) collective-permute-start(f32[56,2,384]{2,1,0:T(2,128)S(1)} %get-tuple-element.49), channel_id=1, source_target_pairs={{1,2},{2,1},{3,4},{4,3},{5,6},{6,5},{9,10},{10,9},{11,12},{12,11},... | collective-permute-start | bytes 516104 | tf_op jit(solution)/shard_map/ppermute | solution.py:726
  60.7 8.7 %copy-start = (f32[31,64,128]{2,1,0:T(8,128)S(1)}, f32[31,64,128]{2,1,0:T(8,128)}, u32[]{:S(2)}) copy-start(f32[31,64,128]{2,1,0:T(8,128)} %hist.1) | copy-start | bytes 3047428
  60.8 8.7 %copy-start.3 = (f32[64,32]{0,1:T(8,128)S(1)}, f32[64,32]{0,1:T(8,128)}, u32[]{:S(2)}) copy-start(f32[64,32]{0,1:T(8,128)} %param.21) | copy-start | bytes 24580
  63.5 0.7 copy-start.1
  64.3 14.4 %all-to-all-start.1 = ((f32[128,2,128]{2,1,0:T(2,128)}), f32[128,2,128]{2,1,0:T(2,128)S(1)}, u32[]{:S(2)}, u32[]{:S(2)}) async-start(f32[128,2,128]{2,1,0:T(2,128)} %bitcast.6), calls=%async_computation.1 | async-start | bytes 262144 | tf_op jit(solution)/shard_map/all_to_all | solution.py:767
  68.7 1.4 %copy-start.2 = (f32[3,16,16,128]{3,2,1,0:T(8,128)S(1)}, f32[3,16,16,128]{3,2,1,0:T(8,128)}, u32[]{:S(2)}) copy-start(f32[3,16,16,128]{3,2,1,0:T(8,128)} %copy-done.1) | copy-start | bytes 1179652
